TPU v7x, 32 devices: a whole 2x2x4 slice. The times are simulated.
32 devices in a mesh: row: 4 (over y, x), col: 4 (over z), depth: 2 (over core).
Axes of the slice: x: 2, y: 2, z: 4, core: 2. Of those that a mesh axis runs over, the one named last changes fastest.
Arguments:
- a_band: bfloat16 [32, 16, 128, 128], P(('row', 'col'))
- a_fill: int32 [32, 16], P(('row', 'col')), may hold values from 0 to 1, as said below
- c_reach: int32 [32], P(('row', 'col')), may hold values from 16 to 24
Outputs:
- squared: bfloat16 [32, 24, 128, 128], P(('row', 'col'), None, 'depth')
Inputs may be any that keep to these rules, and one draw needn't show every extreme that they name: a_fill[i, e] is 0 where i + e >= 32; it is 1 where e = 0 and where e = 15 and i + e < 32.
All inputs are finite; a program needn't handle non-finite values.
Results may differ from a plain program's by a relative error of at most 0.0045.
Values may be sent and summed in bfloat16 or wider, within the bound.
No kernel may reach another device: no remote copies, remote signals or barrier semaphores. Data moves between devices by JAX's collectives and lax.ppermute only.
A program may use at most 64 MiB of HBM per device.

v0:
```python
import jax
import jax.numpy as jnp
from jax import lax
from jax.sharding import PartitionSpec as P

OUT_BAND = 24


def from_behind(value, axis, steps):
    count = lax.axis_size(axis)
    first, last = (max(0, -steps), min(count, count - steps))
    return lax.ppermute(value, axis, [(source, source + steps) for source in range(first, last)])


def contribute(running_sum, left_tiles, remote_tiles, base_offset, k_count, width):
    rows_here = left_tiles.shape[0]
    band_width = remote_tiles.shape[1]
    for local_row in range(rows_here):
        for remote_row in range(rows_here):
            k_offset = base_offset + remote_row - local_row
            if 0 <= k_offset < k_count:
                span_count = min(band_width, width - k_offset)
                product_term = jnp.einsum(
                    "ab,ebc->eac",
                    left_tiles[local_row, k_offset],
                    remote_tiles[remote_row, :span_count],
                    preferred_element_type=jnp.float32,
                )
                running_sum = running_sum.at[local_row, k_offset : k_offset + span_count].add(
                    product_term
                )
    return running_sum


def per_device(a_band, a_fill, c_reach):
    rows_here, band_width, tile_size, _ = a_band.shape
    half_band = band_width // 2
    layer_index = lax.axis_index("depth")
    masked = a_band * a_fill.astype(jnp.bfloat16)[:, :, None, None]
    far_block = from_behind(masked, ("row", "col"), -(half_band // rows_here))
    base_rows = jnp.where(layer_index == 0, masked, far_block)
    left_tiles = jnp.where(layer_index == 0, masked[:, :half_band], masked[:, half_band:])
    running_sum = jnp.zeros((rows_here, OUT_BAND, tile_size, tile_size), jnp.float32)
    running_sum = contribute(running_sum, left_tiles, base_rows, 0, half_band, OUT_BAND)
    for distance in range(1, (half_band + rows_here - 2) // rows_here + 1):
        remote_tiles = from_behind(base_rows, ("row", "col"), -distance)
        running_sum = contribute(
            running_sum, left_tiles, remote_tiles, distance * rows_here, half_band, OUT_BAND
        )
    zero_index = jnp.zeros((), jnp.int32)
    placed = jnp.zeros((rows_here, OUT_BAND + half_band, tile_size, tile_size), jnp.float32)
    placed = lax.dynamic_update_slice(
        placed, running_sum, (zero_index, layer_index * half_band, zero_index, zero_index)
    )
    shares = lax.psum_scatter(
        placed[:, :OUT_BAND].astype(jnp.bfloat16), "depth", scatter_dimension=2, tiled=True
    ).astype(jnp.float32)
    keep_tiles = jnp.arange(OUT_BAND, dtype=jnp.int32)[None, :] < c_reach[:, None]
    return jnp.where(keep_tiles[:, :, None, None], shares, jnp.float32(0.0)).astype(jnp.bfloat16)


def solution(mesh):
    in_specs = (P(("row", "col"), None, None, None), P(("row", "col"), None), P(("row", "col")))
    out_specs = P(("row", "col"), None, "depth", None)
    return jax.shard_map(
        per_device, mesh=mesh, in_specs=in_specs, out_specs=out_specs, check_vma=False
    )
```

profile of v0, /device:TPU:0, one launch (start us, length us, event | category | flops | bytes accessed | tf_op | source)
XLA Modules:
  0.0 164.5 jit_solution(12234073962807032836)
XLA Ops:
  6.5 0.7 convert_element_type.10
  7.2 1.4 broadcast_multiply_fusion
  8.6 1.3 collective-permute-start
  9.9 0.6 fusion.24
  10.6 0.6 fusion.23
  11.2 0.6 fusion.22
  11.8 0.6 fusion.21
  12.4 0.6 fusion.20
  13.0 0.6 fusion.19
  13.6 1.4 and_reduce_fusion.2
  15.0 1.5 and_reduce_fusion
  16.5 20.1 %collective-permute-done = bf16[2,16,128,128]{3,2,1,0:T(8,128)(2,1)S(1)} collective-permute-done((bf16[2,16,128,128]{3,2,1,0:T(8,128)(2,1)S(1)}, bf16[2,16,128,128]{3,2,1,0:T(8,128)(2,1)S(1)}, u32[]{:S(2)}, u32[]{:S(2)}) %collective-permute-start) | collective-permute-done | bytes 1048608 | tf_op jit(solution)/shard_map/ppermute | solution.py:12
  36.6 1.4 broadcast_select_fusion
  38.0 1.3 collective-permute-start.1
  39.3 0.6 fusion.25
  39.9 1.3 collective-permute-start.2
  41.2 1.3 collective-permute-start.3
  42.5 1.3 collective-permute-start.4
  44.5 1.7 %fusion.1 = f32[2,24,128,128]{2,3,1,0:T(8,128)S(1)} fusion(f32[2,24,128,128]{2,3,1,0:T(8,128)S(1)} %scatter-add.54, s32[]{:T(128)} %bitcast.5, s32[]{:T(128)} %bitcast.6, bf16[2,16,128,128]{3,2,1,0:T(8,128)(2,1)S(1)} %broadcast_select_fusion, bf16[2,8,128,128]{3,2,1,0:T(8,128)(2,1)S(1)} %slice_select_fusion), kind=kOutput, calls=%fused_computation.25 | convolution fusion | flops 67371008 | bytes 2654216 | tf_op jit(solution)/shard_map/ab,ebc->eac/dot_general | solution.py:23
  46.6 18.3 %collective-permute-done.1 = bf16[2,16,128,128]{3,2,1,0:T(8,128)(2,1)S(1)} collective-permute-done((bf16[2,16,128,128]{3,2,1,0:T(8,128)(2,1)S(1)}, bf16[2,16,128,128]{3,2,1,0:T(8,128)(2,1)S(1)}, u32[]{:S(2)}, u32[]{:S(2)}) %collective-permute-start.1) | collective-permute-done | bytes 1048608 | tf_op jit(solution)/shard_map/ppermute | solution.py:12
  64.9 2.3 %fusion.8 = f32[2,24,128,128]{2,3,1,0:T(8,128)S(1)} fusion(f32[2,24,128,128]{2,3,1,0:T(8,128)S(1)} %fusion.18, s32[]{:T(128)} %bitcast.16, s32[]{:T(128)} %bitcast.17, pred[]{:T(512)} %get-tuple-element.205, bf16[2,16,128,128]{3,2,1,0:T(8,128)(2,1)S(1)} %collective-permute-done.1, bf16[2,8,128,128]{3,2,1,0:T(8,128)(2,1)S(1)} %slice_select_fusion), kind=kOutput, calls=%fused_computation.32 | convolution fusion | flops 67633152 | bytes 2654217 | tf_op jit(solution)/shard_map/ab,ebc->eac/dot_general | solution.py:23
  67.3 2.2 %fusion.11 = f32[2,24,128,128]{2,3,1,0:T(8,128)S(1)} fusion(f32[2,24,128,128]{2,3,1,0:T(8,128)S(1)} %fusion.8, s32[]{:T(128)} %bitcast.23, s32[]{:T(128)} %bitcast.24, pred[]{:T(512)} %get-tuple-element.206, bf16[2,16,128,128]{3,2,1,0:T(8,128)(2,1)S(1)} %collective-permute-done.1, bf16[2,8,128,128]{3,2,1,0:T(8,128)(2,1)S(1)} %slice_select_fusion), kind=kOutput, calls=%fused_computation.35 | convolution fusion | flops 67633152 | bytes 2654217 | tf_op jit(solution)/shard_map/ab,ebc->eac/dot_general | solution.py:23
  70.2 62.4 %collective-permute-done.2 = bf16[2,16,128,128]{3,2,1,0:T(8,128)(2,1)S(1)} collective-permute-done((bf16[2,16,128,128]{3,2,1,0:T(8,128)(2,1)S(1)}, bf16[2,16,128,128]{3,2,1,0:T(8,128)(2,1)S(1)}, u32[]{:S(2)}, u32[]{:S(2)}) %collective-permute-start.2) | collective-permute-done | bytes 1048608 | tf_op jit(solution)/shard_map/ppermute | solution.py:12
  132.6 2.3 %fusion.12 = f32[2,24,128,128]{2,3,1,0:T(8,128)S(1)} fusion(f32[2,24,128,128]{2,3,1,0:T(8,128)S(1)} %fusion.17, s32[]{:T(128)} %bitcast.38, s32[]{:T(128)} %bitcast.39, pred[]{:T(512)} %get-tuple-element.200, bf16[2,16,128,128]{3,2,1,0:T(8,128)(2,1)S(1)} %collective-permute-done.2, bf16[2,8,128,128]{3,2,1,0:T(8,128)(2,1)S(1)} %slice_select_fusion), kind=kOutput, calls=%fused_computation.36 | convolution fusion | flops 67633152 | bytes 2654217 | tf_op jit(solution)/shard_map/ab,ebc->eac/dot_general | solution.py:23
  134.8 2.3 %fusion.9 = f32[2,24,128,128]{2,3,1,0:T(8,128)S(1)} fusion(f32[2,24,128,128]{2,3,1,0:T(8,128)S(1)} %fusion.12, s32[]{:T(128)} %bitcast.45, s32[]{:T(128)} %bitcast.46, pred[]{:T(512)} %get-tuple-element.199, bf16[2,16,128,128]{3,2,1,0:T(8,128)(2,1)S(1)} %collective-permute-done.2, bf16[2,8,128,128]{3,2,1,0:T(8,128)(2,1)S(1)} %slice_select_fusion), kind=kOutput, calls=%fused_computation.33 | convolution fusion | flops 67633152 | bytes 2654217 | tf_op jit(solution)/shard_map/ab,ebc->eac/dot_general | solution.py:23
  137.8 2.2 %fusion.13 = f32[2,24,128,128]{2,3,1,0:T(8,128)S(1)} fusion(f32[2,24,128,128]{2,3,1,0:T(8,128)S(1)} %fusion.16, s32[]{:T(128)} %bitcast.60, s32[]{:T(128)} %bitcast.61, pred[]{:T(512)} %get-tuple-element.198, bf16[2,16,128,128]{3,2,1,0:T(8,128)(2,1)S(1)} %collective-permute-done.3, bf16[2,8,128,128]{3,2,1,0:T(8,128)(2,1)S(1)} %slice_select_fusion), kind=kOutput, calls=%fused_computation.37 | convolution fusion | flops 67633152 | bytes 2654217 | tf_op jit(solution)/shard_map/ab,ebc->eac/dot_general | solution.py:23
  140.1 2.2 %fusion.10 = f32[2,24,128,128]{2,3,1,0:T(8,128)S(1)} fusion(f32[2,24,128,128]{2,3,1,0:T(8,128)S(1)} %fusion.13, s32[]{:T(128)} %bitcast.67, s32[]{:T(128)} %bitcast.68, pred[]{:T(512)} %get-tuple-element.197, bf16[2,16,128,128]{3,2,1,0:T(8,128)(2,1)S(1)} %collective-permute-done.3, bf16[2,8,128,128]{3,2,1,0:T(8,128)(2,1)S(1)} %slice_select_fusion), kind=kOutput, calls=%fused_computation.34 | convolution fusion | flops 67633152 | bytes 2654217 | tf_op jit(solution)/shard_map/ab,ebc->eac/dot_general | solution.py:23
  143.4 1.7 %copy.20 = bf16[2,24,128,128]{3,2,1,0:T(8,128)(2,1)} copy(f32[2,24,128,128]{2,3,1,0:T(8,128)S(1)} %fusion.14) | data formatting | bytes 4718592 | tf_op jit(solution)/shard_map/scatter-add | solution.py:29
  145.6 0.9 copy-done
  146.7 1.3 slice.801
  148.1 7.3 %reduce-scatter.2.cloned.1.call-done = bf16[2,24,64,128]{3,2,1,0:T(8,128)(2,1)} async-done(((bf16[2,24,128,128]{3,2,1,0:T(8,128)(2,1)}), bf16[2,24,64,128]{3,2,1,0:T(8,128)(2,1)}) %reduce-scatter.2.cloned.1.call-update) | async-done | bytes 786448 | tf_op jit(solution)/shard_map/reduce_scatter | solution.py:55
  155.4 2.2 %select_convert_fusion = bf16[2,24,64,128]{3,2,1,0:T(8,128)(2,1)} fusion(bf16[2,24,64,128]{3,2,1,0:T(8,128)(2,1)} %reduce-scatter.2.cloned.1.call-done, pred[2,24]{1,0:T(4,128)(4,1)S(1)} %iota_compare_fusion), kind=kLoop, calls=%fused_computation.1 | loop fusion | flops 1179648 | bytes 1572912 | tf_op jit(solution)/shard_map/convert_element_type | solution.py:59
  (25 shorter events, 4.5 us)
Async XLA Ops:
  6.5 148.8 %reduce-scatter.2.cloned.1.call-start = ((), (), s32[]{:S(2)}) async-start(), calls=%async_computation.1 | async-start | bytes 2359296 | tf_op jit(solution)/shard_map/reduce_scatter | solution.py:55
  8.6 28.0 %collective-permute-start = (bf16[2,16,128,128]{3,2,1,0:T(8,128)(2,1)S(1)}, bf16[2,16,128,128]{3,2,1,0:T(8,128)(2,1)S(1)}, u32[]{:S(2)}, u32[]{:S(2)}) collective-permute-start(bf16[2,16,128,128]{3,2,1,0:T(8,128)(2,1)S(1)} %broadcast_multiply_fusion), channel_id=1, source_target_pairs={{8,0},{10,2},{12,4},{14,6},{16,8},{18,10},{20,12},{22,14},{24,16},... | collective-permute-start | bytes 3145736 | tf_op jit(solution)/shard_map/ppermute | solution.py:12
  38.0 27.0 %collective-permute-start.1 = (bf16[2,16,128,128]{3,2,1,0:T(8,128)(2,1)S(1)}, bf16[2,16,128,128]{3,2,1,0:T(8,128)(2,1)S(1)}, u32[]{:S(2)}, u32[]{:S(2)}) collective-permute-start(bf16[2,16,128,128]{3,2,1,0:T(8,128)(2,1)S(1)} %broadcast_select_fusion), channel_id=1, source_target_pairs={{2,0},{4,2},{6,4},{8,6},{10,8},{12,10},{14,12},{16,14},{18,16},{20... | collective-permute-start | bytes 3145736 | tf_op jit(solution)/shard_map/ppermute | solution.py:12
  39.9 92.6 %collective-permute-start.2 = (bf16[2,16,128,128]{3,2,1,0:T(8,128)(2,1)S(1)}, bf16[2,16,128,128]{3,2,1,0:T(8,128)(2,1)S(1)}, u32[]{:S(2)}, u32[]{:S(2)}) collective-permute-start(bf16[2,16,128,128]{3,2,1,0:T(8,128)(2,1)S(1)} %broadcast_select_fusion), channel_id=1, source_target_pairs={{4,0},{6,2},{8,4},{10,6},{12,8},{14,10},{16,12},{18,14},{20,16},{2... | collective-permute-start | bytes 3145736 | tf_op jit(solution)/shard_map/ppermute | solution.py:12
  41.2 96.6 %collective-permute-start.3 = (bf16[2,16,128,128]{3,2,1,0:T(8,128)(2,1)S(1)}, bf16[2,16,128,128]{3,2,1,0:T(8,128)(2,1)S(1)}, u32[]{:S(2)}, u32[]{:S(2)}) collective-permute-start(bf16[2,16,128,128]{3,2,1,0:T(8,128)(2,1)S(1)} %broadcast_select_fusion), channel_id=1, source_target_pairs={{6,0},{8,2},{10,4},{12,6},{14,8},{16,10},{18,12},{20,14},{22,16},{... | collective-permute-start | bytes 3145736 | tf_op jit(solution)/shard_map/ppermute | solution.py:12
  42.5 100.5 %collective-permute-start.4 = (bf16[2,16,128,128]{3,2,1,0:T(8,128)(2,1)S(1)}, bf16[2,16,128,128]{3,2,1,0:T(8,128)(2,1)S(1)}, u32[]{:S(2)}, u32[]{:S(2)}) collective-permute-start(bf16[2,16,128,128]{3,2,1,0:T(8,128)(2,1)S(1)} %broadcast_select_fusion), channel_id=1, source_target_pairs={{8,0},{10,2},{12,4},{14,6},{16,8},{18,10},{20,12},{22,14},{24,16},... | collective-permute-start | bytes 3145736 | tf_op jit(solution)/shard_map/ppermute | solution.py:12
  145.1 1.4 copy-start
  146.7 1.3 copy-start.1
Sparse Core Ops, SparseCore 0:
  148.1 7.2 reduce-scatter.1
where the time goes:
time: 165 us; the launch traced here: 164 us
  waiting for transfers between devices  108 us (65%)
  matrix products  18.4 us (11%)
  between operations  13.6 us (8%)
  local copies, waits for them, and re-layouts  9.17 us (6%)
  other arithmetic  8.72 us (5%)
  starting transfers between devices  6.46 us (4%)
    ppermute x5, waiting for transfers between devices, from_behind(): lax.ppermute(value, axis, [(source, source + steps) for source in range(f...  101 us
    dot_general x16, matrix products, contribute(): jnp.einsum('ab,ebc->eac', left_tiles[local_row, k_offset], remote_tiles[r...  18.4 us
    reduce_scatter x1, waiting for transfers between devices, per_device(): lax.psum_scatter(placed[:, :OUT_BAND].astype(jnp.bfloat16), 'depth', scat...  7.28 us
    ppermute x5, starting transfers between devices, from_behind(): lax.ppermute(value, axis, [(source, source + steps) for source in range(f...  6.46 us
    another operation x8, local copies, waits for them, and re-layouts  4.27 us
  transfers between devices with their start and end apart: 6, of which 4 were waited for; matrix products, arithmetic and copies ran while one was open for 16% of the time, Pallas kernels for 0%

commit v1 on v0

v1 whole, which is shorter than its diff:
```python
import functools

import jax
import jax.numpy as jnp
import numpy as np
from jax import lax
from jax.experimental import pallas as pl
from jax.experimental.pallas import tpu as pltpu
from jax.sharding import PartitionSpec as P

OUT_BAND = 24
TILE = 128
SLOTS = 8
SUMS = 16
NO_TERM = 17
RC = ("row", "col")


STEPS = (
    (1, (
        (1, 1, 1), (3, 3, 0), (4, 4, 1), (5, 5, 0), (6, 6, 0), (7, 7, 0), (8, 8, 0), (9, 9, 0),
        (10, 10, 0), (11, 11, 0), (12, 12, 0), (13, 13, 0), (14, 14, 0), (15, 15, 0),
    )),
    (0, (
        (4, 4, 0), (5, 5, 0), (6, 6, 1), (7, 7, 1), (8, 8, 1), (9, 9, 1), (10, 10, 0),
        (11, 11, 1), (12, 12, 0), (13, 13, 0), (14, 14, 0), (15, 15, 0),
    )),
    (5, (
        (2, 2, 1), (5, 5, 0), (6, 6, 0), (8, 8, 0), (9, 9, 0), (10, 10, 1), (11, 11, 1),
        (12, 12, 0), (13, 13, 0), (14, 14, 0), (15, 15, 0),
    )),
    (1, (
        (1, 1, 0), (3, 3, 1), (4, 4, 0), (5, 5, 1), (6, 6, 1), (7, 7, 1), (8, 8, 1), (9, 9, 1),
        (10, 10, 1), (11, 11, 1),
    )),
    (0, (
        (4, 4, 1), (5, 4, 1), (6, 7, 0), (7, 7, 0), (8, 9, 0), (9, 8, 0), (10, 11, 0),
        (11, 11, 0), (12, 13, 0), (13, 12, 0), (14, 15, 0), (15, 14, 0),
    )),
    (6, (
        (1, 9, 0), (2, 6, 1), (4, 5, 0), (5, 5, 1), (6, 7, 0), (8, 8, 1), (9, 9, 1),
        (10, 2, 1), (11, 10, 0), (12, 8, 1), (13, 9, 1), (14, 10, 0), (15, 11, 1),
    )),
    (1, (
        (0, 8, 0), (1, 5, 0), (2, 6, 1), (3, 7, 1), (4, 12, 0), (5, 6, 0), (6, 5, 0),
        (13, 14, 0), (14, 13, 0),
    )),
    (0, (
        (0, 8, 0), (2, 10, 1), (4, 5, 1), (5, 5, 1), (6, 6, 0), (7, 6, 0), (8, 9, 1),
        (11, 10, 1), (13, 14, 0), (14, 13, 0),
    )),
    (6, (
        (1, 4, 1), (2, 3, 1), (5, 4, 0), (6, 7, 1), (8, 13, 0), (9, 8, 1), (10, 10, 1),
        (11, 11, 0), (12, 9, 0), (13, 8, 0), (14, 11, 0), (15, 14, 0),
    )),
    (1, (
        (0, 8, 1), (1, 6, 1), (2, 9, 0), (3, 10, 0), (4, 8, 1), (5, 7, 0), (6, 5, 1),
        (7, 11, 1), (9, 2, 1), (10, 9, 1), (13, 10, 0), (14, 9, 1),
    )),
    (0, (
        (1, 6, 1), (2, 9, 0), (3, 10, 0), (4, 6, 0), (6, 5, 1), (7, 5, 0), (12, 14, 0),
        (13, 10, 0), (15, 13, 0),
    )),
    (6, (
        (1, 8, 0), (2, 2, 0), (5, 12, 0), (6, 10, 1), (10, 15, 0), (12, 9, 1), (14, 15, 0),
        (15, 13, 0),
    )),
    (1, (
        (0, 13, 0), (1, 3, 1), (2, 4, 1), (3, 11, 0), (4, 9, 0), (5, 7, 1), (6, 10, 1),
        (7, 14, 0), (9, 10, 1), (10, 8, 1), (13, 11, 0), (14, 8, 0),
    )),
    (0, (
        (1, 8, 0), (2, 10, 0), (3, 9, 0), (4, 7, 0), (5, 7, 1), (6, 4, 0), (7, 5, 1),
        (12, 10, 0),
    )),
    (6, (
        (2, 3, 0), (5, 8, 1), (6, 11, 1), (8, 2, 1), (9, 12, 0), (10, 11, 1), (11, 9, 1),
        (12, 10, 0), (15, 9, 1),
    )),
    (1, (
        (0, 6, 0), (1, 2, 0), (2, 8, 0), (4, 9, 1), (5, 10, 1), (6, 12, 0), (7, 13, 0),
        (9, 15, 0), (13, 15, 0),
    )),
    (0, (
        (0, 6, 1), (1, 13, 0), (2, 11, 0), (3, 11, 0), (4, 7, 1), (5, 7, 0), (6, 5, 0),
        (7, 10, 1), (12, 11, 0), (13, 11, 0),
    )),
    (4, (
        (1, 8, 1), (2, 4, 0), (11, 8, 1), (12, 11, 0), (13, 11, 0), (14, 8, 0), (15, 8, 0),
    )),
    (1, (
        (0, 2, 1), (1, 3, 0), (2, 4, 0), (3, 9, 1), (4, 10, 0), (5, 11, 1), (6, 8, 1),
        (7, 9, 1), (9, 11, 1), (10, 12, 0),
    )),
)
GROUPS = [0, 8, 13, 17, 19]


def partner(kind, chip):
    z, row = chip % 4, chip // 4
    if kind < 3:
        return chip ^ (4, 1, 8)[kind]
    if z in (1, 2) and (kind - 3) >> (row % 2) & 1:
        return chip ^ 3
    return chip ^ 8


def grid_plan():
    ops = []
    for kind, sends in STEPS:
        sent = {source: (block, part) for source, block, part in sends}
        ops.append([(c, partner(kind, c), sent.get(c)) for c in range(16)])
    groups = [["n0", "n1"]]
    groups += [list(range(a, b)) for a, b in zip(GROUPS, GROUPS[1:])]
    return ops, groups, frozenset(range(12, 16))

def direct_plan(chips):
    ops, groups = [], [["n0", "n1"]]
    for m in range(1, 9):
        for part in range(2 if m < 8 else 1):
            ops.append([(r + m, r, (r + m, part)) for r in range(chips - m)])
        if m % 3 == 0:
            groups.append([])
        if m == 1:
            groups.append([])
        groups[-1] += list(range(len(ops) - (2 if m < 8 else 1), len(ops)))
    return ops, groups, frozenset()


def first_slot(k, core):
    return (k - core + ((core + k) & 1)) // 2


def terms(block, part, chip, packed, core):
    m = block - chip
    if packed:
        ks = [2 * m, 2 * m + 1] if part == 0 else [NO_TERM, NO_TERM]
        at = [first_slot(k, core) for k in ks]
    else:
        ks = [2 * m + part] * 2
        at = [first_slot(ks[0], core), first_slot(ks[0], core) + SLOTS // 2]
    out = []
    for k, slot in zip(ks, at):
        out += [k, slot] if m >= 0 and k < NO_TERM else [NO_TERM, 0]
    return out


def select(index, choices):
    value = choices[-1]
    for i in reversed(range(len(choices) - 1)):
        value = jnp.where(index == i, choices[i], value)
    return value


VMEM = pl.BlockSpec(memory_space=pltpu.VMEM)
SMEM = pl.BlockSpec(memory_space=pltpu.SMEM)


def units_kernel(where_ref, fill_ref, band_ref, *unit_refs):
    for part, unit in enumerate(unit_refs):
        for slot in range(SLOTS):
            at = (part * SLOTS + slot) * 2
            row, entry = where_ref[at], where_ref[at + 1]
            fill = fill_ref[row, entry].astype(jnp.float32)
            tile = band_ref[row, entry].astype(jnp.float32) * fill
            unit[:, slot * TILE : (slot + 1) * TILE] = tile.astype(jnp.bfloat16)


def add_terms(table_ref, base, left_ref, units, sums):
    for i, unit in enumerate(units):
        for half in range(2):
            at = (base + i) * 4 + half * 2
            k, slot = table_ref[at], table_ref[at + 1]

            @pl.when(k < NO_TERM)
            def _(k=k, slot=slot, unit=unit, half=half):
                width = SLOTS // 2 * TILE
                product = jnp.dot(
                    left_ref[k],
                    unit[:, half * width : (half + 1) * width],
                    preferred_element_type=jnp.float32,
                )
                for q in range(SLOTS // 2):
                    sums[slot + q] += product[:, q * TILE : (q + 1) * TILE]


def first_kernel(base, table_ref, fill_ref, band_ref, *refs):
    units, (left, sums) = refs[:-2], refs[-2:]
    zero = jnp.zeros((TILE, TILE), jnp.bfloat16)
    left[0, TILE:] = zero
    left[16, :TILE] = zero
    for row in range(2):
        for entry in range(16):
            fill = fill_ref[row, entry].astype(jnp.float32)
            tile = band_ref[row, entry].astype(jnp.float32) * fill
            left[entry + row, row * TILE : (row + 1) * TILE] = tile.astype(jnp.bfloat16)
    sums[...] = jnp.zeros(sums.shape, jnp.float32)
    add_terms(table_ref, base, left, units, sums)


def more_kernel(base, table_ref, left_ref, *refs):
    units, sums_in, sums = refs[:-2], refs[-2], refs[-1]
    sums[...] = sums_in[...]
    add_terms(table_ref, base, left_ref, units, sums)


def last_kernel(base, table_ref, reach_ref, core_ref, left_ref, *refs):
    units, sums_in, kept, given, sums = refs[:-4], refs[-4], refs[-3], refs[-2], refs[-1]
    sums[...] = sums_in[...]
    add_terms(table_ref, base, left_ref, units, sums)
    core = core_ref[0]
    half = TILE // 2
    for row in range(2):
        odd = core if row == 0 else 1 - core
        shift = 0 if row == 0 else 1 - core
        for s in range(OUT_BAND // 2):
            keep = 2 * s + odd < reach_ref[row]
            for out, side in ((kept, core), (given, 1 - core)):
                start = pl.multiple_of(row * TILE + side * half, half)
                tile = sums[s + shift, pl.ds(start, half), :]
                out[row, s] = jnp.where(keep, tile, 0.0).astype(jnp.bfloat16)


def join_kernel(core_ref, kept_ref, taken_ref, out_ref):
    core = core_ref[0]
    for row in range(2):
        odd = core if row == 0 else 1 - core
        for s in range(OUT_BAND // 2):
            out_ref[row, 2 * s + odd] = kept_ref[row, s]
            out_ref[row, 2 * s + 1 - odd] = taken_ref[row, s]


def per_device(plan, chips, a_band, a_fill, c_reach):
    ops, groups, packed = plan
    core = lax.axis_index("depth")
    chip = lax.axis_index(RC)
    params = pltpu.CompilerParams(vmem_limit_bytes=48 * 2**20)

    where = np.zeros((chips, 2, 2, SLOTS, 2), np.int32)
    for r in range(chips):
        for c in range(2):
            for part in range(2):
                for t in range(SLOTS):
                    h = part
                    if r in packed and part == 0:
                        h = t // 4
                    e = t % 4 if r in packed and part == 0 else t
                    where[r, c, part, t] = (h, 2 * e + ((c + h) & 1))
    where = jnp.asarray(where.reshape(chips, 2, -1))[chip, core]

    held = {"n0": [(r, 0) for r in range(chips)], "n1": [(r, 1) for r in range(chips)]}
    picks = np.zeros((chips, max(1, len(ops))), np.int32)
    choices = []
    for o, moves in enumerate(ops):
        names = []
        got = [None] * chips
        for source, target, unit in moves:
            if unit is None:
                continue
            name = next(n for n, h in held.items() if h[source] == unit)
            if name not in names:
                names.append(name)
            picks[source, o] = names.index(name)
            got[target] = unit
        held[o] = got
        choices.append(names)
    order = [n for group in groups for n in group]
    table = np.full((chips, 2, len(order), 4), NO_TERM, np.int32)
    for r in range(chips):
        done = set()
        for i, n in enumerate(order):
            unit = held[n][r]
            if unit is None or unit in done:
                continue
            done.add(unit)
            for c in range(2):
                table[r, c, i] = terms(*unit, r, unit[0] in packed, c)
    table = jnp.asarray(table.reshape(chips, 2, -1))[chip, core]
    picks = jnp.asarray(picks)[chip]

    unit_shape = jax.ShapeDtypeStruct((TILE, SLOTS * TILE), jnp.bfloat16)
    sums_shape = jax.ShapeDtypeStruct((SUMS, 2 * TILE, TILE), jnp.float32)
    n0, n1 = pl.pallas_call(
        units_kernel,
        out_shape=(unit_shape, unit_shape),
        in_specs=[SMEM, SMEM, VMEM],
        out_specs=(VMEM, VMEM),
        compiler_params=params,
        name="units",
    )(where, a_fill, a_band)
    buffers = {"n0": n0, "n1": n1}
    for o, moves in enumerate(ops):
        payload = select(picks[o], [buffers[n] for n in choices[o]])
        buffers[o] = lax.ppermute(payload, RC, [(s, t) for s, t, _ in moves])

    core_arg = core.reshape(1).astype(jnp.int32)
    base = 0
    for g, group in enumerate(groups):
        units = [buffers[n] for n in group]
        if g == 0:
            left, sums = pl.pallas_call(
                functools.partial(first_kernel, base),
                out_shape=(jax.ShapeDtypeStruct((17, 2 * TILE, TILE), jnp.bfloat16), sums_shape),
                in_specs=[SMEM, SMEM, VMEM] + [VMEM] * len(units),
                out_specs=(VMEM, VMEM),
                compiler_params=params,
                name="first",
            )(table, a_fill, a_band, *units)
        elif g < len(groups) - 1:
            sums = pl.pallas_call(
                functools.partial(more_kernel, base),
                out_shape=sums_shape,
                in_specs=[SMEM, VMEM] + [VMEM] * (len(units) + 1),
                out_specs=VMEM,
                compiler_params=params,
                name="more",
            )(table, left, *units, sums)
        else:
            piece = jax.ShapeDtypeStruct((2, OUT_BAND // 2, TILE // 2, TILE), jnp.bfloat16)
            kept, given = pl.pallas_call(
                functools.partial(last_kernel, base),
                out_shape=(piece, piece),
                in_specs=[SMEM, SMEM, SMEM, VMEM] + [VMEM] * (len(units) + 1),
                out_specs=(VMEM, VMEM),
                scratch_shapes=[pltpu.VMEM(sums_shape.shape, jnp.float32)],
                compiler_params=params,
                name="last",
            )(table, c_reach, core_arg, left, *units, sums)
        base += len(group)
    taken = lax.ppermute(given, "depth", [(0, 1), (1, 0)])
    return pl.pallas_call(
        join_kernel,
        out_shape=jax.ShapeDtypeStruct((2, OUT_BAND, TILE // 2, TILE), jnp.bfloat16),
        in_specs=[SMEM, VMEM, VMEM],
        out_specs=VMEM,
        compiler_params=params,
        name="join",
    )(core_arg, kept, taken)


def solution(mesh):
    rows, cols = mesh.shape["row"], mesh.shape["col"]
    plan = grid_plan() if (rows, cols) == (4, 4) else direct_plan(rows * cols)
    in_specs = (P(RC, None, None, None), P(RC, None), P(RC))
    out_specs = P(RC, None, "depth", None)
    return jax.shard_map(
        functools.partial(per_device, plan, rows * cols),
        mesh=mesh,
        in_specs=in_specs,
        out_specs=out_specs,
        check_vma=False,
    )
```

time: 165 us -> 88.4 us (0.54)
  waiting for transfers between devices: 108 us -> 13.1 us
  starting transfers between devices: 6.46 us -> 25.8 us
  matrix products: 18.4 us -> 0 us
  Pallas kernels: 0 us -> 15.8 us
  between operations: 13.6 us -> 23.7 us
  other arithmetic: 8.72 us -> 0.54 us
    ppermute x5 -> x20, waiting for transfers between devices: 101 us -> 13.1 us  [the longest x19 11.4 us: per_device(): buffers[o] = lax.ppermute(payload, RC, [(s, t) for s, t, _ in moves])]
    ppermute x5 -> x20, starting transfers between devices: 6.46 us -> 25.8 us  [the longest x19 25.8 us: per_device(): buffers[o] = lax.ppermute(payload, RC, [(s, t) for s, t, _ in moves])]
    dot_general x16 -> x0, matrix products: 18.4 us -> none  [contribute(): jnp.einsum('ab,ebc->eac', left_tiles[local_row, k_offset], remote_tiles[r...]
    pallas_call x0 -> x7, Pallas kernels: none -> 15.8 us  [the longest x3 11.3 us: per_device(): pl.pallas_call(functools.partial(more_kernel, base), out_shape=sums_shape...]
    reduce_scatter x1 -> x0, waiting for transfers between devices: 7.28 us -> none  [per_device(): lax.psum_scatter(placed[:, :OUT_BAND].astype(jnp.bfloat16), 'depth', scat...]
    unnamed x4 -> x12, local copies, waits for them, and re-layouts: 0.91 us -> 5.94 us
    another operation x8 -> x0, local copies, waits for them, and re-layouts: 4.27 us -> none
    another operation x5 -> x0, other arithmetic: 2.92 us -> none
  transfers between devices with their start and end apart: 6 -> 20, of which waited for: 4 -> 8; matrix products, arithmetic and copies ran while one was open for 16% -> 1% of each run, Pallas kernels for 0% -> 15%
where the time goes in v1:
time: 88.4 us; the launch traced here: 87.8 us
  starting transfers between devices  25.8 us (29%)
  between operations  23.7 us (27%)
  Pallas kernels  15.8 us (18%)
  waiting for transfers between devices  13.1 us (15%)
  local copies, waits for them, and re-layouts  8.72 us (10%)
    ppermute x19, starting transfers between devices, per_device(): buffers[o] = lax.ppermute(payload, RC, [(s, t) for s, t, _ in moves])  25.8 us
    ppermute x19, waiting for transfers between devices, per_device(): buffers[o] = lax.ppermute(payload, RC, [(s, t) for s, t, _ in moves])  11.4 us
    pallas_call x3, Pallas kernels, per_device(): pl.pallas_call(functools.partial(more_kernel, base), out_shape=sums_shape...  11.3 us
    unnamed x12, local copies, waits for them, and re-layouts  5.94 us
  transfers between devices with their start and end apart: 20, of which 8 were waited for; matrix products, arithmetic and copies ran while one was open for 1% of the time, Pallas kernels for 15%

profile of v1, /device:TPU:0, one launch (start us, length us, event | category | flops | bytes accessed | tf_op | source)
XLA Modules:
  0.0 87.8 jit_solution(2057771053866398183)
XLA Ops:
  0.7 0.7 fusion.2
  3.2 0.7 fusion.1.where_ref
  3.9 1.2 %copy-done.2 = bf16[2,16,128,128]{3,2,1,0:T(8,128)(2,1)S(1)} copy-done((bf16[2,16,128,128]{3,2,1,0:T(8,128)(2,1)S(1)}, bf16[2,16,128,128]{3,2,1,0:T(8,128)(2,1)}, u32[]{:S(2)}) %copy-start.2) | copy-done | bytes 1048600
  6.6 3.0 %collective-permute-start = (bf16[128,1024]{1,0:T(8,128)(2,1)S(1)}, bf16[128,1024]{1,0:T(8,128)(2,1)S(1)}, u32[]{:S(2)}, u32[]{:S(2)}) collective-permute-start(bf16[128,1024]{1,0:T(8,128)(2,1)S(1)} %get-tuple-element.28), channel_id=1, source_target_pairs={{0,16},{2,18},{4,20},{6,22},{8,24},{10,12},{12,10},{14,30},{16,0},... | collective-permute-start | bytes 786440 | tf_op jit(solution)/shard_map/ppermute | solution.py:294
  9.6 1.6 %collective-permute-start.2 = (bf16[128,1024]{1,0:T(8,128)(2,1)S(1)}, bf16[128,1024]{1,0:T(8,128)(2,1)S(1)}, u32[]{:S(2)}, u32[]{:S(2)}) collective-permute-start(bf16[128,1024]{1,0:T(8,128)(2,1)S(1)} %get-tuple-element.26), channel_id=1, source_target_pairs={{0,2},{2,0},{4,6},{6,4},{8,10},{10,8},{12,14},{14,12},{16,18},{18,... | collective-permute-start | bytes 786440 | tf_op jit(solution)/shard_map/ppermute | solution.py:294
  11.2 1.5 %collective-permute-start.1 = (bf16[128,1024]{1,0:T(8,128)(2,1)S(1)}, bf16[128,1024]{1,0:T(8,128)(2,1)S(1)}, u32[]{:S(2)}, u32[]{:S(2)}) collective-permute-start(bf16[128,1024]{1,0:T(8,128)(2,1)S(1)} %get-tuple-element.27), channel_id=1, source_target_pairs={{0,8},{2,10},{4,12},{6,14},{8,0},{10,2},{12,4},{14,6},{16,24},{18,... | collective-permute-start | bytes 786440 | tf_op jit(solution)/shard_map/ppermute | solution.py:294
  17.4 1.3 %collective-permute-done.1.refs_1_ = bf16[128,1024]{1,0:T(8,128)(2,1)S(1)} collective-permute-done((bf16[128,1024]{1,0:T(8,128)(2,1)S(1)}, bf16[128,1024]{1,0:T(8,128)(2,1)S(1)}, u32[]{:S(2)}, u32[]{:S(2)}) %collective-permute-start.1) | collective-permute-done | bytes 262176 | tf_op jit(solution)/shard_map/ppermute | solution.py:294
  18.8 1.4 %collective-permute-start.3 = (bf16[128,1024]{1,0:T(8,128)(2,1)S(1)}, bf16[128,1024]{1,0:T(8,128)(2,1)S(1)}, u32[]{:S(2)}, u32[]{:S(2)}) collective-permute-start(bf16[128,1024]{1,0:T(8,128)(2,1)S(1)} %get-tuple-element.24), channel_id=1, source_target_pairs={{0,16},{2,4},{4,2},{6,22},{8,24},{10,12},{12,10},{14,30},{16,0},{1... | collective-permute-start | bytes 786440 | tf_op jit(solution)/shard_map/ppermute | solution.py:294
  20.2 1.7 %collective-permute-start.6 = (bf16[128,1024]{1,0:T(8,128)(2,1)S(1)}, bf16[128,1024]{1,0:T(8,128)(2,1)S(1)}, u32[]{:S(2)}, u32[]{:S(2)}) collective-permute-start(bf16[128,1024]{1,0:T(8,128)(2,1)S(1)} %get-tuple-element.23), channel_id=1, source_target_pairs={{0,8},{2,10},{4,12},{6,14},{8,0},{10,2},{12,4},{14,6},{16,24},{18,... | collective-permute-start | bytes 786440 | tf_op jit(solution)/shard_map/ppermute | solution.py:294
  21.9 1.6 %collective-permute-start.7 = (bf16[128,1024]{1,0:T(8,128)(2,1)S(1)}, bf16[128,1024]{1,0:T(8,128)(2,1)S(1)}, u32[]{:S(2)}, u32[]{:S(2)}) collective-permute-start(bf16[128,1024]{1,0:T(8,128)(2,1)S(1)} %get-tuple-element.22), channel_id=1, source_target_pairs={{0,2},{2,0},{4,6},{6,4},{8,10},{10,8},{12,14},{14,12},{16,18},{18,... | collective-permute-start | bytes 786440 | tf_op jit(solution)/shard_map/ppermute | solution.py:294
  23.5 1.9 %collective-permute-done.3.refs_5_ = bf16[128,1024]{1,0:T(8,128)(2,1)S(1)} collective-permute-done((bf16[128,1024]{1,0:T(8,128)(2,1)S(1)}, bf16[128,1024]{1,0:T(8,128)(2,1)S(1)}, u32[]{:S(2)}, u32[]{:S(2)}) %collective-permute-start.3) | collective-permute-done | bytes 262176 | tf_op jit(solution)/shard_map/ppermute | solution.py:294
  25.4 1.4 %collective-permute-start.4 = (bf16[128,1024]{1,0:T(8,128)(2,1)S(1)}, bf16[128,1024]{1,0:T(8,128)(2,1)S(1)}, u32[]{:S(2)}, u32[]{:S(2)}) collective-permute-start(bf16[128,1024]{1,0:T(8,128)(2,1)S(1)} %collective-permute-done.3.refs_5_), channel_id=1, source_target_pairs={{0,2},{2,0},{4,6},{6,4},{8,10},{10,8},{12,14},{14,12},{16,18},{18,... | collective-permute-start | bytes 786440 | tf_op jit(solution)/shard_map/ppermute | solution.py:294
  34.6 1.4 %collective-permute-start.10 = (bf16[128,1024]{1,0:T(8,128)(2,1)S(1)}, bf16[128,1024]{1,0:T(8,128)(2,1)S(1)}, u32[]{:S(2)}, u32[]{:S(2)}) collective-permute-start(bf16[128,1024]{1,0:T(8,128)(2,1)S(1)} %get-tuple-element.17), channel_id=1, source_target_pairs={{0,8},{2,10},{4,12},{6,14},{8,0},{10,2},{12,4},{14,6},{16,24},{18,... | collective-permute-start | bytes 786440 | tf_op jit(solution)/shard_map/ppermute | solution.py:294
  36.0 1.5 %collective-permute-start.8 = (bf16[128,1024]{1,0:T(8,128)(2,1)S(1)}, bf16[128,1024]{1,0:T(8,128)(2,1)S(1)}, u32[]{:S(2)}, u32[]{:S(2)}) collective-permute-start(bf16[128,1024]{1,0:T(8,128)(2,1)S(1)} %get-tuple-element.18), channel_id=1, source_target_pairs={{0,16},{2,4},{4,2},{6,22},{8,24},{10,12},{12,10},{14,30},{16,0},{1... | collective-permute-start | bytes 786440 | tf_op jit(solution)/shard_map/ppermute | solution.py:294
  42.4 1.6 %collective-permute-done.8.refs_0_ = bf16[128,1024]{1,0:T(8,128)(2,1)S(1)} collective-permute-done((bf16[128,1024]{1,0:T(8,128)(2,1)S(1)}, bf16[128,1024]{1,0:T(8,128)(2,1)S(1)}, u32[]{:S(2)}, u32[]{:S(2)}) %collective-permute-start.8) | collective-permute-done | bytes 262176 | tf_op jit(solution)/shard_map/ppermute | solution.py:294
  44.1 1.5 %collective-permute-start.11 = (bf16[128,1024]{1,0:T(8,128)(2,1)S(1)}, bf16[128,1024]{1,0:T(8,128)(2,1)S(1)}, u32[]{:S(2)}, u32[]{:S(2)}) collective-permute-start(bf16[128,1024]{1,0:T(8,128)(2,1)S(1)} %get-tuple-element.32), channel_id=1, source_target_pairs={{0,2},{2,0},{4,6},{6,4},{8,10},{10,8},{12,14},{14,12},{16,18},{18,... | collective-permute-start | bytes 786440 | tf_op jit(solution)/shard_map/ppermute | solution.py:294
  45.7 2.6 %collective-permute-start.9 = (bf16[128,1024]{1,0:T(8,128)(2,1)S(1)}, bf16[128,1024]{1,0:T(8,128)(2,1)S(1)}, u32[]{:S(2)}, u32[]{:S(2)}) collective-permute-start(bf16[128,1024]{1,0:T(8,128)(2,1)S(1)} %get-tuple-element.33), channel_id=1, source_target_pairs={{0,8},{2,10},{4,12},{6,14},{8,0},{10,2},{12,4},{14,6},{16,24},{18,... | collective-permute-start | bytes 786440 | tf_op jit(solution)/shard_map/ppermute | solution.py:294
  54.3 1.2 %collective-permute-done.9.refs_0_ = bf16[128,1024]{1,0:T(8,128)(2,1)S(1)} collective-permute-done((bf16[128,1024]{1,0:T(8,128)(2,1)S(1)}, bf16[128,1024]{1,0:T(8,128)(2,1)S(1)}, u32[]{:S(2)}, u32[]{:S(2)}) %collective-permute-start.9) | collective-permute-done | bytes 262176 | tf_op jit(solution)/shard_map/ppermute | solution.py:294
  55.6 2.1 %collective-permute-start.15 = (bf16[128,1024]{1,0:T(8,128)(2,1)S(1)}, bf16[128,1024]{1,0:T(8,128)(2,1)S(1)}, u32[]{:S(2)}, u32[]{:S(2)}) collective-permute-start(bf16[128,1024]{1,0:T(8,128)(2,1)S(1)} %get-tuple-element.30), channel_id=1, source_target_pairs={{0,8},{2,10},{4,12},{6,14},{8,0},{10,2},{12,4},{14,6},{16,24},{18,... | collective-permute-start | bytes 786440 | tf_op jit(solution)/shard_map/ppermute | solution.py:294
  58.4 4.7 %collective-permute-done.16.refs_3_ = bf16[128,1024]{1,0:T(8,128)(2,1)S(1)} collective-permute-done((bf16[128,1024]{1,0:T(8,128)(2,1)S(1)}, bf16[128,1024]{1,0:T(8,128)(2,1)S(1)}, u32[]{:S(2)}, u32[]{:S(2)}) %collective-permute-start.16) | collective-permute-done | bytes 262176 | tf_op jit(solution)/shard_map/ppermute | solution.py:294
  63.2 1.3 %collective-permute-start.12 = (bf16[128,1024]{1,0:T(8,128)(2,1)S(1)}, bf16[128,1024]{1,0:T(8,128)(2,1)S(1)}, u32[]{:S(2)}, u32[]{:S(2)}) collective-permute-start(bf16[128,1024]{1,0:T(8,128)(2,1)S(1)} %get-tuple-element.21), channel_id=1, source_target_pairs={{0,16},{2,4},{4,2},{6,22},{8,24},{10,26},{12,28},{14,30},{16,0},{1... | collective-permute-start | bytes 786440 | tf_op jit(solution)/shard_map/ppermute | solution.py:294
  64.5 1.5 %collective-permute-start.14 = (bf16[128,1024]{1,0:T(8,128)(2,1)S(1)}, bf16[128,1024]{1,0:T(8,128)(2,1)S(1)}, u32[]{:S(2)}, u32[]{:S(2)}) collective-permute-start(bf16[128,1024]{1,0:T(8,128)(2,1)S(1)} %get-tuple-element.29), channel_id=1, source_target_pairs={{0,2},{2,0},{4,6},{6,4},{8,10},{10,8},{12,14},{14,12},{16,18},{18,... | collective-permute-start | bytes 786440 | tf_op jit(solution)/shard_map/ppermute | solution.py:294
  66.7 1.7 %first.1 = (bf16[17,256,128]{2,1,0:T(8,128)(2,1)S(1)}, f32[16,256,128]{2,1,0:T(8,128)S(1)}) custom-call(s32[84]{0:T(128)S(1)} %fusion.table_ref, s32[2,16]{1,0:T(2,128)S(1)} %copy-done.4, bf16[2,16,128,128]{3,2,1,0:T(8,128)(2,1)S(1)} %copy-done.2, bf16[128,1024]{1,0:T(8,128)(2,1)S(1)} %get-tuple-element.11.refs_0_, ...), custom_call_target="tpu_custom_call" | custom-call | tf_op jit(solution)/shard_map/first/pallas_call | solution.py:301
  68.4 1.3 %copy-done.3 = f32[16,256,128]{2,1,0:T(8,128)} copy-done((f32[16,256,128]{2,1,0:T(8,128)}, f32[16,256,128]{2,1,0:T(8,128)S(1)}, u32[]{:S(2)}) %copy-start.3) | copy-done | bytes 2097176
  69.7 4.7 %more.3.refs_5_ = f32[16,256,128]{2,1,0:T(8,128)S(1)} custom-call(s32[84]{0:T(128)S(1)} %fusion.table_ref, bf16[17,256,128]{2,1,0:T(8,128)(2,1)S(1)} %get-tuple-element.13.left_ref, bf16[128,1024]{1,0:T(8,128)(2,1)S(1)} %collective-permute-done.2.refs_0_, bf16[128,1024]{1,0:T(8,128)(2,1)S(1)} %collective-permute-done.1.refs_1_, ...), custom_call_target="tpu_custom_call" | custom-call | tf_op jit(solution)/shard_map/more/pallas_call | solution.py:310
  74.5 1.3 %copy-done.1 = f32[16,256,128]{2,1,0:T(8,128)} copy-done((f32[16,256,128]{2,1,0:T(8,128)}, f32[16,256,128]{2,1,0:T(8,128)S(1)}, u32[]{:S(2)}) %copy-start.1) | copy-done | bytes 2097176
  75.8 3.0 %more.4.refs_4_ = f32[16,256,128]{2,1,0:T(8,128)S(1)} custom-call(s32[84]{0:T(128)S(1)} %fusion.table_ref, bf16[17,256,128]{2,1,0:T(8,128)(2,1)S(1)} %get-tuple-element.13.left_ref, bf16[128,1024]{1,0:T(8,128)(2,1)S(1)} %collective-permute-done.8.refs_0_, bf16[128,1024]{1,0:T(8,128)(2,1)S(1)} %collective-permute-done.4.refs_1_, ...), custom_call_target="tpu_custom_call" | custom-call | tf_op jit(solution)/shard_map/more/pallas_call | solution.py:310
  78.9 1.3 %copy-done = f32[16,256,128]{2,1,0:T(8,128)} copy-done((f32[16,256,128]{2,1,0:T(8,128)}, f32[16,256,128]{2,1,0:T(8,128)S(1)}, u32[]{:S(2)}) %copy-start) | copy-done | bytes 2097176
  80.3 3.5 %more.5.refs_2_ = f32[16,256,128]{2,1,0:T(8,128)S(1)} custom-call(s32[84]{0:T(128)S(1)} %fusion.table_ref, bf16[17,256,128]{2,1,0:T(8,128)(2,1)S(1)} %get-tuple-element.13.left_ref, bf16[128,1024]{1,0:T(8,128)(2,1)S(1)} %collective-permute-done.9.refs_0_, bf16[128,1024]{1,0:T(8,128)(2,1)S(1)} %collective-permute-done.13.refs_1_, ...), custom_call_target="tpu_custom_call" | custom-call | tf_op jit(solution)/shard_map/more/pallas_call | solution.py:310
  83.8 1.3 %last.1 = (bf16[2,12,64,128]{3,2,1,0:T(8,128)(2,1)S(1)}, bf16[2,12,64,128]{3,2,1,0:T(8,128)(2,1)S(1)}) custom-call(s32[84]{0:T(128)S(1)} %fusion.table_ref, s32[2]{0:T(128)S(1)} %copy-done.5, s32[1]{0:T(128)} %bitcast.core_ref, bf16[17,256,128]{2,1,0:T(8,128)(2,1)S(1)} %get-tuple-element.13.left_ref, bf16[128,1024]{1,0:T(8,128)(2,1)S(1)} %collective-permute-done.12.refs_0_, ...), custom_call_target="tpu_custom_call" | custom-call | tf_op jit(solution)/shard_map/last/pallas_call | solution.py:320
  85.1 1.7 %collective-permute-done.19.taken_ref = bf16[2,12,64,128]{3,2,1,0:T(8,128)(2,1)S(1)} collective-permute-done((bf16[2,12,64,128]{3,2,1,0:T(8,128)(2,1)S(1)}, bf16[2,12,64,128]{3,2,1,0:T(8,128)(2,1)S(1)}, u32[]{:S(2)}, u32[]{:S(2)}) %collective-permute-start.19) | collective-permute-done | bytes 393248 | tf_op jit(solution)/shard_map/ppermute | solution.py:330
  86.8 0.9 %join.1 = bf16[2,24,64,128]{3,2,1,0:T(8,128)(2,1)} custom-call(s32[1]{0:T(128)} %bitcast.core_ref, bf16[2,12,64,128]{3,2,1,0:T(8,128)(2,1)S(1)} %get-tuple-element.15.kept_ref, bf16[2,12,64,128]{3,2,1,0:T(8,128)(2,1)S(1)} %collective-permute-done.19.taken_ref), custom_call_target="tpu_custom_call" | custom-call | tf_op jit(solution)/shard_map/join/pallas_call | solution.py:331
  (37 shorter events, 5.5 us)
Async XLA Ops:
  3.9 1.2 %copy-start.2 = (bf16[2,16,128,128]{3,2,1,0:T(8,128)(2,1)S(1)}, bf16[2,16,128,128]{3,2,1,0:T(8,128)(2,1)}, u32[]{:S(2)}) copy-start(bf16[2,16,128,128]{3,2,1,0:T(8,128)(2,1)} %band_ref.3) | copy-start | bytes 3145732
  5.1 0.7 copy-start.4
  6.6 10.4 %collective-permute-start = (bf16[128,1024]{1,0:T(8,128)(2,1)S(1)}, bf16[128,1024]{1,0:T(8,128)(2,1)S(1)}, u32[]{:S(2)}, u32[]{:S(2)}) collective-permute-start(bf16[128,1024]{1,0:T(8,128)(2,1)S(1)} %get-tuple-element.28), channel_id=1, source_target_pairs={{0,16},{2,18},{4,20},{6,22},{8,24},{10,12},{12,10},{14,30},{16,0},... | collective-permute-start | bytes 786440 | tf_op jit(solution)/shard_map/ppermute | solution.py:294
  9.6 7.8 %collective-permute-start.2 = (bf16[128,1024]{1,0:T(8,128)(2,1)S(1)}, bf16[128,1024]{1,0:T(8,128)(2,1)S(1)}, u32[]{:S(2)}, u32[]{:S(2)}) collective-permute-start(bf16[128,1024]{1,0:T(8,128)(2,1)S(1)} %get-tuple-element.26), channel_id=1, source_target_pairs={{0,2},{2,0},{4,6},{6,4},{8,10},{10,8},{12,14},{14,12},{16,18},{18,... | collective-permute-start | bytes 786440 | tf_op jit(solution)/shard_map/ppermute | solution.py:294
  11.2 7.5 %collective-permute-start.1 = (bf16[128,1024]{1,0:T(8,128)(2,1)S(1)}, bf16[128,1024]{1,0:T(8,128)(2,1)S(1)}, u32[]{:S(2)}, u32[]{:S(2)}) collective-permute-start(bf16[128,1024]{1,0:T(8,128)(2,1)S(1)} %get-tuple-element.27), channel_id=1, source_target_pairs={{0,8},{2,10},{4,12},{6,14},{8,0},{10,2},{12,4},{14,6},{16,24},{18,... | collective-permute-start | bytes 786440 | tf_op jit(solution)/shard_map/ppermute | solution.py:294
  18.8 6.6 %collective-permute-start.3 = (bf16[128,1024]{1,0:T(8,128)(2,1)S(1)}, bf16[128,1024]{1,0:T(8,128)(2,1)S(1)}, u32[]{:S(2)}, u32[]{:S(2)}) collective-permute-start(bf16[128,1024]{1,0:T(8,128)(2,1)S(1)} %get-tuple-element.24), channel_id=1, source_target_pairs={{0,16},{2,4},{4,2},{6,22},{8,24},{10,12},{12,10},{14,30},{16,0},{1... | collective-permute-start | bytes 786440 | tf_op jit(solution)/shard_map/ppermute | solution.py:294
  20.2 14.1 %collective-permute-start.6 = (bf16[128,1024]{1,0:T(8,128)(2,1)S(1)}, bf16[128,1024]{1,0:T(8,128)(2,1)S(1)}, u32[]{:S(2)}, u32[]{:S(2)}) collective-permute-start(bf16[128,1024]{1,0:T(8,128)(2,1)S(1)} %get-tuple-element.23), channel_id=1, source_target_pairs={{0,8},{2,10},{4,12},{6,14},{8,0},{10,2},{12,4},{14,6},{16,24},{18,... | collective-permute-start | bytes 786440 | tf_op jit(solution)/shard_map/ppermute | solution.py:294
  21.9 12.3 %collective-permute-start.7 = (bf16[128,1024]{1,0:T(8,128)(2,1)S(1)}, bf16[128,1024]{1,0:T(8,128)(2,1)S(1)}, u32[]{:S(2)}, u32[]{:S(2)}) collective-permute-start(bf16[128,1024]{1,0:T(8,128)(2,1)S(1)} %get-tuple-element.22), channel_id=1, source_target_pairs={{0,2},{2,0},{4,6},{6,4},{8,10},{10,8},{12,14},{14,12},{16,18},{18,... | collective-permute-start | bytes 786440 | tf_op jit(solution)/shard_map/ppermute | solution.py:294
  25.4 9.0 %collective-permute-start.4 = (bf16[128,1024]{1,0:T(8,128)(2,1)S(1)}, bf16[128,1024]{1,0:T(8,128)(2,1)S(1)}, u32[]{:S(2)}, u32[]{:S(2)}) collective-permute-start(bf16[128,1024]{1,0:T(8,128)(2,1)S(1)} %collective-permute-done.3.refs_5_), channel_id=1, source_target_pairs={{0,2},{2,0},{4,6},{6,4},{8,10},{10,8},{12,14},{14,12},{16,18},{18,... | collective-permute-start | bytes 786440 | tf_op jit(solution)/shard_map/ppermute | solution.py:294
  33.6 8.8 %collective-permute-start.5 = (bf16[128,1024]{1,0:T(8,128)(2,1)S(1)}, bf16[128,1024]{1,0:T(8,128)(2,1)S(1)}, u32[]{:S(2)}, u32[]{:S(2)}) collective-permute-start(bf16[128,1024]{1,0:T(8,128)(2,1)S(1)} %get-tuple-element.25), channel_id=1, source_target_pairs={{0,2},{2,0},{4,6},{6,4},{8,10},{10,8},{12,14},{14,12},{16,18},{18,... | collective-permute-start | bytes 786440 | tf_op jit(solution)/shard_map/ppermute | solution.py:294
  34.6 7.8 %collective-permute-start.10 = (bf16[128,1024]{1,0:T(8,128)(2,1)S(1)}, bf16[128,1024]{1,0:T(8,128)(2,1)S(1)}, u32[]{:S(2)}, u32[]{:S(2)}) collective-permute-start(bf16[128,1024]{1,0:T(8,128)(2,1)S(1)} %get-tuple-element.17), channel_id=1, source_target_pairs={{0,8},{2,10},{4,12},{6,14},{8,0},{10,2},{12,4},{14,6},{16,24},{18,... | collective-permute-start | bytes 786440 | tf_op jit(solution)/shard_map/ppermute | solution.py:294
  36.0 8.0 %collective-permute-start.8 = (bf16[128,1024]{1,0:T(8,128)(2,1)S(1)}, bf16[128,1024]{1,0:T(8,128)(2,1)S(1)}, u32[]{:S(2)}, u32[]{:S(2)}) collective-permute-start(bf16[128,1024]{1,0:T(8,128)(2,1)S(1)} %get-tuple-element.18), channel_id=1, source_target_pairs={{0,16},{2,4},{4,2},{6,22},{8,24},{10,12},{12,10},{14,30},{16,0},{1... | collective-permute-start | bytes 786440 | tf_op jit(solution)/shard_map/ppermute | solution.py:294
  41.8 12.4 %collective-permute-start.13 = (bf16[128,1024]{1,0:T(8,128)(2,1)S(1)}, bf16[128,1024]{1,0:T(8,128)(2,1)S(1)}, u32[]{:S(2)}, u32[]{:S(2)}) collective-permute-start(bf16[128,1024]{1,0:T(8,128)(2,1)S(1)} %get-tuple-element.19), channel_id=1, source_target_pairs={{0,16},{2,4},{4,2},{6,22},{8,24},{10,12},{12,10},{14,30},{16,0},{1... | collective-permute-start | bytes 786440 | tf_op jit(solution)/shard_map/ppermute | solution.py:294
  44.1 10.1 %collective-permute-start.11 = (bf16[128,1024]{1,0:T(8,128)(2,1)S(1)}, bf16[128,1024]{1,0:T(8,128)(2,1)S(1)}, u32[]{:S(2)}, u32[]{:S(2)}) collective-permute-start(bf16[128,1024]{1,0:T(8,128)(2,1)S(1)} %get-tuple-element.32), channel_id=1, source_target_pairs={{0,2},{2,0},{4,6},{6,4},{8,10},{10,8},{12,14},{14,12},{16,18},{18,... | collective-permute-start | bytes 786440 | tf_op jit(solution)/shard_map/ppermute | solution.py:294
  45.7 9.8 %collective-permute-start.9 = (bf16[128,1024]{1,0:T(8,128)(2,1)S(1)}, bf16[128,1024]{1,0:T(8,128)(2,1)S(1)}, u32[]{:S(2)}, u32[]{:S(2)}) collective-permute-start(bf16[128,1024]{1,0:T(8,128)(2,1)S(1)} %get-tuple-element.33), channel_id=1, source_target_pairs={{0,8},{2,10},{4,12},{6,14},{8,0},{10,2},{12,4},{14,6},{16,24},{18,... | collective-permute-start | bytes 786440 | tf_op jit(solution)/shard_map/ppermute | solution.py:294
  54.2 8.9 %collective-permute-start.16 = (bf16[128,1024]{1,0:T(8,128)(2,1)S(1)}, bf16[128,1024]{1,0:T(8,128)(2,1)S(1)}, u32[]{:S(2)}, u32[]{:S(2)}) collective-permute-start(bf16[128,1024]{1,0:T(8,128)(2,1)S(1)} %get-tuple-element.31), channel_id=1, source_target_pairs={{0,16},{2,4},{4,2},{6,22},{8,24},{10,12},{12,10},{14,30},{16,0},{1... | collective-permute-start | bytes 786440 | tf_op jit(solution)/shard_map/ppermute | solution.py:294
  55.6 7.5 %collective-permute-start.15 = (bf16[128,1024]{1,0:T(8,128)(2,1)S(1)}, bf16[128,1024]{1,0:T(8,128)(2,1)S(1)}, u32[]{:S(2)}, u32[]{:S(2)}) collective-permute-start(bf16[128,1024]{1,0:T(8,128)(2,1)S(1)} %get-tuple-element.30), channel_id=1, source_target_pairs={{0,8},{2,10},{4,12},{6,14},{8,0},{10,2},{12,4},{14,6},{16,24},{18,... | collective-permute-start | bytes 786440 | tf_op jit(solution)/shard_map/ppermute | solution.py:294
  58.3 22.0 %collective-permute-start.18 = (bf16[128,1024]{1,0:T(8,128)(2,1)S(1)}, bf16[128,1024]{1,0:T(8,128)(2,1)S(1)}, u32[]{:S(2)}, u32[]{:S(2)}) collective-permute-start(bf16[128,1024]{1,0:T(8,128)(2,1)S(1)} %get-tuple-element.20), channel_id=1, source_target_pairs={{0,8},{2,10},{4,12},{6,14},{8,0},{10,2},{12,4},{14,6},{16,24},{18,... | collective-permute-start | bytes 786440 | tf_op jit(solution)/shard_map/ppermute | solution.py:294
  63.1 17.1 %collective-permute-start.17 = (bf16[128,1024]{1,0:T(8,128)(2,1)S(1)}, bf16[128,1024]{1,0:T(8,128)(2,1)S(1)}, u32[]{:S(2)}, u32[]{:S(2)}) collective-permute-start(bf16[128,1024]{1,0:T(8,128)(2,1)S(1)} %broadcast_select_fusion.1), channel_id=1, source_target_pairs={{0,2},{2,0},{4,6},{6,4},{8,10},{10,8},{12,14},{14,12},{16,18},{18,... | collective-permute-start | bytes 786440 | tf_op jit(solution)/shard_map/ppermute | solution.py:294
  63.2 20.5 %collective-permute-start.12 = (bf16[128,1024]{1,0:T(8,128)(2,1)S(1)}, bf16[128,1024]{1,0:T(8,128)(2,1)S(1)}, u32[]{:S(2)}, u32[]{:S(2)}) collective-permute-start(bf16[128,1024]{1,0:T(8,128)(2,1)S(1)} %get-tuple-element.21), channel_id=1, source_target_pairs={{0,16},{2,4},{4,2},{6,22},{8,24},{10,26},{12,28},{14,30},{16,0},{1... | collective-permute-start | bytes 786440 | tf_op jit(solution)/shard_map/ppermute | solution.py:294
  64.5 19.3 %collective-permute-start.14 = (bf16[128,1024]{1,0:T(8,128)(2,1)S(1)}, bf16[128,1024]{1,0:T(8,128)(2,1)S(1)}, u32[]{:S(2)}, u32[]{:S(2)}) collective-permute-start(bf16[128,1024]{1,0:T(8,128)(2,1)S(1)} %get-tuple-element.29), channel_id=1, source_target_pairs={{0,2},{2,0},{4,6},{6,4},{8,10},{10,8},{12,14},{14,12},{16,18},{18,... | collective-permute-start | bytes 786440 | tf_op jit(solution)/shard_map/ppermute | solution.py:294
  68.4 1.4 %copy-start.3 = (f32[16,256,128]{2,1,0:T(8,128)}, f32[16,256,128]{2,1,0:T(8,128)S(1)}, u32[]{:S(2)}) copy-start(f32[16,256,128]{2,1,0:T(8,128)S(1)} %get-tuple-element.14.refs_8_) | copy-start | bytes 6291460
  74.5 1.4 %copy-start.1 = (f32[16,256,128]{2,1,0:T(8,128)}, f32[16,256,128]{2,1,0:T(8,128)S(1)}, u32[]{:S(2)}) copy-start(f32[16,256,128]{2,1,0:T(8,128)S(1)} %more.3.refs_5_) | copy-start | bytes 6291460
  78.9 1.4 %copy-start = (f32[16,256,128]{2,1,0:T(8,128)}, f32[16,256,128]{2,1,0:T(8,128)S(1)}, u32[]{:S(2)}) copy-start(f32[16,256,128]{2,1,0:T(8,128)S(1)} %more.4.refs_4_) | copy-start | bytes 6291460
  80.2 3.5 %copy-start.5 = (s32[2]{0:T(128)S(1)}, s32[2]{0:T(128)}, u32[]{:S(2)}) copy-start(s32[2]{0:T(128)} %reach_ref.1) | copy-start | bytes 28
  85.1 1.8 %collective-permute-start.19 = (bf16[2,12,64,128]{3,2,1,0:T(8,128)(2,1)S(1)}, bf16[2,12,64,128]{3,2,1,0:T(8,128)(2,1)S(1)}, u32[]{:S(2)}, u32[]{:S(2)}) collective-permute-start(bf16[2,12,64,128]{3,2,1,0:T(8,128)(2,1)S(1)} %get-tuple-element.16), channel_id=1, source_target_pairs={{0,1},{1,0},{2,3},{3,2},{4,5},{5,4},{6,7},{7,6},{8,9},{9,8},{10,11... | collective-permute-start | bytes 1179656 | tf_op jit(solution)/shard_map/ppermute | solution.py:330

commit v2 on v1

v2 whole, which is shorter than its diff:
```python
import functools

import jax
import jax.numpy as jnp
import numpy as np
from jax import lax
from jax.experimental import pallas as pl
from jax.experimental.pallas import tpu as pltpu
from jax.sharding import PartitionSpec as P

OUT_BAND = 24
TILE = 128
SLOTS = 8
SUMS = 16
NO_TERM = 17
RC = ("row", "col")


STEPS = (
    (1, (
        (1, 1, 1), (3, 3, 1), (4, 4, 0), (5, 5, 1), (7, 7, 1), (8, 8, 1), (9, 9, 1),
        (10, 10, 1), (11, 11, 0), (12, 12, 0), (13, 13, 0), (14, 14, 0), (15, 15, 0),
    )),
    (0, (
        (2, 2, 1), (4, 4, 1), (5, 5, 0), (6, 6, 0), (7, 7, 0), (8, 8, 0), (9, 9, 0),
        (10, 10, 1), (11, 11, 1), (12, 12, 0), (13, 13, 0), (14, 14, 0), (15, 15, 0),
    )),
    (5, (
        (2, 2, 1), (5, 5, 1), (6, 6, 1), (8, 8, 1), (9, 9, 1), (10, 10, 0), (11, 11, 0),
        (12, 12, 0), (13, 13, 0), (14, 14, 0), (15, 15, 0),
    )),
    (1, (
        (1, 1, 0), (3, 3, 0), (4, 4, 1), (5, 5, 0), (6, 6, 1), (7, 7, 0), (8, 8, 0), (9, 9, 0),
        (11, 11, 1),
    )),
    (0, (
        (4, 5, 1), (5, 4, 0), (6, 7, 1), (7, 7, 1), (8, 9, 1), (9, 8, 1), (10, 10, 0),
        (11, 10, 1), (12, 13, 0), (13, 12, 0), (14, 15, 0), (15, 14, 0),
    )),
    (6, (
        (1, 5, 0), (2, 2, 0), (5, 4, 0), (6, 6, 0), (8, 9, 1), (9, 9, 0), (10, 11, 0),
        (11, 11, 1), (12, 8, 0), (13, 9, 0), (14, 10, 1), (15, 11, 1),
    )),
    (1, (
        (0, 8, 1), (1, 5, 0), (2, 6, 0), (3, 11, 0), (4, 12, 0), (5, 6, 1), (6, 5, 1),
        (13, 14, 0), (14, 13, 0),
    )),
    (0, (
        (0, 8, 1), (2, 10, 0), (3, 11, 0), (4, 4, 0), (5, 4, 1), (6, 7, 0), (7, 6, 1),
        (8, 9, 0),
    )),
    (6, (
        (1, 9, 1), (2, 7, 1), (6, 7, 0), (8, 8, 0), (9, 8, 0), (10, 2, 1), (11, 10, 1),
        (12, 13, 0), (13, 8, 1), (14, 10, 0), (15, 14, 0),
    )),
    (1, (
        (0, 5, 1), (1, 2, 0), (2, 5, 0), (4, 8, 0), (5, 6, 0), (6, 4, 0), (7, 11, 1),
        (9, 11, 0), (10, 9, 0), (13, 10, 1), (14, 9, 0),
    )),
    (0, (
        (0, 9, 1), (1, 8, 1), (2, 11, 0), (4, 6, 1), (5, 6, 0), (6, 4, 0), (7, 5, 1),
        (12, 14, 0),
    )),
    (6, (
        (1, 8, 1), (2, 3, 1), (5, 12, 0), (6, 10, 0), (8, 9, 0), (9, 12, 0), (10, 11, 1),
        (12, 9, 0), (14, 15, 0), (15, 13, 0),
    )),
    (1, (
        (0, 8, 0), (1, 7, 1), (2, 9, 1), (3, 10, 1), (4, 13, 0), (5, 7, 0), (6, 10, 0),
        (7, 14, 0), (9, 2, 1), (10, 8, 0), (13, 10, 0), (14, 8, 1),
    )),
    (0, (
        (1, 7, 1), (2, 9, 1), (3, 10, 1), (4, 6, 0), (5, 6, 1), (6, 6, 1), (7, 4, 0),
        (8, 11, 0), (9, 11, 0), (12, 10, 1), (13, 14, 0), (14, 13, 0),
    )),
    (6, (
        (1, 4, 1), (2, 3, 0), (5, 8, 0), (6, 11, 1), (10, 15, 0), (11, 9, 0), (12, 10, 1),
        (15, 9, 0),
    )),
    (1, (
        (0, 9, 0), (1, 3, 1), (2, 8, 1), (3, 5, 1), (4, 9, 0), (5, 10, 0), (6, 12, 0),
        (7, 13, 0), (9, 11, 1), (10, 12, 0),
    )),
    (0, (
        (0, 7, 1), (1, 9, 1), (2, 10, 1), (3, 9, 1), (4, 7, 0), (5, 7, 0), (7, 10, 0),
        (12, 10, 0), (13, 10, 1),
    )),
    (4, (
        (1, 8, 0), (2, 2, 1), (8, 2, 1), (10, 10, 0), (11, 8, 0), (12, 11, 0), (13, 11, 0),
        (14, 8, 1), (15, 8, 1),
    )),
    (1, (
        (1, 3, 0), (2, 4, 1), (3, 9, 0), (4, 10, 1), (5, 11, 1), (6, 8, 0), (7, 9, 0),
        (9, 15, 0), (10, 13, 0), (13, 15, 0),
    )),
)


def partner(kind, chip):
    z, row = chip % 4, chip // 4
    if kind < 3:
        return chip ^ (4, 1, 8)[kind]
    if z in (1, 2) and (kind - 3) >> (row % 2) & 1:
        return chip ^ 3
    return chip ^ 8


def grid_plan():
    ops = []
    for kind, sends in STEPS:
        sent = {source: (block, part) for source, block, part in sends}
        ops.append([(c, partner(kind, c), sent.get(c)) for c in range(16)])
    return ops, frozenset(range(12, 16))


def direct_plan(chips):
    ops = []
    for m in range(1, 9):
        for part in range(2 if m < 8 else 1):
            ops.append([(r + m, r, (r + m, part)) for r in range(chips - m)])
    return ops, frozenset()


def first_slot(k, core):
    return (k - core + ((core + k) & 1)) // 2


def terms(block, part, chip, packed, core):
    m = block - chip
    if packed:
        ks = [2 * m, 2 * m + 1] if part == 0 else [NO_TERM, NO_TERM]
        at = [first_slot(k, core) for k in ks]
    else:
        ks = [2 * m + part] * 2
        at = [first_slot(ks[0], core), first_slot(ks[0], core) + SLOTS // 2]
    out = []
    for k, slot in zip(ks, at):
        out += [k, slot] if m >= 0 and k < NO_TERM else [NO_TERM, 0]
    return out


VMEM = pl.BlockSpec(memory_space=pltpu.VMEM)
SMEM = pl.BlockSpec(memory_space=pltpu.SMEM)
HBM = pl.BlockSpec(memory_space=pltpu.HBM)
VMEM_LIMIT = 12 * 2**20
FIRST = 3
LAG = 5
LAST = 1


def units_kernel(packed_from, masks, fill_hbm, band_hbm, *refs):
    outs, (fill_ref, band_ref, sems) = refs[:-3], refs[-3:]
    fill_copy = pltpu.make_async_copy(fill_hbm, fill_ref, sems.at[0])
    band_copy = pltpu.make_async_copy(band_hbm, band_ref, sems.at[1])
    fill_copy.start()
    band_copy.start()
    core = lax.axis_index("depth")
    chip = lax.axis_index("row") * lax.axis_size("col") + lax.axis_index("col")
    packed = chip >= packed_from
    fill_copy.wait()
    band_copy.wait()
    parts = [0, 1] + [(mask >> chip) & 1 for mask in masks]
    for part, unit in zip(parts, outs):
        for slot in range(SLOTS):
            both = packed & (part == 0)
            row = jnp.where(both, slot // 4, part)
            entry = 2 * jnp.where(both, slot % 4, slot) + ((core + row) & 1)
            fill = fill_ref[row, entry].astype(jnp.float32)
            tile = band_ref[row, entry].astype(jnp.float32) * fill
            unit[:, slot * TILE : (slot + 1) * TILE] = tile.astype(jnp.bfloat16)


def add_terms(table_ref, base, left_ref, units, sums):
    width = SLOTS // 2 * TILE
    for i, unit in enumerate(units):
        for half in range(2):
            at = (base + i) * 4 + half * 2
            k, slot = table_ref[at], table_ref[at + 1]
            product = jnp.dot(
                left_ref[k],
                unit[:, half * width : (half + 1) * width],
                preferred_element_type=jnp.float32,
            )
            for q in range(SLOTS // 2):
                sums[slot + q] += product[:, q * TILE : (q + 1) * TILE]


def first_kernel(base, table_ref, fill_ref, band_ref, *refs):
    units, (left, sums) = refs[:-2], refs[-2:]
    zero = jnp.zeros((TILE, TILE), jnp.bfloat16)
    left[0, TILE:] = zero
    left[16, :TILE] = zero
    left[NO_TERM] = jnp.zeros((2 * TILE, TILE), jnp.bfloat16)
    for row in range(2):
        for entry in range(16):
            fill = fill_ref[row, entry].astype(jnp.float32)
            tile = band_ref[row, entry].astype(jnp.float32) * fill
            left[entry + row, row * TILE : (row + 1) * TILE] = tile.astype(jnp.bfloat16)
    sums[...] = jnp.zeros(sums.shape, jnp.float32)
    add_terms(table_ref, base, left, units, sums)


def step_kernel(base, picked, n_units, table_ref, left_ref, *refs):
    units, choices, outs = refs[:n_units], refs[n_units:-3 if picked is not None else -2], refs[-2:]
    sums = refs[-1]
    if picked is not None:
        out = refs[-2]
        index = table_ref[picked]
        for i, choice in enumerate(choices):

            @pl.when(index == i)
            def _(choice=choice):
                out[...] = choice[...]

    add_terms(table_ref, base, left_ref, units, sums)


def last_kernel(base, table_ref, reach_ref, left_ref, *refs):
    units, kept, given, sums = refs[:-4], refs[-3], refs[-2], refs[-1]
    add_terms(table_ref, base, left_ref, units, sums)
    core = lax.axis_index("depth")
    half = TILE // 2
    for row in range(2):
        odd = core if row == 0 else 1 - core
        shift = 0 if row == 0 else 1 - core
        for s in range(OUT_BAND // 2):
            keep = 2 * s + odd < reach_ref[row]
            for out, side in ((kept, core), (given, 1 - core)):
                start = pl.multiple_of(row * TILE + side * half, half)
                tile = sums[s + shift, pl.ds(start, half), :]
                out[row, s] = jnp.where(keep, tile, 0.0).astype(jnp.bfloat16)


def join_kernel(kept_ref, taken_ref, out_ref):
    core = lax.axis_index("depth")
    for row in range(2):
        odd = core if row == 0 else 1 - core
        for s in range(OUT_BAND // 2):
            out_ref[row, 2 * s + odd] = kept_ref[row, s]
            out_ref[row, 2 * s + 1 - odd] = taken_ref[row, s]


def lookup(plan, chips):
    ops, packed = plan
    held = {"n0": [(r, 0) for r in range(chips)], "n1": [(r, 1) for r in range(chips)]}
    order = ["n0", "n1"] + list(range(len(ops)))
    picks = np.zeros((chips, 2, len(ops)), np.int32)
    choices = []
    for o, moves in enumerate(ops):
        names = []
        got = [None] * chips
        for source, target, unit in moves:
            if unit is None:
                continue
            name = next(n for n in order if n in held and held[n][source] == unit)
            if name not in names:
                names.append(name)
            picks[source, :, o] = names.index(name)
            got[target] = unit
        held[o] = got
        choices.append(names)
    table = np.zeros((chips, 2, len(order), 4), np.int32)
    for r in range(chips):
        done = set()
        for i, n in enumerate(order):
            unit = held[n][r]
            fresh = unit is not None and unit not in done
            done.add(unit)
            for c in range(2):
                none = [NO_TERM, 0, NO_TERM, 0]
                table[r, c, i] = terms(*unit, r, unit[0] in packed, c) if fresh else none
    whole = np.concatenate([table.reshape(chips * 2, -1), picks.reshape(chips * 2, -1)], 1)
    return whole, table.shape[2] * 4, choices


def per_device(plan, chips, a_band, a_fill, c_reach):
    ops, packed = plan
    whole, picks_at, choices = lookup(plan, chips)
    device = lax.axis_index(RC + ("depth",))
    table = jnp.asarray(whole)[device]
    params = pltpu.CompilerParams(vmem_limit_bytes=VMEM_LIMIT)
    unit_shape = jax.ShapeDtypeStruct((TILE, SLOTS * TILE), jnp.bfloat16)
    sums_shape = jax.ShapeDtypeStruct((SUMS, 2 * TILE, TILE), jnp.float32)
    early = [o for o in range(len(ops)) if set(choices[o]) == {"n0", "n1"}]
    at = [choices[o].index("n1") for o in early]
    bits = whole[::2, picks_at:]
    masks = [sum(int(bits[r, o] == i) << r for r in range(chips)) for o, i in zip(early, at)]
    n0, n1, *sent = pl.pallas_call(
        functools.partial(units_kernel, min(packed, default=chips), masks),
        out_shape=(unit_shape,) * (2 + len(early)),
        in_specs=[HBM, HBM],
        out_specs=(VMEM,) * (2 + len(early)),
        scratch_shapes=[
            pltpu.SMEM(a_fill.shape, a_fill.dtype),
            pltpu.VMEM(a_band.shape, a_band.dtype),
            pltpu.SemaphoreType.DMA((2,)),
        ],
        compiler_params=params,
        name="units",
    )(a_fill, a_band)
    buffers = {"n0": n0, "n1": n1}
    left = sums = None
    added = 0

    def start():
        return pl.pallas_call(
            functools.partial(first_kernel, 0),
            out_shape=(
                jax.ShapeDtypeStruct((NO_TERM + 1, 2 * TILE, TILE), jnp.bfloat16),
                sums_shape,
            ),
            in_specs=[SMEM, SMEM, VMEM, VMEM, VMEM],
            out_specs=(VMEM, VMEM),
            compiler_params=params,
            name="first",
        )(table, a_fill, a_band, n0, n1)

    def step(sums, picked, sources, units, base):
        out_shape = ([unit_shape] if picked is not None else []) + [sums_shape]
        n_in = 2 + len(units) + len(sources)
        return pl.pallas_call(
            functools.partial(step_kernel, base, picked, len(units)),
            out_shape=out_shape,
            in_specs=[SMEM] + [VMEM] * n_in,
            out_specs=[VMEM] * len(out_shape),
            input_output_aliases={n_in: len(out_shape) - 1},
            compiler_params=params,
            name="step",
        )(table, left, *units, *sources, sums)

    for o, moves in enumerate(ops):
        sources = [buffers[n] for n in choices[o]]
        if o == FIRST:
            left, sums = start()
        ready = max(added, min(o - LAG, o))
        units = [buffers[n] for n in range(added, ready)]
        if o in early or len(sources) == 1:
            payload = sent[early.index(o)] if o in early else sources[0]
            if units and o >= FIRST:
                (sums,) = step(sums, None, [], units, 2 + added)
                added = ready
        else:
            payload, sums = step(sums, picks_at + o, sources, units, 2 + added)
            added = ready
        buffers[o] = lax.ppermute(payload, RC, [(s, t) for s, t, _ in moves])
    while added < len(ops) - LAST:
        (sums,) = step(sums, None, [], [buffers[added]], 2 + added)
        added += 1

    piece = jax.ShapeDtypeStruct((2, OUT_BAND // 2, TILE // 2, TILE), jnp.bfloat16)
    units = [buffers[n] for n in range(added, len(ops))]
    n_in = 3 + len(units)
    kept, given, _ = pl.pallas_call(
        functools.partial(last_kernel, 2 + added),
        out_shape=(piece, piece, sums_shape),
        in_specs=[SMEM, SMEM] + [VMEM] * (n_in - 1),
        out_specs=(VMEM, VMEM, VMEM),
        input_output_aliases={n_in: 2},
        compiler_params=params,
        name="last",
    )(table, c_reach, left, *units, sums)
    taken = lax.ppermute(given, "depth", [(0, 1), (1, 0)])
    return pl.pallas_call(
        join_kernel,
        out_shape=jax.ShapeDtypeStruct((2, OUT_BAND, TILE // 2, TILE), jnp.bfloat16),
        in_specs=[VMEM, VMEM],
        out_specs=VMEM,
        compiler_params=params,
        name="join",
    )(kept, taken)


def solution(mesh):
    rows, cols = mesh.shape["row"], mesh.shape["col"]
    plan = grid_plan() if (rows, cols) == (4, 4) else direct_plan(rows * cols)
    in_specs = (P(RC, None, None, None), P(RC, None), P(RC))
    out_specs = P(RC, None, "depth", None)
    return jax.shard_map(
        functools.partial(per_device, plan, rows * cols),
        mesh=mesh,
        in_specs=in_specs,
        out_specs=out_specs,
        check_vma=False,
    )
```

time: 88.4 us -> 56.3 us (0.64)
  between operations: 23.7 us -> 0.23 us
  waiting for transfers between devices: 13.1 us -> 5.17 us
  Pallas kernels: 15.8 us -> 20.4 us
  local copies, waits for them, and re-layouts: 8.72 us -> 4.5 us
    ppermute x19, waiting for transfers between devices: 11.4 us -> 3.46 us  [per_device(): buffers[o] = lax.ppermute(payload, RC, [(s, t) for s, t, _ in moves])]
    pallas_call x6 -> x23, Pallas kernels: 14.9 us -> 19.5 us  [the longest x20 16.3 us: step(): pl.pallas_call(functools.partial(step_kernel, base, picked, len(units)),...]
    unnamed x12 -> x10, local copies, waits for them, and re-layouts: 5.94 us -> 3.81 us
  transfers between devices with their start and end apart: 20 -> 20, of which waited for: 8 -> 5; matrix products, arithmetic and copies ran while one was open for 1% -> 1% of each run, Pallas kernels for 15% -> 31%
where the time goes in v2:
time: 56.3 us; the launch traced here: 56 us
  starting transfers between devices  25.7 us (46%)
  Pallas kernels  20.4 us (36%)
  waiting for transfers between devices  5.17 us (9%)
  local copies, waits for them, and re-layouts  4.5 us (8%)
    ppermute x19, starting transfers between devices, per_device(): buffers[o] = lax.ppermute(payload, RC, [(s, t) for s, t, _ in moves])  25.6 us
    pallas_call x20, Pallas kernels, step(): pl.pallas_call(functools.partial(step_kernel, base, picked, len(units)),...  16.3 us
    unnamed x10, local copies, waits for them, and re-layouts  3.81 us
    ppermute x19, waiting for transfers between devices, per_device(): buffers[o] = lax.ppermute(payload, RC, [(s, t) for s, t, _ in moves])  3.46 us
    ppermute x1, waiting for transfers between devices, per_device(): taken = lax.ppermute(given, 'depth', [(0, 1), (1, 0)])  1.71 us
    pallas_call x1, Pallas kernels, start(): pl.pallas_call(functools.partial(first_kernel, 0), out_shape=(jax.ShapeDt...  1.22 us
  transfers between devices with their start and end apart: 20, of which 5 were waited for; matrix products, arithmetic and copies ran while one was open for 1% of the time, Pallas kernels for 31%

profile of v2, /device:TPU:0, one launch (start us, length us, event | category | flops | bytes accessed | tf_op | source)
XLA Modules:
  0.0 56.0 jit_solution(3469454458365459374)
XLA Ops:
  0.0 1.2 %copy-done = bf16[2,16,128,128]{3,2,1,0:T(8,128)(2,1)S(1)} copy-done((bf16[2,16,128,128]{3,2,1,0:T(8,128)(2,1)S(1)}, bf16[2,16,128,128]{3,2,1,0:T(8,128)(2,1)}, u32[]{:S(2)}) %copy-start) | copy-done | bytes 1048600
  1.9 1.0 %units.1 = (bf16[128,1024]{1,0:T(8,128)(2,1)S(1)}, bf16[128,1024]{1,0:T(8,128)(2,1)S(1)}, bf16[128,1024]{1,0:T(8,128)(2,1)S(1)}, bf16[128,1024]{1,0:T(8,128)(2,1...) custom-call(s32[2,16]{1,0:T(2,128)S(1)} %copy-done.2, bf16[2,16,128,128]{3,2,1,0:T(8,128)(2,1)S(1)} %copy-done), custom_call_target="tpu_custom_call" | custom-call | tf_op jit(solution)/shard_map/units/pallas_call | solution.py:288
  2.9 3.1 %collective-permute-start = (bf16[128,1024]{1,0:T(8,128)(2,1)S(1)}, bf16[128,1024]{1,0:T(8,128)(2,1)S(1)}, u32[]{:S(2)}, u32[]{:S(2)}) collective-permute-start(bf16[128,1024]{1,0:T(8,128)(2,1)S(1)} %get-tuple-element.48), channel_id=1, source_target_pairs={{0,2},{2,0},{4,6},{6,4},{8,10},{10,8},{12,14},{14,12},{16,18},{18,... | collective-permute-start | bytes 786440 | tf_op jit(solution)/shard_map/ppermute | solution.py:345
  6.0 1.5 %collective-permute-start.2 = (bf16[128,1024]{1,0:T(8,128)(2,1)S(1)}, bf16[128,1024]{1,0:T(8,128)(2,1)S(1)}, u32[]{:S(2)}, u32[]{:S(2)}) collective-permute-start(bf16[128,1024]{1,0:T(8,128)(2,1)S(1)} %get-tuple-element.50), channel_id=1, source_target_pairs={{0,8},{2,10},{4,12},{6,14},{8,0},{10,2},{12,4},{14,6},{16,24},{18,... | collective-permute-start | bytes 786440 | tf_op jit(solution)/shard_map/ppermute | solution.py:345
  7.5 1.5 %collective-permute-start.1 = (bf16[128,1024]{1,0:T(8,128)(2,1)S(1)}, bf16[128,1024]{1,0:T(8,128)(2,1)S(1)}, u32[]{:S(2)}, u32[]{:S(2)}) collective-permute-start(bf16[128,1024]{1,0:T(8,128)(2,1)S(1)} %get-tuple-element.49), channel_id=1, source_target_pairs={{0,16},{2,18},{4,20},{6,22},{8,24},{10,12},{12,10},{14,30},{16,0},... | collective-permute-start | bytes 786440 | tf_op jit(solution)/shard_map/ppermute | solution.py:345
  10.1 1.2 %copy-done.1 = bf16[2,16,128,128]{3,2,1,0:T(8,128)(2,1)S(1)} copy-done((bf16[2,16,128,128]{3,2,1,0:T(8,128)(2,1)S(1)}, bf16[2,16,128,128]{3,2,1,0:T(8,128)(2,1)}, u32[]{:S(2)}) %copy-start.1) | copy-done | bytes 1048600
  12.0 1.2 %first.1 = (bf16[18,256,128]{2,1,0:T(8,128)(2,1)S(1)}, f32[16,256,128]{2,1,0:T(8,128)S(1)}) custom-call(s32[103]{0:T(128)S(1)} %dynamic-slice_bitcast_fusion.table_ref, s32[2,16]{1,0:T(2,128)S(1)} %copy-done.3, bf16[2,16,128,128]{3,2,1,0:T(8,128)(2,1)S(1)} %copy-done.1, bf16[128,1024]{1,0:T(8,128)(2,1)S(1)} %get-tuple-element.45.refs_0_.refs_2_.refs_1_.refs_4_.refs_3_, ...), custom_call_target="tpu_custom_call" | custom-call | tf_op jit(solution)/shard_map/first/pallas_call | solution.py:306
  13.9 1.9 %collective-permute-start.4 = (bf16[128,1024]{1,0:T(8,128)(2,1)S(1)}, bf16[128,1024]{1,0:T(8,128)(2,1)S(1)}, u32[]{:S(2)}, u32[]{:S(2)}) collective-permute-start(bf16[128,1024]{1,0:T(8,128)(2,1)S(1)} %get-tuple-element.55), channel_id=1, source_target_pairs={{0,8},{2,10},{4,12},{6,14},{8,0},{10,2},{12,4},{14,6},{16,24},{18,... | collective-permute-start | bytes 786440 | tf_op jit(solution)/shard_map/ppermute | solution.py:345
  16.3 1.6 %collective-permute-start.8 = (bf16[128,1024]{1,0:T(8,128)(2,1)S(1)}, bf16[128,1024]{1,0:T(8,128)(2,1)S(1)}, u32[]{:S(2)}, u32[]{:S(2)}) collective-permute-start(bf16[128,1024]{1,0:T(8,128)(2,1)S(1)} %get-tuple-element.61), channel_id=1, source_target_pairs={{0,16},{2,4},{4,2},{6,22},{8,24},{10,12},{12,10},{14,30},{16,0},{1... | collective-permute-start | bytes 786440 | tf_op jit(solution)/shard_map/ppermute | solution.py:345
  17.9 0.9 %step.22 = (bf16[128,1024]{1,0:T(8,128)(2,1)S(1)}, f32[16,256,128]{2,1,0:T(8,128)S(1)}) custom-call(s32[103]{0:T(128)S(1)} %dynamic-slice_bitcast_fusion.table_ref, bf16[18,256,128]{2,1,0:T(8,128)(2,1)S(1)} %get-tuple-element.47.left_ref, bf16[128,1024]{1,0:T(8,128)(2,1)S(1)} %collective-permute-done.refs_0_.refs_2_.refs_5_, ...), custom_call_target="tpu_custom_call", output_to_operand_aliasing={{1}: (5, {})} | custom-call | tf_op jit(solution)/shard_map/step/pallas_call | solution.py:321
  18.8 1.7 %collective-permute-start.3 = (bf16[128,1024]{1,0:T(8,128)(2,1)S(1)}, bf16[128,1024]{1,0:T(8,128)(2,1)S(1)}, u32[]{:S(2)}, u32[]{:S(2)}) collective-permute-start(bf16[128,1024]{1,0:T(8,128)(2,1)S(1)} %get-tuple-element.54), channel_id=1, source_target_pairs={{0,2},{2,0},{4,6},{6,4},{8,10},{10,8},{12,14},{14,12},{16,18},{18,... | collective-permute-start | bytes 786440 | tf_op jit(solution)/shard_map/ppermute | solution.py:345
  20.5 0.9 %step.23 = (bf16[128,1024]{1,0:T(8,128)(2,1)S(1)}, f32[16,256,128]{2,1,0:T(8,128)S(1)}) custom-call(s32[103]{0:T(128)S(1)} %dynamic-slice_bitcast_fusion.table_ref, bf16[18,256,128]{2,1,0:T(8,128)(2,1)S(1)} %get-tuple-element.47.left_ref, bf16[128,1024]{1,0:T(8,128)(2,1)S(1)} %collective-permute-done.2.refs_0_.refs_2_, ...), custom_call_target="tpu_custom_call", output_to_operand_aliasing={{1}: (6, {})} | custom-call | tf_op jit(solution)/shard_map/step/pallas_call | solution.py:321
  21.9 0.9 %step.24 = (bf16[128,1024]{1,0:T(8,128)(2,1)S(1)}, f32[16,256,128]{2,1,0:T(8,128)S(1)}) custom-call(s32[103]{0:T(128)S(1)} %dynamic-slice_bitcast_fusion.table_ref, bf16[18,256,128]{2,1,0:T(8,128)(2,1)S(1)} %get-tuple-element.47.left_ref, ...), custom_call_target="tpu_custom_call", output_to_operand_aliasing={{1}: (8, {})} | custom-call | tf_op jit(solution)/shard_map/step/pallas_call | solution.py:321
  22.8 1.6 %collective-permute-start.6 = (bf16[128,1024]{1,0:T(8,128)(2,1)S(1)}, bf16[128,1024]{1,0:T(8,128)(2,1)S(1)}, u32[]{:S(2)}, u32[]{:S(2)}) collective-permute-start(bf16[128,1024]{1,0:T(8,128)(2,1)S(1)} %get-tuple-element.59), channel_id=1, source_target_pairs={{0,16},{2,4},{4,2},{6,22},{8,24},{10,12},{12,10},{14,30},{16,0},{1... | collective-permute-start | bytes 786440 | tf_op jit(solution)/shard_map/ppermute | solution.py:345
  25.2 1.6 %collective-permute-start.10 = (bf16[128,1024]{1,0:T(8,128)(2,1)S(1)}, bf16[128,1024]{1,0:T(8,128)(2,1)S(1)}, u32[]{:S(2)}, u32[]{:S(2)}) collective-permute-start(bf16[128,1024]{1,0:T(8,128)(2,1)S(1)} %get-tuple-element.67), channel_id=1, source_target_pairs={{0,2},{2,0},{4,6},{6,4},{8,10},{10,8},{12,14},{14,12},{16,18},{18,... | collective-permute-start | bytes 786440 | tf_op jit(solution)/shard_map/ppermute | solution.py:345
  27.8 0.9 %step.27 = (bf16[128,1024]{1,0:T(8,128)(2,1)S(1)}, f32[16,256,128]{2,1,0:T(8,128)S(1)}) custom-call(s32[103]{0:T(128)S(1)} %dynamic-slice_bitcast_fusion.table_ref, bf16[18,256,128]{2,1,0:T(8,128)(2,1)S(1)} %get-tuple-element.47.left_ref, ...), custom_call_target="tpu_custom_call", output_to_operand_aliasing={{1}: (8, {})} | custom-call | tf_op jit(solution)/shard_map/step/pallas_call | solution.py:321
  28.6 1.6 %collective-permute-start.13 = (bf16[128,1024]{1,0:T(8,128)(2,1)S(1)}, bf16[128,1024]{1,0:T(8,128)(2,1)S(1)}, u32[]{:S(2)}, u32[]{:S(2)}) collective-permute-start(bf16[128,1024]{1,0:T(8,128)(2,1)S(1)} %get-tuple-element.72), channel_id=1, source_target_pairs={{0,16},{2,4},{4,2},{6,22},{8,24},{10,12},{12,10},{14,30},{16,0},{1... | collective-permute-start | bytes 786440 | tf_op jit(solution)/shard_map/ppermute | solution.py:345
  30.8 0.8 %step.28 = (bf16[128,1024]{1,0:T(8,128)(2,1)S(1)}, f32[16,256,128]{2,1,0:T(8,128)S(1)}) custom-call(s32[103]{0:T(128)S(1)} %dynamic-slice_bitcast_fusion.table_ref, bf16[18,256,128]{2,1,0:T(8,128)(2,1)S(1)} %get-tuple-element.47.left_ref, bf16[128,1024]{1,0:T(8,128)(2,1)S(1)} %collective-permute-done.3.refs_2_.refs_1_.refs_0_, ...), custom_call_target="tpu_custom_call", output_to_operand_aliasing={{1}: (5, {})} | custom-call | tf_op jit(solution)/shard_map/step/pallas_call | solution.py:321
  31.6 1.6 %collective-permute-start.9 = (bf16[128,1024]{1,0:T(8,128)(2,1)S(1)}, bf16[128,1024]{1,0:T(8,128)(2,1)S(1)}, u32[]{:S(2)}, u32[]{:S(2)}) collective-permute-start(bf16[128,1024]{1,0:T(8,128)(2,1)S(1)} %get-tuple-element.66), channel_id=1, source_target_pairs={{0,2},{2,0},{4,6},{6,4},{8,10},{10,8},{12,14},{14,12},{16,18},{18,... | collective-permute-start | bytes 786440 | tf_op jit(solution)/shard_map/ppermute | solution.py:345
  33.3 0.9 %step.29 = (bf16[128,1024]{1,0:T(8,128)(2,1)S(1)}, f32[16,256,128]{2,1,0:T(8,128)S(1)}) custom-call(s32[103]{0:T(128)S(1)} %dynamic-slice_bitcast_fusion.table_ref, bf16[18,256,128]{2,1,0:T(8,128)(2,1)S(1)} %get-tuple-element.47.left_ref, ...), custom_call_target="tpu_custom_call", output_to_operand_aliasing={{1}: (8, {})} | custom-call | tf_op jit(solution)/shard_map/step/pallas_call | solution.py:321
  34.1 1.5 %collective-permute-start.12 = (bf16[128,1024]{1,0:T(8,128)(2,1)S(1)}, bf16[128,1024]{1,0:T(8,128)(2,1)S(1)}, u32[]{:S(2)}, u32[]{:S(2)}) collective-permute-start(bf16[128,1024]{1,0:T(8,128)(2,1)S(1)} %get-tuple-element.71), channel_id=1, source_target_pairs={{0,8},{2,10},{4,12},{6,14},{8,0},{10,2},{12,4},{14,6},{16,24},{18,... | collective-permute-start | bytes 786440 | tf_op jit(solution)/shard_map/ppermute | solution.py:345
  35.7 0.9 %step.30 = (bf16[128,1024]{1,0:T(8,128)(2,1)S(1)}, f32[16,256,128]{2,1,0:T(8,128)S(1)}) custom-call(s32[103]{0:T(128)S(1)} %dynamic-slice_bitcast_fusion.table_ref, bf16[18,256,128]{2,1,0:T(8,128)(2,1)S(1)} %get-tuple-element.47.left_ref, ...), custom_call_target="tpu_custom_call", output_to_operand_aliasing={{1}: (7, {})} | custom-call | tf_op jit(solution)/shard_map/step/pallas_call | solution.py:321
  37.1 1.2 %collective-permute-done.14.refs_2_.refs_0_ = bf16[128,1024]{1,0:T(8,128)(2,1)S(1)} collective-permute-done((bf16[128,1024]{1,0:T(8,128)(2,1)S(1)}, bf16[128,1024]{1,0:T(8,128)(2,1)S(1)}, u32[]{:S(2)}, u32[]{:S(2)}) %collective-permute-start.14) | collective-permute-done | bytes 262176 | tf_op jit(solution)/shard_map/ppermute | solution.py:345
  39.2 1.0 %collective-permute-start.18 = (bf16[128,1024]{1,0:T(8,128)(2,1)S(1)}, bf16[128,1024]{1,0:T(8,128)(2,1)S(1)}, u32[]{:S(2)}, u32[]{:S(2)}) collective-permute-start(bf16[128,1024]{1,0:T(8,128)(2,1)S(1)} %get-tuple-element.81), channel_id=1, source_target_pairs={{0,2},{2,0},{4,6},{6,4},{8,10},{10,8},{12,14},{14,12},{16,18},{18,... | collective-permute-start | bytes 786440 | tf_op jit(solution)/shard_map/ppermute | solution.py:345
  40.2 0.9 %step.32 = (bf16[128,1024]{1,0:T(8,128)(2,1)S(1)}, f32[16,256,128]{2,1,0:T(8,128)S(1)}) custom-call(s32[103]{0:T(128)S(1)} %dynamic-slice_bitcast_fusion.table_ref, bf16[18,256,128]{2,1,0:T(8,128)(2,1)S(1)} %get-tuple-element.47.left_ref, bf16[128,1024]{1,0:T(8,128)(2,1)S(1)} %collective-permute-done.14.refs_2_.refs_0_, ...), custom_call_target="tpu_custom_call", output_to_operand_aliasing={{1}: (7, {})} | custom-call | tf_op jit(solution)/shard_map/step/pallas_call | solution.py:321
  41.1 0.9 %step.33 = (bf16[128,1024]{1,0:T(8,128)(2,1)S(1)}, f32[16,256,128]{2,1,0:T(8,128)S(1)}) custom-call(s32[103]{0:T(128)S(1)} %dynamic-slice_bitcast_fusion.table_ref, bf16[18,256,128]{2,1,0:T(8,128)(2,1)S(1)} %get-tuple-element.47.left_ref, bf16[128,1024]{1,0:T(8,128)(2,1)S(1)} %collective-permute-done.13.refs_1_.refs_0_.refs_3_, ...), custom_call_target="tpu_custom_call", output_to_operand_aliasing={{1}: (8, {})} | custom-call | tf_op jit(solution)/shard_map/step/pallas_call | solution.py:321
  42.0 1.6 %collective-permute-start.16 = (bf16[128,1024]{1,0:T(8,128)(2,1)S(1)}, bf16[128,1024]{1,0:T(8,128)(2,1)S(1)}, u32[]{:S(2)}, u32[]{:S(2)}) collective-permute-start(bf16[128,1024]{1,0:T(8,128)(2,1)S(1)} %get-tuple-element.79), channel_id=1, source_target_pairs={{0,16},{2,4},{4,2},{6,22},{8,24},{10,26},{12,28},{14,30},{16,0},{1... | collective-permute-start | bytes 786440 | tf_op jit(solution)/shard_map/ppermute | solution.py:345
  43.6 1.4 %collective-permute-start.17 = (bf16[128,1024]{1,0:T(8,128)(2,1)S(1)}, bf16[128,1024]{1,0:T(8,128)(2,1)S(1)}, u32[]{:S(2)}, u32[]{:S(2)}) collective-permute-start(bf16[128,1024]{1,0:T(8,128)(2,1)S(1)} %get-tuple-element.80), channel_id=1, source_target_pairs={{0,8},{2,10},{4,12},{6,14},{8,0},{10,2},{12,4},{14,6},{16,24},{18,... | collective-permute-start | bytes 786440 | tf_op jit(solution)/shard_map/ppermute | solution.py:345
  48.6 1.4 %collective-permute-done.17.refs_0_ = bf16[128,1024]{1,0:T(8,128)(2,1)S(1)} collective-permute-done((bf16[128,1024]{1,0:T(8,128)(2,1)S(1)}, bf16[128,1024]{1,0:T(8,128)(2,1)S(1)}, u32[]{:S(2)}, u32[]{:S(2)}) %collective-permute-start.17) | collective-permute-done | bytes 262176 | tf_op jit(solution)/shard_map/ppermute | solution.py:345
  52.3 1.0 %last.1 = (bf16[2,12,64,128]{3,2,1,0:T(8,128)(2,1)S(1)}, bf16[2,12,64,128]{3,2,1,0:T(8,128)(2,1)S(1)}, f32[16,256,128]{2,1,0:T(8,128)S(1)}) custom-call(s32[103]{0:T(128)S(1)} %dynamic-slice_bitcast_fusion.table_ref, s32[2]{0:T(128)S(1)} %copy-done.4, bf16[18,256,128]{2,1,0:T(8,128)(2,1)S(1)} %get-tuple-element.47.left_ref, ...), custom_call_target="tpu_custom_call", output_to_operand_aliasing={{2}: (4, {})} | custom-call | tf_op jit(solution)/shard_map/last/pallas_call | solution.py:353
  53.4 1.7 %collective-permute-done.19.taken_ref = bf16[2,12,64,128]{3,2,1,0:T(8,128)(2,1)S(1)} collective-permute-done((bf16[2,12,64,128]{3,2,1,0:T(8,128)(2,1)S(1)}, bf16[2,12,64,128]{3,2,1,0:T(8,128)(2,1)S(1)}, u32[]{:S(2)}, u32[]{:S(2)}) %collective-permute-start.19) | collective-permute-done | bytes 393248 | tf_op jit(solution)/shard_map/ppermute | solution.py:362
  55.1 0.9 %join.1 = bf16[2,24,64,128]{3,2,1,0:T(8,128)(2,1)} custom-call(bf16[2,12,64,128]{3,2,1,0:T(8,128)(2,1)S(1)} %get-tuple-element.83.kept_ref, bf16[2,12,64,128]{3,2,1,0:T(8,128)(2,1)S(1)} %collective-permute-done.19.taken_ref), custom_call_target="tpu_custom_call" | custom-call | tf_op jit(solution)/shard_map/join/pallas_call | solution.py:363
  (43 shorter events, 14.0 us)
Async XLA Ops:
  0.0 1.2 %copy-start = (bf16[2,16,128,128]{3,2,1,0:T(8,128)(2,1)S(1)}, bf16[2,16,128,128]{3,2,1,0:T(8,128)(2,1)}, u32[]{:S(2)}) copy-start(bf16[2,16,128,128]{3,2,1,0:T(8,128)(2,1)} %band_ref.1) | copy-start | bytes 3145732
  1.2 0.7 %copy-start.2 = (s32[2,16]{1,0:T(2,128)S(1)}, s32[2,16]{1,0:T(2,128)}, u32[]{:S(2)}) copy-start(s32[2,16]{1,0:T(2,128)} %fill_ref.1) | copy-start | bytes 388
  2.9 10.4 %collective-permute-start = (bf16[128,1024]{1,0:T(8,128)(2,1)S(1)}, bf16[128,1024]{1,0:T(8,128)(2,1)S(1)}, u32[]{:S(2)}, u32[]{:S(2)}) collective-permute-start(bf16[128,1024]{1,0:T(8,128)(2,1)S(1)} %get-tuple-element.48), channel_id=1, source_target_pairs={{0,2},{2,0},{4,6},{6,4},{8,10},{10,8},{12,14},{14,12},{16,18},{18,... | collective-permute-start | bytes 786440 | tf_op jit(solution)/shard_map/ppermute | solution.py:345
  6.0 9.8 %collective-permute-start.2 = (bf16[128,1024]{1,0:T(8,128)(2,1)S(1)}, bf16[128,1024]{1,0:T(8,128)(2,1)S(1)}, u32[]{:S(2)}, u32[]{:S(2)}) collective-permute-start(bf16[128,1024]{1,0:T(8,128)(2,1)S(1)} %get-tuple-element.50), channel_id=1, source_target_pairs={{0,8},{2,10},{4,12},{6,14},{8,0},{10,2},{12,4},{14,6},{16,24},{18,... | collective-permute-start | bytes 786440 | tf_op jit(solution)/shard_map/ppermute | solution.py:345
  7.5 10.4 %collective-permute-start.1 = (bf16[128,1024]{1,0:T(8,128)(2,1)S(1)}, bf16[128,1024]{1,0:T(8,128)(2,1)S(1)}, u32[]{:S(2)}, u32[]{:S(2)}) collective-permute-start(bf16[128,1024]{1,0:T(8,128)(2,1)S(1)} %get-tuple-element.49), channel_id=1, source_target_pairs={{0,16},{2,18},{4,20},{6,22},{8,24},{10,12},{12,10},{14,30},{16,0},... | collective-permute-start | bytes 786440 | tf_op jit(solution)/shard_map/ppermute | solution.py:345
  9.0 11.5 %collective-permute-start.5 = (bf16[128,1024]{1,0:T(8,128)(2,1)S(1)}, bf16[128,1024]{1,0:T(8,128)(2,1)S(1)}, u32[]{:S(2)}, u32[]{:S(2)}) collective-permute-start(bf16[128,1024]{1,0:T(8,128)(2,1)S(1)} %get-tuple-element.56), channel_id=1, source_target_pairs={{0,2},{2,0},{4,6},{6,4},{8,10},{10,8},{12,14},{14,12},{16,18},{18,... | collective-permute-start | bytes 786440 | tf_op jit(solution)/shard_map/ppermute | solution.py:345
  10.1 1.2 %copy-start.1 = (bf16[2,16,128,128]{3,2,1,0:T(8,128)(2,1)S(1)}, bf16[2,16,128,128]{3,2,1,0:T(8,128)(2,1)}, u32[]{:S(2)}) copy-start(bf16[2,16,128,128]{3,2,1,0:T(8,128)(2,1)} %band_ref.1) | copy-start | bytes 3145732
  11.4 0.7 %copy-start.3 = (s32[2,16]{1,0:T(2,128)S(1)}, s32[2,16]{1,0:T(2,128)}, u32[]{:S(2)}) copy-start(s32[2,16]{1,0:T(2,128)} %fill_ref.1) | copy-start | bytes 388
  13.9 8.1 %collective-permute-start.4 = (bf16[128,1024]{1,0:T(8,128)(2,1)S(1)}, bf16[128,1024]{1,0:T(8,128)(2,1)S(1)}, u32[]{:S(2)}, u32[]{:S(2)}) collective-permute-start(bf16[128,1024]{1,0:T(8,128)(2,1)S(1)} %get-tuple-element.55), channel_id=1, source_target_pairs={{0,8},{2,10},{4,12},{6,14},{8,0},{10,2},{12,4},{14,6},{16,24},{18,... | collective-permute-start | bytes 786440 | tf_op jit(solution)/shard_map/ppermute | solution.py:345
  16.3 8.1 %collective-permute-start.8 = (bf16[128,1024]{1,0:T(8,128)(2,1)S(1)}, bf16[128,1024]{1,0:T(8,128)(2,1)S(1)}, u32[]{:S(2)}, u32[]{:S(2)}) collective-permute-start(bf16[128,1024]{1,0:T(8,128)(2,1)S(1)} %get-tuple-element.61), channel_id=1, source_target_pairs={{0,16},{2,4},{4,2},{6,22},{8,24},{10,12},{12,10},{14,30},{16,0},{1... | collective-permute-start | bytes 786440 | tf_op jit(solution)/shard_map/ppermute | solution.py:345
  18.8 8.1 %collective-permute-start.3 = (bf16[128,1024]{1,0:T(8,128)(2,1)S(1)}, bf16[128,1024]{1,0:T(8,128)(2,1)S(1)}, u32[]{:S(2)}, u32[]{:S(2)}) collective-permute-start(bf16[128,1024]{1,0:T(8,128)(2,1)S(1)} %get-tuple-element.54), channel_id=1, source_target_pairs={{0,2},{2,0},{4,6},{6,4},{8,10},{10,8},{12,14},{14,12},{16,18},{18,... | collective-permute-start | bytes 786440 | tf_op jit(solution)/shard_map/ppermute | solution.py:345
  21.3 6.4 %collective-permute-start.7 = (bf16[128,1024]{1,0:T(8,128)(2,1)S(1)}, bf16[128,1024]{1,0:T(8,128)(2,1)S(1)}, u32[]{:S(2)}, u32[]{:S(2)}) collective-permute-start(bf16[128,1024]{1,0:T(8,128)(2,1)S(1)} %get-tuple-element.60), channel_id=1, source_target_pairs={{0,8},{2,10},{4,12},{6,14},{8,0},{10,2},{12,4},{14,6},{16,24},{18,... | collective-permute-start | bytes 786440 | tf_op jit(solution)/shard_map/ppermute | solution.py:345
  22.8 8.0 %collective-permute-start.6 = (bf16[128,1024]{1,0:T(8,128)(2,1)S(1)}, bf16[128,1024]{1,0:T(8,128)(2,1)S(1)}, u32[]{:S(2)}, u32[]{:S(2)}) collective-permute-start(bf16[128,1024]{1,0:T(8,128)(2,1)S(1)} %get-tuple-element.59), channel_id=1, source_target_pairs={{0,16},{2,4},{4,2},{6,22},{8,24},{10,12},{12,10},{14,30},{16,0},{1... | collective-permute-start | bytes 786440 | tf_op jit(solution)/shard_map/ppermute | solution.py:345
  25.2 8.0 %collective-permute-start.10 = (bf16[128,1024]{1,0:T(8,128)(2,1)S(1)}, bf16[128,1024]{1,0:T(8,128)(2,1)S(1)}, u32[]{:S(2)}, u32[]{:S(2)}) collective-permute-start(bf16[128,1024]{1,0:T(8,128)(2,1)S(1)} %get-tuple-element.67), channel_id=1, source_target_pairs={{0,2},{2,0},{4,6},{6,4},{8,10},{10,8},{12,14},{14,12},{16,18},{18,... | collective-permute-start | bytes 786440 | tf_op jit(solution)/shard_map/ppermute | solution.py:345
  28.6 8.5 %collective-permute-start.13 = (bf16[128,1024]{1,0:T(8,128)(2,1)S(1)}, bf16[128,1024]{1,0:T(8,128)(2,1)S(1)}, u32[]{:S(2)}, u32[]{:S(2)}) collective-permute-start(bf16[128,1024]{1,0:T(8,128)(2,1)S(1)} %get-tuple-element.72), channel_id=1, source_target_pairs={{0,16},{2,4},{4,2},{6,22},{8,24},{10,12},{12,10},{14,30},{16,0},{1... | collective-permute-start | bytes 786440 | tf_op jit(solution)/shard_map/ppermute | solution.py:345
  30.2 8.1 %collective-permute-start.14 = (bf16[128,1024]{1,0:T(8,128)(2,1)S(1)}, bf16[128,1024]{1,0:T(8,128)(2,1)S(1)}, u32[]{:S(2)}, u32[]{:S(2)}) collective-permute-start(bf16[128,1024]{1,0:T(8,128)(2,1)S(1)} %get-tuple-element.73), channel_id=1, source_target_pairs={{0,8},{2,10},{4,12},{6,14},{8,0},{10,2},{12,4},{14,6},{16,24},{18,... | collective-permute-start | bytes 786440 | tf_op jit(solution)/shard_map/ppermute | solution.py:345
  31.6 8.6 %collective-permute-start.9 = (bf16[128,1024]{1,0:T(8,128)(2,1)S(1)}, bf16[128,1024]{1,0:T(8,128)(2,1)S(1)}, u32[]{:S(2)}, u32[]{:S(2)}) collective-permute-start(bf16[128,1024]{1,0:T(8,128)(2,1)S(1)} %get-tuple-element.66), channel_id=1, source_target_pairs={{0,2},{2,0},{4,6},{6,4},{8,10},{10,8},{12,14},{14,12},{16,18},{18,... | collective-permute-start | bytes 786440 | tf_op jit(solution)/shard_map/ppermute | solution.py:345
  34.1 7.0 %collective-permute-start.12 = (bf16[128,1024]{1,0:T(8,128)(2,1)S(1)}, bf16[128,1024]{1,0:T(8,128)(2,1)S(1)}, u32[]{:S(2)}, u32[]{:S(2)}) collective-permute-start(bf16[128,1024]{1,0:T(8,128)(2,1)S(1)} %get-tuple-element.71), channel_id=1, source_target_pairs={{0,8},{2,10},{4,12},{6,14},{8,0},{10,2},{12,4},{14,6},{16,24},{18,... | collective-permute-start | bytes 786440 | tf_op jit(solution)/shard_map/ppermute | solution.py:345
  36.5 8.5 %collective-permute-start.11 = (bf16[128,1024]{1,0:T(8,128)(2,1)S(1)}, bf16[128,1024]{1,0:T(8,128)(2,1)S(1)}, u32[]{:S(2)}, u32[]{:S(2)}) collective-permute-start(bf16[128,1024]{1,0:T(8,128)(2,1)S(1)} %get-tuple-element.70), channel_id=1, source_target_pairs={{0,16},{2,4},{4,2},{6,22},{8,24},{10,12},{12,10},{14,30},{16,0},{1... | collective-permute-start | bytes 786440 | tf_op jit(solution)/shard_map/ppermute | solution.py:345
  39.2 8.5 %collective-permute-start.18 = (bf16[128,1024]{1,0:T(8,128)(2,1)S(1)}, bf16[128,1024]{1,0:T(8,128)(2,1)S(1)}, u32[]{:S(2)}, u32[]{:S(2)}) collective-permute-start(bf16[128,1024]{1,0:T(8,128)(2,1)S(1)} %get-tuple-element.81), channel_id=1, source_target_pairs={{0,2},{2,0},{4,6},{6,4},{8,10},{10,8},{12,14},{14,12},{16,18},{18,... | collective-permute-start | bytes 786440 | tf_op jit(solution)/shard_map/ppermute | solution.py:345
  42.0 8.8 %collective-permute-start.16 = (bf16[128,1024]{1,0:T(8,128)(2,1)S(1)}, bf16[128,1024]{1,0:T(8,128)(2,1)S(1)}, u32[]{:S(2)}, u32[]{:S(2)}) collective-permute-start(bf16[128,1024]{1,0:T(8,128)(2,1)S(1)} %get-tuple-element.79), channel_id=1, source_target_pairs={{0,16},{2,4},{4,2},{6,22},{8,24},{10,26},{12,28},{14,30},{16,0},{1... | collective-permute-start | bytes 786440 | tf_op jit(solution)/shard_map/ppermute | solution.py:345
  43.6 6.4 %collective-permute-start.17 = (bf16[128,1024]{1,0:T(8,128)(2,1)S(1)}, bf16[128,1024]{1,0:T(8,128)(2,1)S(1)}, u32[]{:S(2)}, u32[]{:S(2)}) collective-permute-start(bf16[128,1024]{1,0:T(8,128)(2,1)S(1)} %get-tuple-element.80), channel_id=1, source_target_pairs={{0,8},{2,10},{4,12},{6,14},{8,0},{10,2},{12,4},{14,6},{16,24},{18,... | collective-permute-start | bytes 786440 | tf_op jit(solution)/shard_map/ppermute | solution.py:345
  45.9 6.4 %collective-permute-start.15 = (bf16[128,1024]{1,0:T(8,128)(2,1)S(1)}, bf16[128,1024]{1,0:T(8,128)(2,1)S(1)}, u32[]{:S(2)}, u32[]{:S(2)}) collective-permute-start(bf16[128,1024]{1,0:T(8,128)(2,1)S(1)} %get-tuple-element.78), channel_id=1, source_target_pairs={{0,2},{2,0},{4,6},{6,4},{8,10},{10,8},{12,14},{14,12},{16,18},{18,... | collective-permute-start | bytes 786440 | tf_op jit(solution)/shard_map/ppermute | solution.py:345
  50.8 1.5 %copy-start.4 = (s32[2]{0:T(128)S(1)}, s32[2]{0:T(128)}, u32[]{:S(2)}) copy-start(s32[2]{0:T(128)} %reach_ref.1) | copy-start | bytes 28
  53.3 1.8 %collective-permute-start.19 = (bf16[2,12,64,128]{3,2,1,0:T(8,128)(2,1)S(1)}, bf16[2,12,64,128]{3,2,1,0:T(8,128)(2,1)S(1)}, u32[]{:S(2)}, u32[]{:S(2)}) collective-permute-start(bf16[2,12,64,128]{3,2,1,0:T(8,128)(2,1)S(1)} %get-tuple-element.84), channel_id=1, source_target_pairs={{0,1},{1,0},{2,3},{3,2},{4,5},{5,4},{6,7},{7,6},{8,9},{9,8},{10,11... | collective-permute-start | bytes 1179656 | tf_op jit(solution)/shard_map/ppermute | solution.py:362

commit v3 on v2

--- a/solution.py
+++ b/solution.py
@@ -143,13 +143,14 @@
 SMEM = pl.BlockSpec(memory_space=pltpu.SMEM)
 HBM = pl.BlockSpec(memory_space=pltpu.HBM)
 VMEM_LIMIT = 12 * 2**20
-FIRST = 3
-LAG = 5
-LAST = 1
-
-
-def units_kernel(packed_from, masks, fill_hbm, band_hbm, *refs):
-    outs, (fill_ref, band_ref, sems) = refs[:-3], refs[-3:]
+FIRST = 4
+LAG = 4
+ADD_AT = (8, 11, 14, 17)
+LAST = (3, 1)
+
+
+def units_kernel(packed_from, masks, choice_masks, fill_hbm, band_hbm, *refs):
+    outs, flags, (fill_ref, band_ref, sems) = refs[:-4], refs[-4], refs[-3:]
     fill_copy = pltpu.make_async_copy(fill_hbm, fill_ref, sems.at[0])
     band_copy = pltpu.make_async_copy(band_hbm, band_ref, sems.at[1])
     fill_copy.start()
@@ -168,6 +169,9 @@
             fill = fill_ref[row, entry].astype(jnp.float32)
             tile = band_ref[row, entry].astype(jnp.float32) * fill
             unit[:, slot * TILE : (slot + 1) * TILE] = tile.astype(jnp.bfloat16)
+    for i, mask in enumerate(choice_masks):
+        bit = ((mask >> chip) & 1).astype(jnp.float32)
+        flags[i : i + 1, :] = jnp.full((1, flags.shape[1]), bit, flags.dtype)
 
 
 def add_terms(table_ref, base, left_ref, units, sums):
@@ -186,7 +190,8 @@
 
 
 def first_kernel(base, table_ref, fill_ref, band_ref, *refs):
-    units, (left, sums) = refs[:-2], refs[-2:]
+    units, (left, token, sums) = refs[:-3], refs[-3:]
+    token[...] = jnp.zeros(token.shape, token.dtype)
     zero = jnp.zeros((TILE, TILE), jnp.bfloat16)
     left[0, TILE:] = zero
     left[16, :TILE] = zero
@@ -200,18 +205,9 @@
     add_terms(table_ref, base, left, units, sums)
 
 
-def step_kernel(base, picked, n_units, table_ref, left_ref, *refs):
-    units, choices, outs = refs[:n_units], refs[n_units:-3 if picked is not None else -2], refs[-2:]
-    sums = refs[-1]
-    if picked is not None:
-        out = refs[-2]
-        index = table_ref[picked]
-        for i, choice in enumerate(choices):
-
-            @pl.when(index == i)
-            def _(choice=choice):
-                out[...] = choice[...]
-
+def more_kernel(base, table_ref, left_ref, after_ref, *refs):
+    units, (token, sums) = refs[:-3], refs[-2:]
+    token[...] = jnp.zeros(token.shape, token.dtype)
     add_terms(table_ref, base, left_ref, units, sums)
 
 
@@ -244,7 +240,7 @@
     ops, packed = plan
     held = {"n0": [(r, 0) for r in range(chips)], "n1": [(r, 1) for r in range(chips)]}
     order = ["n0", "n1"] + list(range(len(ops)))
-    picks = np.zeros((chips, 2, len(ops)), np.int32)
+    picks = np.zeros((chips, len(ops)), np.int32)
     choices = []
     for o, moves in enumerate(ops):
         names = []
@@ -255,7 +251,7 @@
             name = next(n for n in order if n in held and held[n][source] == unit)
             if name not in names:
                 names.append(name)
-            picks[source, :, o] = names.index(name)
+            picks[source, o] = names.index(name)
             got[target] = unit
         held[o] = got
         choices.append(names)
@@ -269,27 +265,32 @@
             for c in range(2):
                 none = [NO_TERM, 0, NO_TERM, 0]
                 table[r, c, i] = terms(*unit, r, unit[0] in packed, c) if fresh else none
-    whole = np.concatenate([table.reshape(chips * 2, -1), picks.reshape(chips * 2, -1)], 1)
-    return whole, table.shape[2] * 4, choices
+    return table.reshape(chips * 2, -1), picks, choices
 
 
 def per_device(plan, chips, a_band, a_fill, c_reach):
     ops, packed = plan
-    whole, picks_at, choices = lookup(plan, chips)
-    device = lax.axis_index(RC + ("depth",))
-    table = jnp.asarray(whole)[device]
+    table, picks, choices = lookup(plan, chips)
+    table = jnp.asarray(table)[lax.axis_index(RC + ("depth",))]
     params = pltpu.CompilerParams(vmem_limit_bytes=VMEM_LIMIT)
     unit_shape = jax.ShapeDtypeStruct((TILE, SLOTS * TILE), jnp.bfloat16)
+    token_shape = jax.ShapeDtypeStruct((1, SLOTS * TILE), jnp.float32)
     sums_shape = jax.ShapeDtypeStruct((SUMS, 2 * TILE, TILE), jnp.float32)
     early = [o for o in range(len(ops)) if set(choices[o]) == {"n0", "n1"}]
     at = [choices[o].index("n1") for o in early]
-    bits = whole[::2, picks_at:]
-    masks = [sum(int(bits[r, o] == i) << r for r in range(chips)) for o, i in zip(early, at)]
-    n0, n1, *sent = pl.pallas_call(
-        functools.partial(units_kernel, min(packed, default=chips), masks),
-        out_shape=(unit_shape,) * (2 + len(early)),
+    masks = [sum(int(picks[r, o] == i) << r for r in range(chips)) for o, i in zip(early, at)]
+    choice_masks, flag_at = [], {}
+    for o, names in enumerate(choices):
+        if o not in early:
+            flag_at[o] = len(choice_masks)
+            for i in range(len(names) - 1):
+                choice_masks.append(sum(int(picks[r, o] == i) << r for r in range(chips)))
+    flags_shape = jax.ShapeDtypeStruct((max(8, len(choice_masks)), SLOTS * TILE), jnp.float32)
+    *sent, flags = pl.pallas_call(
+        functools.partial(units_kernel, min(packed, default=chips), masks, choice_masks),
+        out_shape=(unit_shape,) * (2 + len(early)) + (flags_shape,),
         in_specs=[HBM, HBM],
-        out_specs=(VMEM,) * (2 + len(early)),
+        out_specs=(VMEM,) * (3 + len(early)),
         scratch_shapes=[
             pltpu.SMEM(a_fill.shape, a_fill.dtype),
             pltpu.VMEM(a_band.shape, a_band.dtype),
@@ -298,8 +299,9 @@
         compiler_params=params,
         name="units",
     )(a_fill, a_band)
+    n0, n1, *sent = sent
     buffers = {"n0": n0, "n1": n1}
-    left = sums = None
+    payload = left = sums = None
     added = 0
 
     def start():
@@ -307,45 +309,51 @@
             functools.partial(first_kernel, 0),
             out_shape=(
                 jax.ShapeDtypeStruct((NO_TERM + 1, 2 * TILE, TILE), jnp.bfloat16),
+                token_shape,
                 sums_shape,
             ),
             in_specs=[SMEM, SMEM, VMEM, VMEM, VMEM],
-            out_specs=(VMEM, VMEM),
+            out_specs=(VMEM, VMEM, VMEM),
             compiler_params=params,
             name="first",
         )(table, a_fill, a_band, n0, n1)
 
-    def step(sums, picked, sources, units, base):
-        out_shape = ([unit_shape] if picked is not None else []) + [sums_shape]
-        n_in = 2 + len(units) + len(sources)
+    def more(after, sums, units, base):
         return pl.pallas_call(
-            functools.partial(step_kernel, base, picked, len(units)),
-            out_shape=out_shape,
-            in_specs=[SMEM] + [VMEM] * n_in,
-            out_specs=[VMEM] * len(out_shape),
-            input_output_aliases={n_in: len(out_shape) - 1},
+            functools.partial(more_kernel, base),
+            out_shape=(token_shape, sums_shape),
+            in_specs=[SMEM] + [VMEM] * (3 + len(units)),
+            out_specs=(VMEM, VMEM),
+            input_output_aliases={3 + len(units): 1},
             compiler_params=params,
-            name="step",
-        )(table, left, *units, *sources, sums)
+            name="more",
+        )(table, left, after, *units, sums)
 
     for o, moves in enumerate(ops):
         sources = [buffers[n] for n in choices[o]]
-        if o == FIRST:
-            left, sums = start()
-        ready = max(added, min(o - LAG, o))
-        units = [buffers[n] for n in range(added, ready)]
-        if o in early or len(sources) == 1:
-            payload = sent[early.index(o)] if o in early else sources[0]
-            if units and o >= FIRST:
-                (sums,) = step(sums, None, [], units, 2 + added)
-                added = ready
+        if o in early:
+            payload = sent[early.index(o)]
         else:
-            payload, sums = step(sums, picks_at + o, sources, units, 2 + added)
-            added = ready
+            order = 0 * payload[:1].astype(jnp.float32) if o > 0 else 0
+            if o == FIRST:
+                left, token, sums = start()
+                order += token
+            elif o in ADD_AT:
+                units = [buffers[n] for n in range(added, o - LAG)]
+                token, sums = more(payload, sums, units, 2 + added)
+                added = o - LAG
+                order += token
+            payload = sources[-1]
+            for i in reversed(range(len(sources) - 1)):
+                at = flag_at[o] + i
+                payload = jnp.where(flags[at : at + 1] + order > 0.5, sources[i], payload)
         buffers[o] = lax.ppermute(payload, RC, [(s, t) for s, t, _ in moves])
-    while added < len(ops) - LAST:
-        (sums,) = step(sums, None, [], [buffers[added]], 2 + added)
-        added += 1
+    if sums is None:
+        left, _, sums = start()
+    for count in LAST:
+        units = [buffers[n] for n in range(added, len(ops) - count)]
+        _, sums = more(units[0], sums, units, 2 + added)
+        added += len(units)
 
     piece = jax.ShapeDtypeStruct((2, OUT_BAND // 2, TILE // 2, TILE), jnp.bfloat16)
     units = [buffers[n] for n in range(added, len(ops))]

time: 56.3 us -> 53.2 us (0.945)
  Pallas kernels: 20.4 us -> 11.8 us
  starting transfers between devices: 25.7 us -> 28.1 us
  other arithmetic: 0 us -> 1.63 us
  waiting for transfers between devices: 5.17 us -> 6.66 us
    pallas_call x20 -> x6, Pallas kernels: 16.3 us -> 7.65 us  [more(): pl.pallas_call(functools.partial(more_kernel, base), out_shape=(token_sha...]
    ppermute x19, starting transfers between devices: 25.6 us -> 28 us  [per_device(): buffers[o] = lax.ppermute(payload, RC, [(s, t) for s, t, _ in moves])]
    ppermute x19, waiting for transfers between devices: 3.46 us -> 4.95 us  [per_device(): buffers[o] = lax.ppermute(payload, RC, [(s, t) for s, t, _ in moves])]
    select_n x0 -> x15, other arithmetic: none -> 0.87 us  [per_device(): payload = jnp.where(flags[at:at + 1] + order > 0.5, sources[i], payload)]
    gt x0 -> x15, other arithmetic: none -> 0.76 us  [per_device(): payload = jnp.where(flags[at:at + 1] + order > 0.5, sources[i], payload)]
  transfers between devices with their start and end apart: 20 -> 20, of which waited for: 5 -> 7; matrix products, arithmetic and copies ran while one was open for 1% -> 4% of each run, Pallas kernels for 31% -> 17%
where the time goes in v3:
time: 53.2 us; the launch traced here: 52.9 us
  starting transfers between devices  28.1 us (53%)
  Pallas kernels  11.8 us (22%)
  waiting for transfers between devices  6.66 us (13%)
  local copies, waits for them, and re-layouts  4.5 us (8%)
  other arithmetic  1.63 us (3%)
    ppermute x19, starting transfers between devices, per_device(): buffers[o] = lax.ppermute(payload, RC, [(s, t) for s, t, _ in moves])  28 us
    pallas_call x6, Pallas kernels, more(): pl.pallas_call(functools.partial(more_kernel, base), out_shape=(token_sha...  7.65 us
    ppermute x19, waiting for transfers between devices, per_device(): buffers[o] = lax.ppermute(payload, RC, [(s, t) for s, t, _ in moves])  4.95 us
    unnamed x10, local copies, waits for them, and re-layouts  3.81 us
    ppermute x1, waiting for transfers between devices, per_device(): taken = lax.ppermute(given, 'depth', [(0, 1), (1, 0)])  1.71 us
    pallas_call x1, Pallas kernels, start(): pl.pallas_call(functools.partial(first_kernel, 0), out_shape=(jax.ShapeDt...  1.23 us
  transfers between devices with their start and end apart: 20, of which 7 were waited for; matrix products, arithmetic and copies ran while one was open for 4% of the time, Pallas kernels for 17%

profile of v3, /device:TPU:0, one launch (start us, length us, event | category | flops | bytes accessed | tf_op | source)
XLA Modules:
  0.0 52.9 jit_solution(15437137033203039508)
XLA Ops:
  0.0 1.2 %copy-done = bf16[2,16,128,128]{3,2,1,0:T(8,128)(2,1)S(1)} copy-done((bf16[2,16,128,128]{3,2,1,0:T(8,128)(2,1)S(1)}, bf16[2,16,128,128]{3,2,1,0:T(8,128)(2,1)}, u32[]{:S(2)}) %copy-start) | copy-done | bytes 1048600
  1.9 1.0 %units.1 = (bf16[128,1024]{1,0:T(8,128)(2,1)S(1)}, bf16[128,1024]{1,0:T(8,128)(2,1)S(1)}, bf16[128,1024]{1,0:T(8,128)(2,1)S(1)}, bf16[128,1024]{1,0:T(8,128)(2,1...) custom-call(s32[2,16]{1,0:T(2,128)S(1)} %copy-done.2, ...), custom_call_target="tpu_custom_call" | custom-call | tf_op jit(solution)/shard_map/units/pallas_call | solution.py:289
  2.9 3.1 %collective-permute-start = (bf16[128,1024]{1,0:T(8,128)(2,1)S(1)}, bf16[128,1024]{1,0:T(8,128)(2,1)S(1)}, u32[]{:S(2)}, u32[]{:S(2)}) collective-permute-start(bf16[128,1024]{1,0:T(8,128)(2,1)S(1)} %get-tuple-element.33), channel_id=1, source_target_pairs={{0,2},{2,0},{4,6},{6,4},{8,10},{10,8},{12,14},{14,12},{16,18},{18,... | collective-permute-start | bytes 786440 | tf_op jit(solution)/shard_map/ppermute | solution.py:350
  6.0 1.5 %collective-permute-start.1 = (bf16[128,1024]{1,0:T(8,128)(2,1)S(1)}, bf16[128,1024]{1,0:T(8,128)(2,1)S(1)}, u32[]{:S(2)}, u32[]{:S(2)}) collective-permute-start(bf16[128,1024]{1,0:T(8,128)(2,1)S(1)} %get-tuple-element.34), channel_id=1, source_target_pairs={{0,8},{2,10},{4,12},{6,14},{8,0},{10,2},{12,4},{14,6},{16,24},{18,... | collective-permute-start | bytes 786440 | tf_op jit(solution)/shard_map/ppermute | solution.py:350
  7.5 1.5 %collective-permute-start.2 = (bf16[128,1024]{1,0:T(8,128)(2,1)S(1)}, bf16[128,1024]{1,0:T(8,128)(2,1)S(1)}, u32[]{:S(2)}, u32[]{:S(2)}) collective-permute-start(bf16[128,1024]{1,0:T(8,128)(2,1)S(1)} %get-tuple-element.35), channel_id=1, source_target_pairs={{0,16},{2,18},{4,20},{6,22},{8,24},{10,12},{12,10},{14,30},{16,0},... | collective-permute-start | bytes 786440 | tf_op jit(solution)/shard_map/ppermute | solution.py:350
  10.2 1.2 %copy-done.1 = bf16[2,16,128,128]{3,2,1,0:T(8,128)(2,1)S(1)} copy-done((bf16[2,16,128,128]{3,2,1,0:T(8,128)(2,1)S(1)}, bf16[2,16,128,128]{3,2,1,0:T(8,128)(2,1)}, u32[]{:S(2)}) %copy-start.1) | copy-done | bytes 1048600
  12.1 1.2 %first.1 = (bf16[18,256,128]{2,1,0:T(8,128)(2,1)S(1)}, f32[1,1024]{1,0:T(1,128)S(1)}, f32[16,256,128]{2,1,0:T(8,128)S(1)}) custom-call(s32[84]{0:T(128)S(1)} %dynamic-slice_bitcast_fusion.table_ref, s32[2,16]{1,0:T(2,128)S(1)} %copy-done.3, bf16[2,16,128,128]{3,2,1,0:T(8,128)(2,1)S(1)} %copy-done.1, bf16[128,1024]{1,0:T(8,128)(2,1)S(1)} %get-tuple-element.27.refs_0_, ...), custom_call_target="tpu_custom_call" | custom-call | tf_op jit(solution)/shard_map/first/pallas_call | solution.py:308
  13.4 1.8 %collective-permute-start.4 = (bf16[128,1024]{1,0:T(8,128)(2,1)S(1)}, bf16[128,1024]{1,0:T(8,128)(2,1)S(1)}, u32[]{:S(2)}, u32[]{:S(2)}) collective-permute-start(bf16[128,1024]{1,0:T(8,128)(2,1)S(1)} %select_select_fusion.9), channel_id=1, source_target_pairs={{0,8},{2,10},{4,12},{6,14},{8,0},{10,2},{12,4},{14,6},{16,24},{18,... | collective-permute-start | bytes 786440 | tf_op jit(solution)/shard_map/ppermute | solution.py:350
  15.3 1.6 %collective-permute-start.5 = (bf16[128,1024]{1,0:T(8,128)(2,1)S(1)}, bf16[128,1024]{1,0:T(8,128)(2,1)S(1)}, u32[]{:S(2)}, u32[]{:S(2)}) collective-permute-start(bf16[128,1024]{1,0:T(8,128)(2,1)S(1)} %select_select_fusion.8), channel_id=1, source_target_pairs={{0,16},{2,4},{4,2},{6,22},{8,24},{10,12},{12,10},{14,30},{16,0},{1... | collective-permute-start | bytes 786440 | tf_op jit(solution)/shard_map/ppermute | solution.py:350
  17.0 1.7 %collective-permute-start.6 = (bf16[128,1024]{1,0:T(8,128)(2,1)S(1)}, bf16[128,1024]{1,0:T(8,128)(2,1)S(1)}, u32[]{:S(2)}, u32[]{:S(2)}) collective-permute-start(bf16[128,1024]{1,0:T(8,128)(2,1)S(1)} %broadcast_select_fusion.4), channel_id=1, source_target_pairs={{0,2},{2,0},{4,6},{6,4},{8,10},{10,8},{12,14},{14,12},{16,18},{18,... | collective-permute-start | bytes 786440 | tf_op jit(solution)/shard_map/ppermute | solution.py:350
  18.8 2.0 %collective-permute-start.7 = (bf16[128,1024]{1,0:T(8,128)(2,1)S(1)}, bf16[128,1024]{1,0:T(8,128)(2,1)S(1)}, u32[]{:S(2)}, u32[]{:S(2)}) collective-permute-start(bf16[128,1024]{1,0:T(8,128)(2,1)S(1)} %select_select_fusion.7.after_ref), channel_id=1, source_target_pairs={{0,8},{2,10},{4,12},{6,14},{8,0},{10,2},{12,4},{14,6},{16,24},{18,... | collective-permute-start | bytes 786440 | tf_op jit(solution)/shard_map/ppermute | solution.py:350
  20.8 1.2 %more.6 = (f32[1,1024]{1,0:T(1,128)S(1)}, f32[16,256,128]{2,1,0:T(8,128)S(1)}) custom-call(s32[84]{0:T(128)S(1)} %dynamic-slice_bitcast_fusion.table_ref, bf16[18,256,128]{2,1,0:T(8,128)(2,1)S(1)} %get-tuple-element.29.left_ref, bf16[128,1024]{1,0:T(8,128)(2,1)S(1)} %select_select_fusion.7.after_ref, ...), custom_call_target="tpu_custom_call", output_to_operand_aliasing={{1}: (7, {})} | custom-call | tf_op jit(solution)/shard_map/more/pallas_call | solution.py:322
  22.2 1.6 %collective-permute-start.8 = (bf16[128,1024]{1,0:T(8,128)(2,1)S(1)}, bf16[128,1024]{1,0:T(8,128)(2,1)S(1)}, u32[]{:S(2)}, u32[]{:S(2)}) collective-permute-start(bf16[128,1024]{1,0:T(8,128)(2,1)S(1)} %select_select_fusion.6), channel_id=1, source_target_pairs={{0,16},{2,4},{4,2},{6,22},{8,24},{10,12},{12,10},{14,30},{16,0},{1... | collective-permute-start | bytes 786440 | tf_op jit(solution)/shard_map/ppermute | solution.py:350
  23.9 1.7 %collective-permute-start.9 = (bf16[128,1024]{1,0:T(8,128)(2,1)S(1)}, bf16[128,1024]{1,0:T(8,128)(2,1)S(1)}, u32[]{:S(2)}, u32[]{:S(2)}) collective-permute-start(bf16[128,1024]{1,0:T(8,128)(2,1)S(1)} %broadcast_select_fusion.3), channel_id=1, source_target_pairs={{0,2},{2,0},{4,6},{6,4},{8,10},{10,8},{12,14},{14,12},{16,18},{18,... | collective-permute-start | bytes 786440 | tf_op jit(solution)/shard_map/ppermute | solution.py:350
  26.3 1.1 %more.7 = (f32[1,1024]{1,0:T(1,128)S(1)}, f32[16,256,128]{2,1,0:T(8,128)S(1)}) custom-call(s32[84]{0:T(128)S(1)} %dynamic-slice_bitcast_fusion.table_ref, bf16[18,256,128]{2,1,0:T(8,128)(2,1)S(1)} %get-tuple-element.29.left_ref, bf16[128,1024]{1,0:T(8,128)(2,1)S(1)} %broadcast_select_fusion.2.after_ref, ...), custom_call_target="tpu_custom_call", output_to_operand_aliasing={{1}: (6, {})} | custom-call | tf_op jit(solution)/shard_map/more/pallas_call | solution.py:322
  27.6 1.6 %collective-permute-start.10 = (bf16[128,1024]{1,0:T(8,128)(2,1)S(1)}, bf16[128,1024]{1,0:T(8,128)(2,1)S(1)}, u32[]{:S(2)}, u32[]{:S(2)}) collective-permute-start(bf16[128,1024]{1,0:T(8,128)(2,1)S(1)} %select_select_fusion.5), channel_id=1, source_target_pairs={{0,16},{2,4},{4,2},{6,22},{8,24},{10,12},{12,10},{14,30},{16,0},{1... | collective-permute-start | bytes 786440 | tf_op jit(solution)/shard_map/ppermute | solution.py:350
  29.8 1.5 %collective-permute-start.12 = (bf16[128,1024]{1,0:T(8,128)(2,1)S(1)}, bf16[128,1024]{1,0:T(8,128)(2,1)S(1)}, u32[]{:S(2)}, u32[]{:S(2)}) collective-permute-start(bf16[128,1024]{1,0:T(8,128)(2,1)S(1)} %broadcast_select_fusion.1), channel_id=1, source_target_pairs={{0,2},{2,0},{4,6},{6,4},{8,10},{10,8},{12,14},{14,12},{16,18},{18,... | collective-permute-start | bytes 786440 | tf_op jit(solution)/shard_map/ppermute | solution.py:350
  31.6 1.0 %collective-permute-start.13 = (bf16[128,1024]{1,0:T(8,128)(2,1)S(1)}, bf16[128,1024]{1,0:T(8,128)(2,1)S(1)}, u32[]{:S(2)}, u32[]{:S(2)}) collective-permute-start(bf16[128,1024]{1,0:T(8,128)(2,1)S(1)} %select_select_fusion.4.after_ref), channel_id=1, source_target_pairs={{0,8},{2,10},{4,12},{6,14},{8,0},{10,2},{12,4},{14,6},{16,24},{18,... | collective-permute-start | bytes 786440 | tf_op jit(solution)/shard_map/ppermute | solution.py:350
  32.6 1.1 %more.8 = (f32[1,1024]{1,0:T(1,128)S(1)}, f32[16,256,128]{2,1,0:T(8,128)S(1)}) custom-call(s32[84]{0:T(128)S(1)} %dynamic-slice_bitcast_fusion.table_ref, bf16[18,256,128]{2,1,0:T(8,128)(2,1)S(1)} %get-tuple-element.29.left_ref, bf16[128,1024]{1,0:T(8,128)(2,1)S(1)} %select_select_fusion.4.after_ref, ...), custom_call_target="tpu_custom_call", output_to_operand_aliasing={{1}: (6, {})} | custom-call | tf_op jit(solution)/shard_map/more/pallas_call | solution.py:322
  33.9 1.2 %collective-permute-start.14 = (bf16[128,1024]{1,0:T(8,128)(2,1)S(1)}, bf16[128,1024]{1,0:T(8,128)(2,1)S(1)}, u32[]{:S(2)}, u32[]{:S(2)}) collective-permute-start(bf16[128,1024]{1,0:T(8,128)(2,1)S(1)} %select_select_fusion.3), channel_id=1, source_target_pairs={{0,16},{2,4},{4,2},{6,22},{8,24},{10,12},{12,10},{14,30},{16,0},{1... | collective-permute-start | bytes 786440 | tf_op jit(solution)/shard_map/ppermute | solution.py:350
  35.1 1.1 %collective-permute-done.10.refs_1_ = bf16[128,1024]{1,0:T(8,128)(2,1)S(1)} collective-permute-done((bf16[128,1024]{1,0:T(8,128)(2,1)S(1)}, bf16[128,1024]{1,0:T(8,128)(2,1)S(1)}, u32[]{:S(2)}, u32[]{:S(2)}) %collective-permute-start.10) | collective-permute-done | bytes 262176 | tf_op jit(solution)/shard_map/ppermute | solution.py:350
  36.2 2.0 %collective-permute-start.18 = (bf16[128,1024]{1,0:T(8,128)(2,1)S(1)}, bf16[128,1024]{1,0:T(8,128)(2,1)S(1)}, u32[]{:S(2)}, u32[]{:S(2)}) collective-permute-start(bf16[128,1024]{1,0:T(8,128)(2,1)S(1)} %broadcast_select_fusion), channel_id=1, source_target_pairs={{0,2},{2,0},{4,6},{6,4},{8,10},{10,8},{12,14},{14,12},{16,18},{18,... | collective-permute-start | bytes 786440 | tf_op jit(solution)/shard_map/ppermute | solution.py:350
  39.1 1.1 %more.9 = (f32[1,1024]{1,0:T(1,128)S(1)}, f32[16,256,128]{2,1,0:T(8,128)S(1)}) custom-call(s32[84]{0:T(128)S(1)} %dynamic-slice_bitcast_fusion.table_ref, bf16[18,256,128]{2,1,0:T(8,128)(2,1)S(1)} %get-tuple-element.29.left_ref, bf16[128,1024]{1,0:T(8,128)(2,1)S(1)} %select_select_fusion.2.after_ref, ...), custom_call_target="tpu_custom_call", output_to_operand_aliasing={{1}: (6, {})} | custom-call | tf_op jit(solution)/shard_map/more/pallas_call | solution.py:322
  40.4 1.3 %collective-permute-start.17 = (bf16[128,1024]{1,0:T(8,128)(2,1)S(1)}, bf16[128,1024]{1,0:T(8,128)(2,1)S(1)}, u32[]{:S(2)}, u32[]{:S(2)}) collective-permute-start(bf16[128,1024]{1,0:T(8,128)(2,1)S(1)} %select_select_fusion.1), channel_id=1, source_target_pairs={{0,16},{2,4},{4,2},{6,22},{8,24},{10,26},{12,28},{14,30},{16,0},{1... | collective-permute-start | bytes 786440 | tf_op jit(solution)/shard_map/ppermute | solution.py:350
  41.7 1.0 %collective-permute-done.14.refs_1_ = bf16[128,1024]{1,0:T(8,128)(2,1)S(1)} collective-permute-done((bf16[128,1024]{1,0:T(8,128)(2,1)S(1)}, bf16[128,1024]{1,0:T(8,128)(2,1)S(1)}, u32[]{:S(2)}, u32[]{:S(2)}) %collective-permute-start.14) | collective-permute-done | bytes 262176 | tf_op jit(solution)/shard_map/ppermute | solution.py:350
  42.8 1.1 %collective-permute-start.15 = (bf16[128,1024]{1,0:T(8,128)(2,1)S(1)}, bf16[128,1024]{1,0:T(8,128)(2,1)S(1)}, u32[]{:S(2)}, u32[]{:S(2)}) collective-permute-start(bf16[128,1024]{1,0:T(8,128)(2,1)S(1)} %select_select_fusion), channel_id=1, source_target_pairs={{0,2},{2,0},{4,6},{6,4},{8,10},{10,8},{12,14},{14,12},{16,18},{18,... | collective-permute-start | bytes 786440 | tf_op jit(solution)/shard_map/ppermute | solution.py:350
  43.9 1.5 %collective-permute-done.18.refs_2_ = bf16[128,1024]{1,0:T(8,128)(2,1)S(1)} collective-permute-done((bf16[128,1024]{1,0:T(8,128)(2,1)S(1)}, bf16[128,1024]{1,0:T(8,128)(2,1)S(1)}, u32[]{:S(2)}, u32[]{:S(2)}) %collective-permute-start.18) | collective-permute-done | bytes 262176 | tf_op jit(solution)/shard_map/ppermute | solution.py:350
  45.4 1.6 %more.10 = (f32[1,1024]{1,0:T(1,128)}, f32[16,256,128]{2,1,0:T(8,128)S(1)}) custom-call(s32[84]{0:T(128)S(1)} %dynamic-slice_bitcast_fusion.table_ref, bf16[18,256,128]{2,1,0:T(8,128)(2,1)S(1)} %get-tuple-element.29.left_ref, bf16[128,1024]{1,0:T(8,128)(2,1)S(1)} %collective-permute-done.13.after_ref.refs_0_, ...), custom_call_target="tpu_custom_call", output_to_operand_aliasing={{1}: (6, {})} | custom-call | tf_op jit(solution)/shard_map/more/pallas_call | solution.py:322
  47.1 1.5 %more.11 = (f32[1,1024]{1,0:T(1,128)}, f32[16,256,128]{2,1,0:T(8,128)S(1)}) custom-call(s32[84]{0:T(128)S(1)} %dynamic-slice_bitcast_fusion.table_ref, bf16[18,256,128]{2,1,0:T(8,128)(2,1)S(1)} %get-tuple-element.29.left_ref, bf16[128,1024]{1,0:T(8,128)(2,1)S(1)} %collective-permute-done.16.after_ref.refs_0_, ...), custom_call_target="tpu_custom_call", output_to_operand_aliasing={{1}: (5, {})} | custom-call | tf_op jit(solution)/shard_map/more/pallas_call | solution.py:322
  49.2 1.0 %last.1 = (bf16[2,12,64,128]{3,2,1,0:T(8,128)(2,1)S(1)}, bf16[2,12,64,128]{3,2,1,0:T(8,128)(2,1)S(1)}, f32[16,256,128]{2,1,0:T(8,128)S(1)}) custom-call(s32[84]{0:T(128)S(1)} %dynamic-slice_bitcast_fusion.table_ref, s32[2]{0:T(128)S(1)} %copy-done.4, bf16[18,256,128]{2,1,0:T(8,128)(2,1)S(1)} %get-tuple-element.29.left_ref, ...), custom_call_target="tpu_custom_call", output_to_operand_aliasing={{2}: (4, {})} | custom-call | tf_op jit(solution)/shard_map/last/pallas_call | solution.py:361
  50.3 1.7 %collective-permute-done.19.taken_ref = bf16[2,12,64,128]{3,2,1,0:T(8,128)(2,1)S(1)} collective-permute-done((bf16[2,12,64,128]{3,2,1,0:T(8,128)(2,1)S(1)}, bf16[2,12,64,128]{3,2,1,0:T(8,128)(2,1)S(1)}, u32[]{:S(2)}, u32[]{:S(2)}) %collective-permute-start.19) | collective-permute-done | bytes 393248 | tf_op jit(solution)/shard_map/ppermute | solution.py:370
  52.0 0.9 %join.1 = bf16[2,24,64,128]{3,2,1,0:T(8,128)(2,1)} custom-call(bf16[2,12,64,128]{3,2,1,0:T(8,128)(2,1)S(1)} %get-tuple-element.47.kept_ref, bf16[2,12,64,128]{3,2,1,0:T(8,128)(2,1)S(1)} %collective-permute-done.19.taken_ref), custom_call_target="tpu_custom_call" | custom-call | tf_op jit(solution)/shard_map/join/pallas_call | solution.py:371
  (59 shorter events, 6.8 us)
Async XLA Ops:
  0.0 1.2 %copy-start = (bf16[2,16,128,128]{3,2,1,0:T(8,128)(2,1)S(1)}, bf16[2,16,128,128]{3,2,1,0:T(8,128)(2,1)}, u32[]{:S(2)}) copy-start(bf16[2,16,128,128]{3,2,1,0:T(8,128)(2,1)} %band_ref.1) | copy-start | bytes 3145732
  1.2 0.7 %copy-start.2 = (s32[2,16]{1,0:T(2,128)S(1)}, s32[2,16]{1,0:T(2,128)}, u32[]{:S(2)}) copy-start(s32[2,16]{1,0:T(2,128)} %fill_ref.1) | copy-start | bytes 388
  2.9 10.4 %collective-permute-start = (bf16[128,1024]{1,0:T(8,128)(2,1)S(1)}, bf16[128,1024]{1,0:T(8,128)(2,1)S(1)}, u32[]{:S(2)}, u32[]{:S(2)}) collective-permute-start(bf16[128,1024]{1,0:T(8,128)(2,1)S(1)} %get-tuple-element.33), channel_id=1, source_target_pairs={{0,2},{2,0},{4,6},{6,4},{8,10},{10,8},{12,14},{14,12},{16,18},{18,... | collective-permute-start | bytes 786440 | tf_op jit(solution)/shard_map/ppermute | solution.py:350
  6.0 9.3 %collective-permute-start.1 = (bf16[128,1024]{1,0:T(8,128)(2,1)S(1)}, bf16[128,1024]{1,0:T(8,128)(2,1)S(1)}, u32[]{:S(2)}, u32[]{:S(2)}) collective-permute-start(bf16[128,1024]{1,0:T(8,128)(2,1)S(1)} %get-tuple-element.34), channel_id=1, source_target_pairs={{0,8},{2,10},{4,12},{6,14},{8,0},{10,2},{12,4},{14,6},{16,24},{18,... | collective-permute-start | bytes 786440 | tf_op jit(solution)/shard_map/ppermute | solution.py:350
  7.5 9.5 %collective-permute-start.2 = (bf16[128,1024]{1,0:T(8,128)(2,1)S(1)}, bf16[128,1024]{1,0:T(8,128)(2,1)S(1)}, u32[]{:S(2)}, u32[]{:S(2)}) collective-permute-start(bf16[128,1024]{1,0:T(8,128)(2,1)S(1)} %get-tuple-element.35), channel_id=1, source_target_pairs={{0,16},{2,18},{4,20},{6,22},{8,24},{10,12},{12,10},{14,30},{16,0},... | collective-permute-start | bytes 786440 | tf_op jit(solution)/shard_map/ppermute | solution.py:350
  9.0 9.7 %collective-permute-start.3 = (bf16[128,1024]{1,0:T(8,128)(2,1)S(1)}, bf16[128,1024]{1,0:T(8,128)(2,1)S(1)}, u32[]{:S(2)}, u32[]{:S(2)}) collective-permute-start(bf16[128,1024]{1,0:T(8,128)(2,1)S(1)} %get-tuple-element.31), channel_id=1, source_target_pairs={{0,2},{2,0},{4,6},{6,4},{8,10},{10,8},{12,14},{14,12},{16,18},{18,... | collective-permute-start | bytes 786440 | tf_op jit(solution)/shard_map/ppermute | solution.py:350
  10.2 1.2 %copy-start.1 = (bf16[2,16,128,128]{3,2,1,0:T(8,128)(2,1)S(1)}, bf16[2,16,128,128]{3,2,1,0:T(8,128)(2,1)}, u32[]{:S(2)}) copy-start(bf16[2,16,128,128]{3,2,1,0:T(8,128)(2,1)} %band_ref.1) | copy-start | bytes 3145732
  11.4 0.7 %copy-start.3 = (s32[2,16]{1,0:T(2,128)S(1)}, s32[2,16]{1,0:T(2,128)}, u32[]{:S(2)}) copy-start(s32[2,16]{1,0:T(2,128)} %fill_ref.1) | copy-start | bytes 388
  13.4 8.8 %collective-permute-start.4 = (bf16[128,1024]{1,0:T(8,128)(2,1)S(1)}, bf16[128,1024]{1,0:T(8,128)(2,1)S(1)}, u32[]{:S(2)}, u32[]{:S(2)}) collective-permute-start(bf16[128,1024]{1,0:T(8,128)(2,1)S(1)} %select_select_fusion.9), channel_id=1, source_target_pairs={{0,8},{2,10},{4,12},{6,14},{8,0},{10,2},{12,4},{14,6},{16,24},{18,... | collective-permute-start | bytes 786440 | tf_op jit(solution)/shard_map/ppermute | solution.py:350
  15.3 8.5 %collective-permute-start.5 = (bf16[128,1024]{1,0:T(8,128)(2,1)S(1)}, bf16[128,1024]{1,0:T(8,128)(2,1)S(1)}, u32[]{:S(2)}, u32[]{:S(2)}) collective-permute-start(bf16[128,1024]{1,0:T(8,128)(2,1)S(1)} %select_select_fusion.8), channel_id=1, source_target_pairs={{0,16},{2,4},{4,2},{6,22},{8,24},{10,12},{12,10},{14,30},{16,0},{1... | collective-permute-start | bytes 786440 | tf_op jit(solution)/shard_map/ppermute | solution.py:350
  17.0 8.6 %collective-permute-start.6 = (bf16[128,1024]{1,0:T(8,128)(2,1)S(1)}, bf16[128,1024]{1,0:T(8,128)(2,1)S(1)}, u32[]{:S(2)}, u32[]{:S(2)}) collective-permute-start(bf16[128,1024]{1,0:T(8,128)(2,1)S(1)} %broadcast_select_fusion.4), channel_id=1, source_target_pairs={{0,2},{2,0},{4,6},{6,4},{8,10},{10,8},{12,14},{14,12},{16,18},{18,... | collective-permute-start | bytes 786440 | tf_op jit(solution)/shard_map/ppermute | solution.py:350
  18.8 8.7 %collective-permute-start.7 = (bf16[128,1024]{1,0:T(8,128)(2,1)S(1)}, bf16[128,1024]{1,0:T(8,128)(2,1)S(1)}, u32[]{:S(2)}, u32[]{:S(2)}) collective-permute-start(bf16[128,1024]{1,0:T(8,128)(2,1)S(1)} %select_select_fusion.7.after_ref), channel_id=1, source_target_pairs={{0,8},{2,10},{4,12},{6,14},{8,0},{10,2},{12,4},{14,6},{16,24},{18,... | collective-permute-start | bytes 786440 | tf_op jit(solution)/shard_map/ppermute | solution.py:350
  22.2 7.5 %collective-permute-start.8 = (bf16[128,1024]{1,0:T(8,128)(2,1)S(1)}, bf16[128,1024]{1,0:T(8,128)(2,1)S(1)}, u32[]{:S(2)}, u32[]{:S(2)}) collective-permute-start(bf16[128,1024]{1,0:T(8,128)(2,1)S(1)} %select_select_fusion.6), channel_id=1, source_target_pairs={{0,16},{2,4},{4,2},{6,22},{8,24},{10,12},{12,10},{14,30},{16,0},{1... | collective-permute-start | bytes 786440 | tf_op jit(solution)/shard_map/ppermute | solution.py:350
  23.9 7.5 %collective-permute-start.9 = (bf16[128,1024]{1,0:T(8,128)(2,1)S(1)}, bf16[128,1024]{1,0:T(8,128)(2,1)S(1)}, u32[]{:S(2)}, u32[]{:S(2)}) collective-permute-start(bf16[128,1024]{1,0:T(8,128)(2,1)S(1)} %broadcast_select_fusion.3), channel_id=1, source_target_pairs={{0,2},{2,0},{4,6},{6,4},{8,10},{10,8},{12,14},{14,12},{16,18},{18,... | collective-permute-start | bytes 786440 | tf_op jit(solution)/shard_map/ppermute | solution.py:350
  25.7 10.5 %collective-permute-start.11 = (bf16[128,1024]{1,0:T(8,128)(2,1)S(1)}, bf16[128,1024]{1,0:T(8,128)(2,1)S(1)}, u32[]{:S(2)}, u32[]{:S(2)}) collective-permute-start(bf16[128,1024]{1,0:T(8,128)(2,1)S(1)} %broadcast_select_fusion.2.after_ref), channel_id=1, source_target_pairs={{0,8},{2,10},{4,12},{6,14},{8,0},{10,2},{12,4},{14,6},{16,24},{18,... | collective-permute-start | bytes 786440 | tf_op jit(solution)/shard_map/ppermute | solution.py:350
  27.6 8.6 %collective-permute-start.10 = (bf16[128,1024]{1,0:T(8,128)(2,1)S(1)}, bf16[128,1024]{1,0:T(8,128)(2,1)S(1)}, u32[]{:S(2)}, u32[]{:S(2)}) collective-permute-start(bf16[128,1024]{1,0:T(8,128)(2,1)S(1)} %select_select_fusion.5), channel_id=1, source_target_pairs={{0,16},{2,4},{4,2},{6,22},{8,24},{10,12},{12,10},{14,30},{16,0},{1... | collective-permute-start | bytes 786440 | tf_op jit(solution)/shard_map/ppermute | solution.py:350
  29.8 8.5 %collective-permute-start.12 = (bf16[128,1024]{1,0:T(8,128)(2,1)S(1)}, bf16[128,1024]{1,0:T(8,128)(2,1)S(1)}, u32[]{:S(2)}, u32[]{:S(2)}) collective-permute-start(bf16[128,1024]{1,0:T(8,128)(2,1)S(1)} %broadcast_select_fusion.1), channel_id=1, source_target_pairs={{0,2},{2,0},{4,6},{6,4},{8,10},{10,8},{12,14},{14,12},{16,18},{18,... | collective-permute-start | bytes 786440 | tf_op jit(solution)/shard_map/ppermute | solution.py:350
  31.6 8.7 %collective-permute-start.13 = (bf16[128,1024]{1,0:T(8,128)(2,1)S(1)}, bf16[128,1024]{1,0:T(8,128)(2,1)S(1)}, u32[]{:S(2)}, u32[]{:S(2)}) collective-permute-start(bf16[128,1024]{1,0:T(8,128)(2,1)S(1)} %select_select_fusion.4.after_ref), channel_id=1, source_target_pairs={{0,8},{2,10},{4,12},{6,14},{8,0},{10,2},{12,4},{14,6},{16,24},{18,... | collective-permute-start | bytes 786440 | tf_op jit(solution)/shard_map/ppermute | solution.py:350
  33.9 8.9 %collective-permute-start.14 = (bf16[128,1024]{1,0:T(8,128)(2,1)S(1)}, bf16[128,1024]{1,0:T(8,128)(2,1)S(1)}, u32[]{:S(2)}, u32[]{:S(2)}) collective-permute-start(bf16[128,1024]{1,0:T(8,128)(2,1)S(1)} %select_select_fusion.3), channel_id=1, source_target_pairs={{0,16},{2,4},{4,2},{6,22},{8,24},{10,12},{12,10},{14,30},{16,0},{1... | collective-permute-start | bytes 786440 | tf_op jit(solution)/shard_map/ppermute | solution.py:350
  36.2 9.2 %collective-permute-start.18 = (bf16[128,1024]{1,0:T(8,128)(2,1)S(1)}, bf16[128,1024]{1,0:T(8,128)(2,1)S(1)}, u32[]{:S(2)}, u32[]{:S(2)}) collective-permute-start(bf16[128,1024]{1,0:T(8,128)(2,1)S(1)} %broadcast_select_fusion), channel_id=1, source_target_pairs={{0,2},{2,0},{4,6},{6,4},{8,10},{10,8},{12,14},{14,12},{16,18},{18,... | collective-permute-start | bytes 786440 | tf_op jit(solution)/shard_map/ppermute | solution.py:350
  38.4 8.7 %collective-permute-start.16 = (bf16[128,1024]{1,0:T(8,128)(2,1)S(1)}, bf16[128,1024]{1,0:T(8,128)(2,1)S(1)}, u32[]{:S(2)}, u32[]{:S(2)}) collective-permute-start(bf16[128,1024]{1,0:T(8,128)(2,1)S(1)} %select_select_fusion.2.after_ref), channel_id=1, source_target_pairs={{0,8},{2,10},{4,12},{6,14},{8,0},{10,2},{12,4},{14,6},{16,24},{18,... | collective-permute-start | bytes 786440 | tf_op jit(solution)/shard_map/ppermute | solution.py:350
  40.4 6.6 %collective-permute-start.17 = (bf16[128,1024]{1,0:T(8,128)(2,1)S(1)}, bf16[128,1024]{1,0:T(8,128)(2,1)S(1)}, u32[]{:S(2)}, u32[]{:S(2)}) collective-permute-start(bf16[128,1024]{1,0:T(8,128)(2,1)S(1)} %select_select_fusion.1), channel_id=1, source_target_pairs={{0,16},{2,4},{4,2},{6,22},{8,24},{10,26},{12,28},{14,30},{16,0},{1... | collective-permute-start | bytes 786440 | tf_op jit(solution)/shard_map/ppermute | solution.py:350
  42.8 6.4 %collective-permute-start.15 = (bf16[128,1024]{1,0:T(8,128)(2,1)S(1)}, bf16[128,1024]{1,0:T(8,128)(2,1)S(1)}, u32[]{:S(2)}, u32[]{:S(2)}) collective-permute-start(bf16[128,1024]{1,0:T(8,128)(2,1)S(1)} %select_select_fusion), channel_id=1, source_target_pairs={{0,2},{2,0},{4,6},{6,4},{8,10},{10,8},{12,14},{14,12},{16,18},{18,... | collective-permute-start | bytes 786440 | tf_op jit(solution)/shard_map/ppermute | solution.py:350
  47.0 2.2 %copy-start.4 = (s32[2]{0:T(128)S(1)}, s32[2]{0:T(128)}, u32[]{:S(2)}) copy-start(s32[2]{0:T(128)} %reach_ref.1) | copy-start | bytes 28
  50.2 1.8 %collective-permute-start.19 = (bf16[2,12,64,128]{3,2,1,0:T(8,128)(2,1)S(1)}, bf16[2,12,64,128]{3,2,1,0:T(8,128)(2,1)S(1)}, u32[]{:S(2)}, u32[]{:S(2)}) collective-permute-start(bf16[2,12,64,128]{3,2,1,0:T(8,128)(2,1)S(1)} %get-tuple-element.48), channel_id=1, source_target_pairs={{0,1},{1,0},{2,3},{3,2},{4,5},{5,4},{6,7},{7,6},{8,9},{9,8},{10,11... | collective-permute-start | bytes 1179656 | tf_op jit(solution)/shard_map/ppermute | solution.py:370

commit v4 on v3

--- a/solution.py
+++ b/solution.py
@@ -272,6 +272,8 @@
     ops, packed = plan
     table, picks, choices = lookup(plan, chips)
     table = jnp.asarray(table)[lax.axis_index(RC + ("depth",))]
+    fill = pltpu.with_memory_space_constraint(a_fill, pltpu.HBM)
+    band = pltpu.with_memory_space_constraint(a_band, pltpu.HBM)
     params = pltpu.CompilerParams(vmem_limit_bytes=VMEM_LIMIT)
     unit_shape = jax.ShapeDtypeStruct((TILE, SLOTS * TILE), jnp.bfloat16)
     token_shape = jax.ShapeDtypeStruct((1, SLOTS * TILE), jnp.float32)
@@ -298,7 +300,7 @@
         ],
         compiler_params=params,
         name="units",
-    )(a_fill, a_band)
+    )(fill, band)
     n0, n1, *sent = sent
     buffers = {"n0": n0, "n1": n1}
     payload = left = sums = None

time: 53.2 us -> 51.9 us (0.976)
  local copies, waits for them, and re-layouts: 4.5 us -> 2.6 us
  Pallas kernels: 11.8 us -> 12.5 us
    unnamed x10 -> x6, local copies, waits for them, and re-layouts: 3.81 us -> 1.91 us
    pallas_call x1, Pallas kernels: 0.99 us -> 1.67 us  [per_device(): pl.pallas_call(functools.partial(units_kernel, min(packed, default=chips)...]
where the time goes in v4:
time: 51.9 us; the launch traced here: 51.7 us
  starting transfers between devices  28.1 us (54%)
  Pallas kernels  12.5 us (24%)
  waiting for transfers between devices  6.66 us (13%)
  local copies, waits for them, and re-layouts  2.6 us (5%)
  other arithmetic  1.63 us (3%)
    ppermute x19, starting transfers between devices, per_device(): buffers[o] = lax.ppermute(payload, RC, [(s, t) for s, t, _ in moves])  28 us
    pallas_call x6, Pallas kernels, more(): pl.pallas_call(functools.partial(more_kernel, base), out_shape=(token_sha...  7.65 us
    ppermute x19, waiting for transfers between devices, per_device(): buffers[o] = lax.ppermute(payload, RC, [(s, t) for s, t, _ in moves])  4.95 us
    unnamed x6, local copies, waits for them, and re-layouts  1.91 us
    ppermute x1, waiting for transfers between devices, per_device(): taken = lax.ppermute(given, 'depth', [(0, 1), (1, 0)])  1.71 us
    pallas_call x1, Pallas kernels, per_device(): pl.pallas_call(functools.partial(units_kernel, min(packed, default=chips)...  1.67 us
    pallas_call x1, Pallas kernels, start(): pl.pallas_call(functools.partial(first_kernel, 0), out_shape=(jax.ShapeDt...  1.23 us
  transfers between devices with their start and end apart: 20, of which 7 were waited for; matrix products, arithmetic and copies ran while one was open for 4% of the time, Pallas kernels for 17%

profile of v4, /device:TPU:0, one launch (start us, length us, event | category | flops | bytes accessed | tf_op | source)
XLA Modules:
  0.0 51.7 jit_solution(7206160801263552817)
XLA Ops:
  0.0 1.7 %units.1 = (bf16[128,1024]{1,0:T(8,128)(2,1)S(1)}, bf16[128,1024]{1,0:T(8,128)(2,1)S(1)}, bf16[128,1024]{1,0:T(8,128)(2,1)S(1)}, bf16[128,1024]{1,0:T(8,128)(2,1...) custom-call(s32[2,16]{1,0:T(2,128)} %fill_ref.1, ...), custom_call_target="tpu_custom_call" | custom-call | tf_op jit(solution)/shard_map/units/pallas_call | solution.py:291
  1.7 3.1 %collective-permute-start = (bf16[128,1024]{1,0:T(8,128)(2,1)S(1)}, bf16[128,1024]{1,0:T(8,128)(2,1)S(1)}, u32[]{:S(2)}, u32[]{:S(2)}) collective-permute-start(bf16[128,1024]{1,0:T(8,128)(2,1)S(1)} %get-tuple-element.33), channel_id=1, source_target_pairs={{0,2},{2,0},{4,6},{6,4},{8,10},{10,8},{12,14},{14,12},{16,18},{18,... | collective-permute-start | bytes 786440 | tf_op jit(solution)/shard_map/ppermute | solution.py:352
  4.8 1.5 %collective-permute-start.1 = (bf16[128,1024]{1,0:T(8,128)(2,1)S(1)}, bf16[128,1024]{1,0:T(8,128)(2,1)S(1)}, u32[]{:S(2)}, u32[]{:S(2)}) collective-permute-start(bf16[128,1024]{1,0:T(8,128)(2,1)S(1)} %get-tuple-element.34), channel_id=1, source_target_pairs={{0,8},{2,10},{4,12},{6,14},{8,0},{10,2},{12,4},{14,6},{16,24},{18,... | collective-permute-start | bytes 786440 | tf_op jit(solution)/shard_map/ppermute | solution.py:352
  6.3 1.5 %collective-permute-start.2 = (bf16[128,1024]{1,0:T(8,128)(2,1)S(1)}, bf16[128,1024]{1,0:T(8,128)(2,1)S(1)}, u32[]{:S(2)}, u32[]{:S(2)}) collective-permute-start(bf16[128,1024]{1,0:T(8,128)(2,1)S(1)} %get-tuple-element.35), channel_id=1, source_target_pairs={{0,16},{2,18},{4,20},{6,22},{8,24},{10,12},{12,10},{14,30},{16,0},... | collective-permute-start | bytes 786440 | tf_op jit(solution)/shard_map/ppermute | solution.py:352
  8.9 1.2 %copy-done = bf16[2,16,128,128]{3,2,1,0:T(8,128)(2,1)S(1)} copy-done((bf16[2,16,128,128]{3,2,1,0:T(8,128)(2,1)S(1)}, bf16[2,16,128,128]{3,2,1,0:T(8,128)(2,1)}, u32[]{:S(2)}) %copy-start) | copy-done | bytes 1048600
  10.8 1.2 %first.1 = (bf16[18,256,128]{2,1,0:T(8,128)(2,1)S(1)}, f32[1,1024]{1,0:T(1,128)S(1)}, f32[16,256,128]{2,1,0:T(8,128)S(1)}) custom-call(s32[84]{0:T(128)S(1)} %dynamic-slice_bitcast_fusion.table_ref, s32[2,16]{1,0:T(2,128)S(1)} %copy-done.1, bf16[2,16,128,128]{3,2,1,0:T(8,128)(2,1)S(1)} %copy-done, bf16[128,1024]{1,0:T(8,128)(2,1)S(1)} %get-tuple-element.27.refs_0_, ...), custom_call_target="tpu_custom_call" | custom-call | tf_op jit(solution)/shard_map/first/pallas_call | solution.py:310
  12.2 1.8 %collective-permute-start.4 = (bf16[128,1024]{1,0:T(8,128)(2,1)S(1)}, bf16[128,1024]{1,0:T(8,128)(2,1)S(1)}, u32[]{:S(2)}, u32[]{:S(2)}) collective-permute-start(bf16[128,1024]{1,0:T(8,128)(2,1)S(1)} %select_select_fusion.9), channel_id=1, source_target_pairs={{0,8},{2,10},{4,12},{6,14},{8,0},{10,2},{12,4},{14,6},{16,24},{18,... | collective-permute-start | bytes 786440 | tf_op jit(solution)/shard_map/ppermute | solution.py:352
  14.1 1.6 %collective-permute-start.5 = (bf16[128,1024]{1,0:T(8,128)(2,1)S(1)}, bf16[128,1024]{1,0:T(8,128)(2,1)S(1)}, u32[]{:S(2)}, u32[]{:S(2)}) collective-permute-start(bf16[128,1024]{1,0:T(8,128)(2,1)S(1)} %select_select_fusion.8), channel_id=1, source_target_pairs={{0,16},{2,4},{4,2},{6,22},{8,24},{10,12},{12,10},{14,30},{16,0},{1... | collective-permute-start | bytes 786440 | tf_op jit(solution)/shard_map/ppermute | solution.py:352
  15.8 1.7 %collective-permute-start.6 = (bf16[128,1024]{1,0:T(8,128)(2,1)S(1)}, bf16[128,1024]{1,0:T(8,128)(2,1)S(1)}, u32[]{:S(2)}, u32[]{:S(2)}) collective-permute-start(bf16[128,1024]{1,0:T(8,128)(2,1)S(1)} %broadcast_select_fusion.4), channel_id=1, source_target_pairs={{0,2},{2,0},{4,6},{6,4},{8,10},{10,8},{12,14},{14,12},{16,18},{18,... | collective-permute-start | bytes 786440 | tf_op jit(solution)/shard_map/ppermute | solution.py:352
  17.6 2.0 %collective-permute-start.7 = (bf16[128,1024]{1,0:T(8,128)(2,1)S(1)}, bf16[128,1024]{1,0:T(8,128)(2,1)S(1)}, u32[]{:S(2)}, u32[]{:S(2)}) collective-permute-start(bf16[128,1024]{1,0:T(8,128)(2,1)S(1)} %select_select_fusion.7.after_ref), channel_id=1, source_target_pairs={{0,8},{2,10},{4,12},{6,14},{8,0},{10,2},{12,4},{14,6},{16,24},{18,... | collective-permute-start | bytes 786440 | tf_op jit(solution)/shard_map/ppermute | solution.py:352
  19.6 1.2 %more.6 = (f32[1,1024]{1,0:T(1,128)S(1)}, f32[16,256,128]{2,1,0:T(8,128)S(1)}) custom-call(s32[84]{0:T(128)S(1)} %dynamic-slice_bitcast_fusion.table_ref, bf16[18,256,128]{2,1,0:T(8,128)(2,1)S(1)} %get-tuple-element.29.left_ref, bf16[128,1024]{1,0:T(8,128)(2,1)S(1)} %select_select_fusion.7.after_ref, ...), custom_call_target="tpu_custom_call", output_to_operand_aliasing={{1}: (7, {})} | custom-call | tf_op jit(solution)/shard_map/more/pallas_call | solution.py:324
  21.0 1.6 %collective-permute-start.8 = (bf16[128,1024]{1,0:T(8,128)(2,1)S(1)}, bf16[128,1024]{1,0:T(8,128)(2,1)S(1)}, u32[]{:S(2)}, u32[]{:S(2)}) collective-permute-start(bf16[128,1024]{1,0:T(8,128)(2,1)S(1)} %select_select_fusion.6), channel_id=1, source_target_pairs={{0,16},{2,4},{4,2},{6,22},{8,24},{10,12},{12,10},{14,30},{16,0},{1... | collective-permute-start | bytes 786440 | tf_op jit(solution)/shard_map/ppermute | solution.py:352
  22.7 1.7 %collective-permute-start.9 = (bf16[128,1024]{1,0:T(8,128)(2,1)S(1)}, bf16[128,1024]{1,0:T(8,128)(2,1)S(1)}, u32[]{:S(2)}, u32[]{:S(2)}) collective-permute-start(bf16[128,1024]{1,0:T(8,128)(2,1)S(1)} %broadcast_select_fusion.3), channel_id=1, source_target_pairs={{0,2},{2,0},{4,6},{6,4},{8,10},{10,8},{12,14},{14,12},{16,18},{18,... | collective-permute-start | bytes 786440 | tf_op jit(solution)/shard_map/ppermute | solution.py:352
  25.1 1.1 %more.7 = (f32[1,1024]{1,0:T(1,128)S(1)}, f32[16,256,128]{2,1,0:T(8,128)S(1)}) custom-call(s32[84]{0:T(128)S(1)} %dynamic-slice_bitcast_fusion.table_ref, bf16[18,256,128]{2,1,0:T(8,128)(2,1)S(1)} %get-tuple-element.29.left_ref, bf16[128,1024]{1,0:T(8,128)(2,1)S(1)} %broadcast_select_fusion.2.after_ref, ...), custom_call_target="tpu_custom_call", output_to_operand_aliasing={{1}: (6, {})} | custom-call | tf_op jit(solution)/shard_map/more/pallas_call | solution.py:324
  26.3 1.6 %collective-permute-start.10 = (bf16[128,1024]{1,0:T(8,128)(2,1)S(1)}, bf16[128,1024]{1,0:T(8,128)(2,1)S(1)}, u32[]{:S(2)}, u32[]{:S(2)}) collective-permute-start(bf16[128,1024]{1,0:T(8,128)(2,1)S(1)} %select_select_fusion.5), channel_id=1, source_target_pairs={{0,16},{2,4},{4,2},{6,22},{8,24},{10,12},{12,10},{14,30},{16,0},{1... | collective-permute-start | bytes 786440 | tf_op jit(solution)/shard_map/ppermute | solution.py:352
  28.5 1.5 %collective-permute-start.12 = (bf16[128,1024]{1,0:T(8,128)(2,1)S(1)}, bf16[128,1024]{1,0:T(8,128)(2,1)S(1)}, u32[]{:S(2)}, u32[]{:S(2)}) collective-permute-start(bf16[128,1024]{1,0:T(8,128)(2,1)S(1)} %broadcast_select_fusion.1), channel_id=1, source_target_pairs={{0,2},{2,0},{4,6},{6,4},{8,10},{10,8},{12,14},{14,12},{16,18},{18,... | collective-permute-start | bytes 786440 | tf_op jit(solution)/shard_map/ppermute | solution.py:352
  30.4 1.0 %collective-permute-start.13 = (bf16[128,1024]{1,0:T(8,128)(2,1)S(1)}, bf16[128,1024]{1,0:T(8,128)(2,1)S(1)}, u32[]{:S(2)}, u32[]{:S(2)}) collective-permute-start(bf16[128,1024]{1,0:T(8,128)(2,1)S(1)} %select_select_fusion.4.after_ref), channel_id=1, source_target_pairs={{0,8},{2,10},{4,12},{6,14},{8,0},{10,2},{12,4},{14,6},{16,24},{18,... | collective-permute-start | bytes 786440 | tf_op jit(solution)/shard_map/ppermute | solution.py:352
  31.4 1.1 %more.8 = (f32[1,1024]{1,0:T(1,128)S(1)}, f32[16,256,128]{2,1,0:T(8,128)S(1)}) custom-call(s32[84]{0:T(128)S(1)} %dynamic-slice_bitcast_fusion.table_ref, bf16[18,256,128]{2,1,0:T(8,128)(2,1)S(1)} %get-tuple-element.29.left_ref, bf16[128,1024]{1,0:T(8,128)(2,1)S(1)} %select_select_fusion.4.after_ref, ...), custom_call_target="tpu_custom_call", output_to_operand_aliasing={{1}: (6, {})} | custom-call | tf_op jit(solution)/shard_map/more/pallas_call | solution.py:324
  32.6 1.2 %collective-permute-start.14 = (bf16[128,1024]{1,0:T(8,128)(2,1)S(1)}, bf16[128,1024]{1,0:T(8,128)(2,1)S(1)}, u32[]{:S(2)}, u32[]{:S(2)}) collective-permute-start(bf16[128,1024]{1,0:T(8,128)(2,1)S(1)} %select_select_fusion.3), channel_id=1, source_target_pairs={{0,16},{2,4},{4,2},{6,22},{8,24},{10,12},{12,10},{14,30},{16,0},{1... | collective-permute-start | bytes 786440 | tf_op jit(solution)/shard_map/ppermute | solution.py:352
  33.9 1.1 %collective-permute-done.10.refs_1_ = bf16[128,1024]{1,0:T(8,128)(2,1)S(1)} collective-permute-done((bf16[128,1024]{1,0:T(8,128)(2,1)S(1)}, bf16[128,1024]{1,0:T(8,128)(2,1)S(1)}, u32[]{:S(2)}, u32[]{:S(2)}) %collective-permute-start.10) | collective-permute-done | bytes 262176 | tf_op jit(solution)/shard_map/ppermute | solution.py:352
  35.0 2.0 %collective-permute-start.18 = (bf16[128,1024]{1,0:T(8,128)(2,1)S(1)}, bf16[128,1024]{1,0:T(8,128)(2,1)S(1)}, u32[]{:S(2)}, u32[]{:S(2)}) collective-permute-start(bf16[128,1024]{1,0:T(8,128)(2,1)S(1)} %broadcast_select_fusion), channel_id=1, source_target_pairs={{0,2},{2,0},{4,6},{6,4},{8,10},{10,8},{12,14},{14,12},{16,18},{18,... | collective-permute-start | bytes 786440 | tf_op jit(solution)/shard_map/ppermute | solution.py:352
  37.2 0.7 %collective-permute-start.16 = (bf16[128,1024]{1,0:T(8,128)(2,1)S(1)}, bf16[128,1024]{1,0:T(8,128)(2,1)S(1)}, u32[]{:S(2)}, u32[]{:S(2)}) collective-permute-start(bf16[128,1024]{1,0:T(8,128)(2,1)S(1)} %select_select_fusion.2.after_ref), channel_id=1, source_target_pairs={{0,8},{2,10},{4,12},{6,14},{8,0},{10,2},{12,4},{14,6},{16,24},{18,... | collective-permute-start | bytes 786440 | tf_op jit(solution)/shard_map/ppermute | solution.py:352
  37.9 1.1 %more.9 = (f32[1,1024]{1,0:T(1,128)S(1)}, f32[16,256,128]{2,1,0:T(8,128)S(1)}) custom-call(s32[84]{0:T(128)S(1)} %dynamic-slice_bitcast_fusion.table_ref, bf16[18,256,128]{2,1,0:T(8,128)(2,1)S(1)} %get-tuple-element.29.left_ref, bf16[128,1024]{1,0:T(8,128)(2,1)S(1)} %select_select_fusion.2.after_ref, ...), custom_call_target="tpu_custom_call", output_to_operand_aliasing={{1}: (6, {})} | custom-call | tf_op jit(solution)/shard_map/more/pallas_call | solution.py:324
  39.2 1.3 %collective-permute-start.17 = (bf16[128,1024]{1,0:T(8,128)(2,1)S(1)}, bf16[128,1024]{1,0:T(8,128)(2,1)S(1)}, u32[]{:S(2)}, u32[]{:S(2)}) collective-permute-start(bf16[128,1024]{1,0:T(8,128)(2,1)S(1)} %select_select_fusion.1), channel_id=1, source_target_pairs={{0,16},{2,4},{4,2},{6,22},{8,24},{10,26},{12,28},{14,30},{16,0},{1... | collective-permute-start | bytes 786440 | tf_op jit(solution)/shard_map/ppermute | solution.py:352
  40.5 1.0 %collective-permute-done.14.refs_1_ = bf16[128,1024]{1,0:T(8,128)(2,1)S(1)} collective-permute-done((bf16[128,1024]{1,0:T(8,128)(2,1)S(1)}, bf16[128,1024]{1,0:T(8,128)(2,1)S(1)}, u32[]{:S(2)}, u32[]{:S(2)}) %collective-permute-start.14) | collective-permute-done | bytes 262176 | tf_op jit(solution)/shard_map/ppermute | solution.py:352
  41.5 1.1 %collective-permute-start.15 = (bf16[128,1024]{1,0:T(8,128)(2,1)S(1)}, bf16[128,1024]{1,0:T(8,128)(2,1)S(1)}, u32[]{:S(2)}, u32[]{:S(2)}) collective-permute-start(bf16[128,1024]{1,0:T(8,128)(2,1)S(1)} %select_select_fusion), channel_id=1, source_target_pairs={{0,2},{2,0},{4,6},{6,4},{8,10},{10,8},{12,14},{14,12},{16,18},{18,... | collective-permute-start | bytes 786440 | tf_op jit(solution)/shard_map/ppermute | solution.py:352
  42.7 1.5 %collective-permute-done.18.refs_2_ = bf16[128,1024]{1,0:T(8,128)(2,1)S(1)} collective-permute-done((bf16[128,1024]{1,0:T(8,128)(2,1)S(1)}, bf16[128,1024]{1,0:T(8,128)(2,1)S(1)}, u32[]{:S(2)}, u32[]{:S(2)}) %collective-permute-start.18) | collective-permute-done | bytes 262176 | tf_op jit(solution)/shard_map/ppermute | solution.py:352
  44.2 1.6 %more.10 = (f32[1,1024]{1,0:T(1,128)}, f32[16,256,128]{2,1,0:T(8,128)S(1)}) custom-call(s32[84]{0:T(128)S(1)} %dynamic-slice_bitcast_fusion.table_ref, bf16[18,256,128]{2,1,0:T(8,128)(2,1)S(1)} %get-tuple-element.29.left_ref, bf16[128,1024]{1,0:T(8,128)(2,1)S(1)} %collective-permute-done.13.after_ref.refs_0_, ...), custom_call_target="tpu_custom_call", output_to_operand_aliasing={{1}: (6, {})} | custom-call | tf_op jit(solution)/shard_map/more/pallas_call | solution.py:324
  45.8 1.5 %more.11 = (f32[1,1024]{1,0:T(1,128)}, f32[16,256,128]{2,1,0:T(8,128)S(1)}) custom-call(s32[84]{0:T(128)S(1)} %dynamic-slice_bitcast_fusion.table_ref, bf16[18,256,128]{2,1,0:T(8,128)(2,1)S(1)} %get-tuple-element.29.left_ref, bf16[128,1024]{1,0:T(8,128)(2,1)S(1)} %collective-permute-done.16.after_ref.refs_0_, ...), custom_call_target="tpu_custom_call", output_to_operand_aliasing={{1}: (5, {})} | custom-call | tf_op jit(solution)/shard_map/more/pallas_call | solution.py:324
  48.0 1.0 %last.1 = (bf16[2,12,64,128]{3,2,1,0:T(8,128)(2,1)S(1)}, bf16[2,12,64,128]{3,2,1,0:T(8,128)(2,1)S(1)}, f32[16,256,128]{2,1,0:T(8,128)S(1)}) custom-call(s32[84]{0:T(128)S(1)} %dynamic-slice_bitcast_fusion.table_ref, s32[2]{0:T(128)S(1)} %copy-done.2, bf16[18,256,128]{2,1,0:T(8,128)(2,1)S(1)} %get-tuple-element.29.left_ref, ...), custom_call_target="tpu_custom_call", output_to_operand_aliasing={{2}: (4, {})} | custom-call | tf_op jit(solution)/shard_map/last/pallas_call | solution.py:363
  49.0 1.7 %collective-permute-done.19.taken_ref = bf16[2,12,64,128]{3,2,1,0:T(8,128)(2,1)S(1)} collective-permute-done((bf16[2,12,64,128]{3,2,1,0:T(8,128)(2,1)S(1)}, bf16[2,12,64,128]{3,2,1,0:T(8,128)(2,1)S(1)}, u32[]{:S(2)}, u32[]{:S(2)}) %collective-permute-start.19) | collective-permute-done | bytes 393248 | tf_op jit(solution)/shard_map/ppermute | solution.py:372
  50.7 0.9 %join.1 = bf16[2,24,64,128]{3,2,1,0:T(8,128)(2,1)} custom-call(bf16[2,12,64,128]{3,2,1,0:T(8,128)(2,1)S(1)} %get-tuple-element.47.kept_ref, bf16[2,12,64,128]{3,2,1,0:T(8,128)(2,1)S(1)} %collective-permute-done.19.taken_ref), custom_call_target="tpu_custom_call" | custom-call | tf_op jit(solution)/shard_map/join/pallas_call | solution.py:373
  (55 shorter events, 5.4 us)
Async XLA Ops:
  1.7 10.4 %collective-permute-start = (bf16[128,1024]{1,0:T(8,128)(2,1)S(1)}, bf16[128,1024]{1,0:T(8,128)(2,1)S(1)}, u32[]{:S(2)}, u32[]{:S(2)}) collective-permute-start(bf16[128,1024]{1,0:T(8,128)(2,1)S(1)} %get-tuple-element.33), channel_id=1, source_target_pairs={{0,2},{2,0},{4,6},{6,4},{8,10},{10,8},{12,14},{14,12},{16,18},{18,... | collective-permute-start | bytes 786440 | tf_op jit(solution)/shard_map/ppermute | solution.py:352
  4.8 9.3 %collective-permute-start.1 = (bf16[128,1024]{1,0:T(8,128)(2,1)S(1)}, bf16[128,1024]{1,0:T(8,128)(2,1)S(1)}, u32[]{:S(2)}, u32[]{:S(2)}) collective-permute-start(bf16[128,1024]{1,0:T(8,128)(2,1)S(1)} %get-tuple-element.34), channel_id=1, source_target_pairs={{0,8},{2,10},{4,12},{6,14},{8,0},{10,2},{12,4},{14,6},{16,24},{18,... | collective-permute-start | bytes 786440 | tf_op jit(solution)/shard_map/ppermute | solution.py:352
  6.3 9.5 %collective-permute-start.2 = (bf16[128,1024]{1,0:T(8,128)(2,1)S(1)}, bf16[128,1024]{1,0:T(8,128)(2,1)S(1)}, u32[]{:S(2)}, u32[]{:S(2)}) collective-permute-start(bf16[128,1024]{1,0:T(8,128)(2,1)S(1)} %get-tuple-element.35), channel_id=1, source_target_pairs={{0,16},{2,18},{4,20},{6,22},{8,24},{10,12},{12,10},{14,30},{16,0},... | collective-permute-start | bytes 786440 | tf_op jit(solution)/shard_map/ppermute | solution.py:352
  7.8 9.7 %collective-permute-start.3 = (bf16[128,1024]{1,0:T(8,128)(2,1)S(1)}, bf16[128,1024]{1,0:T(8,128)(2,1)S(1)}, u32[]{:S(2)}, u32[]{:S(2)}) collective-permute-start(bf16[128,1024]{1,0:T(8,128)(2,1)S(1)} %get-tuple-element.31), channel_id=1, source_target_pairs={{0,2},{2,0},{4,6},{6,4},{8,10},{10,8},{12,14},{14,12},{16,18},{18,... | collective-permute-start | bytes 786440 | tf_op jit(solution)/shard_map/ppermute | solution.py:352
  8.9 1.2 %copy-start = (bf16[2,16,128,128]{3,2,1,0:T(8,128)(2,1)S(1)}, bf16[2,16,128,128]{3,2,1,0:T(8,128)(2,1)}, u32[]{:S(2)}) copy-start(bf16[2,16,128,128]{3,2,1,0:T(8,128)(2,1)} %band_ref.1) | copy-start | bytes 3145732
  10.1 0.7 %copy-start.1 = (s32[2,16]{1,0:T(2,128)S(1)}, s32[2,16]{1,0:T(2,128)}, u32[]{:S(2)}) copy-start(s32[2,16]{1,0:T(2,128)} %fill_ref.1) | copy-start | bytes 388
  12.2 8.8 %collective-permute-start.4 = (bf16[128,1024]{1,0:T(8,128)(2,1)S(1)}, bf16[128,1024]{1,0:T(8,128)(2,1)S(1)}, u32[]{:S(2)}, u32[]{:S(2)}) collective-permute-start(bf16[128,1024]{1,0:T(8,128)(2,1)S(1)} %select_select_fusion.9), channel_id=1, source_target_pairs={{0,8},{2,10},{4,12},{6,14},{8,0},{10,2},{12,4},{14,6},{16,24},{18,... | collective-permute-start | bytes 786440 | tf_op jit(solution)/shard_map/ppermute | solution.py:352
  14.1 8.5 %collective-permute-start.5 = (bf16[128,1024]{1,0:T(8,128)(2,1)S(1)}, bf16[128,1024]{1,0:T(8,128)(2,1)S(1)}, u32[]{:S(2)}, u32[]{:S(2)}) collective-permute-start(bf16[128,1024]{1,0:T(8,128)(2,1)S(1)} %select_select_fusion.8), channel_id=1, source_target_pairs={{0,16},{2,4},{4,2},{6,22},{8,24},{10,12},{12,10},{14,30},{16,0},{1... | collective-permute-start | bytes 786440 | tf_op jit(solution)/shard_map/ppermute | solution.py:352
  15.8 8.6 %collective-permute-start.6 = (bf16[128,1024]{1,0:T(8,128)(2,1)S(1)}, bf16[128,1024]{1,0:T(8,128)(2,1)S(1)}, u32[]{:S(2)}, u32[]{:S(2)}) collective-permute-start(bf16[128,1024]{1,0:T(8,128)(2,1)S(1)} %broadcast_select_fusion.4), channel_id=1, source_target_pairs={{0,2},{2,0},{4,6},{6,4},{8,10},{10,8},{12,14},{14,12},{16,18},{18,... | collective-permute-start | bytes 786440 | tf_op jit(solution)/shard_map/ppermute | solution.py:352
  17.6 8.7 %collective-permute-start.7 = (bf16[128,1024]{1,0:T(8,128)(2,1)S(1)}, bf16[128,1024]{1,0:T(8,128)(2,1)S(1)}, u32[]{:S(2)}, u32[]{:S(2)}) collective-permute-start(bf16[128,1024]{1,0:T(8,128)(2,1)S(1)} %select_select_fusion.7.after_ref), channel_id=1, source_target_pairs={{0,8},{2,10},{4,12},{6,14},{8,0},{10,2},{12,4},{14,6},{16,24},{18,... | collective-permute-start | bytes 786440 | tf_op jit(solution)/shard_map/ppermute | solution.py:352
  21.0 7.5 %collective-permute-start.8 = (bf16[128,1024]{1,0:T(8,128)(2,1)S(1)}, bf16[128,1024]{1,0:T(8,128)(2,1)S(1)}, u32[]{:S(2)}, u32[]{:S(2)}) collective-permute-start(bf16[128,1024]{1,0:T(8,128)(2,1)S(1)} %select_select_fusion.6), channel_id=1, source_target_pairs={{0,16},{2,4},{4,2},{6,22},{8,24},{10,12},{12,10},{14,30},{16,0},{1... | collective-permute-start | bytes 786440 | tf_op jit(solution)/shard_map/ppermute | solution.py:352
  22.7 7.5 %collective-permute-start.9 = (bf16[128,1024]{1,0:T(8,128)(2,1)S(1)}, bf16[128,1024]{1,0:T(8,128)(2,1)S(1)}, u32[]{:S(2)}, u32[]{:S(2)}) collective-permute-start(bf16[128,1024]{1,0:T(8,128)(2,1)S(1)} %broadcast_select_fusion.3), channel_id=1, source_target_pairs={{0,2},{2,0},{4,6},{6,4},{8,10},{10,8},{12,14},{14,12},{16,18},{18,... | collective-permute-start | bytes 786440 | tf_op jit(solution)/shard_map/ppermute | solution.py:352
  24.5 10.5 %collective-permute-start.11 = (bf16[128,1024]{1,0:T(8,128)(2,1)S(1)}, bf16[128,1024]{1,0:T(8,128)(2,1)S(1)}, u32[]{:S(2)}, u32[]{:S(2)}) collective-permute-start(bf16[128,1024]{1,0:T(8,128)(2,1)S(1)} %broadcast_select_fusion.2.after_ref), channel_id=1, source_target_pairs={{0,8},{2,10},{4,12},{6,14},{8,0},{10,2},{12,4},{14,6},{16,24},{18,... | collective-permute-start | bytes 786440 | tf_op jit(solution)/shard_map/ppermute | solution.py:352
  26.3 8.7 %collective-permute-start.10 = (bf16[128,1024]{1,0:T(8,128)(2,1)S(1)}, bf16[128,1024]{1,0:T(8,128)(2,1)S(1)}, u32[]{:S(2)}, u32[]{:S(2)}) collective-permute-start(bf16[128,1024]{1,0:T(8,128)(2,1)S(1)} %select_select_fusion.5), channel_id=1, source_target_pairs={{0,16},{2,4},{4,2},{6,22},{8,24},{10,12},{12,10},{14,30},{16,0},{1... | collective-permute-start | bytes 786440 | tf_op jit(solution)/shard_map/ppermute | solution.py:352
  28.5 8.5 %collective-permute-start.12 = (bf16[128,1024]{1,0:T(8,128)(2,1)S(1)}, bf16[128,1024]{1,0:T(8,128)(2,1)S(1)}, u32[]{:S(2)}, u32[]{:S(2)}) collective-permute-start(bf16[128,1024]{1,0:T(8,128)(2,1)S(1)} %broadcast_select_fusion.1), channel_id=1, source_target_pairs={{0,2},{2,0},{4,6},{6,4},{8,10},{10,8},{12,14},{14,12},{16,18},{18,... | collective-permute-start | bytes 786440 | tf_op jit(solution)/shard_map/ppermute | solution.py:352
  30.4 8.7 %collective-permute-start.13 = (bf16[128,1024]{1,0:T(8,128)(2,1)S(1)}, bf16[128,1024]{1,0:T(8,128)(2,1)S(1)}, u32[]{:S(2)}, u32[]{:S(2)}) collective-permute-start(bf16[128,1024]{1,0:T(8,128)(2,1)S(1)} %select_select_fusion.4.after_ref), channel_id=1, source_target_pairs={{0,8},{2,10},{4,12},{6,14},{8,0},{10,2},{12,4},{14,6},{16,24},{18,... | collective-permute-start | bytes 786440 | tf_op jit(solution)/shard_map/ppermute | solution.py:352
  32.6 8.9 %collective-permute-start.14 = (bf16[128,1024]{1,0:T(8,128)(2,1)S(1)}, bf16[128,1024]{1,0:T(8,128)(2,1)S(1)}, u32[]{:S(2)}, u32[]{:S(2)}) collective-permute-start(bf16[128,1024]{1,0:T(8,128)(2,1)S(1)} %select_select_fusion.3), channel_id=1, source_target_pairs={{0,16},{2,4},{4,2},{6,22},{8,24},{10,12},{12,10},{14,30},{16,0},{1... | collective-permute-start | bytes 786440 | tf_op jit(solution)/shard_map/ppermute | solution.py:352
  35.0 9.2 %collective-permute-start.18 = (bf16[128,1024]{1,0:T(8,128)(2,1)S(1)}, bf16[128,1024]{1,0:T(8,128)(2,1)S(1)}, u32[]{:S(2)}, u32[]{:S(2)}) collective-permute-start(bf16[128,1024]{1,0:T(8,128)(2,1)S(1)} %broadcast_select_fusion), channel_id=1, source_target_pairs={{0,2},{2,0},{4,6},{6,4},{8,10},{10,8},{12,14},{14,12},{16,18},{18,... | collective-permute-start | bytes 786440 | tf_op jit(solution)/shard_map/ppermute | solution.py:352
  37.2 8.7 %collective-permute-start.16 = (bf16[128,1024]{1,0:T(8,128)(2,1)S(1)}, bf16[128,1024]{1,0:T(8,128)(2,1)S(1)}, u32[]{:S(2)}, u32[]{:S(2)}) collective-permute-start(bf16[128,1024]{1,0:T(8,128)(2,1)S(1)} %select_select_fusion.2.after_ref), channel_id=1, source_target_pairs={{0,8},{2,10},{4,12},{6,14},{8,0},{10,2},{12,4},{14,6},{16,24},{18,... | collective-permute-start | bytes 786440 | tf_op jit(solution)/shard_map/ppermute | solution.py:352
  39.2 6.7 %collective-permute-start.17 = (bf16[128,1024]{1,0:T(8,128)(2,1)S(1)}, bf16[128,1024]{1,0:T(8,128)(2,1)S(1)}, u32[]{:S(2)}, u32[]{:S(2)}) collective-permute-start(bf16[128,1024]{1,0:T(8,128)(2,1)S(1)} %select_select_fusion.1), channel_id=1, source_target_pairs={{0,16},{2,4},{4,2},{6,22},{8,24},{10,26},{12,28},{14,30},{16,0},{1... | collective-permute-start | bytes 786440 | tf_op jit(solution)/shard_map/ppermute | solution.py:352
  41.5 6.4 %collective-permute-start.15 = (bf16[128,1024]{1,0:T(8,128)(2,1)S(1)}, bf16[128,1024]{1,0:T(8,128)(2,1)S(1)}, u32[]{:S(2)}, u32[]{:S(2)}) collective-permute-start(bf16[128,1024]{1,0:T(8,128)(2,1)S(1)} %select_select_fusion), channel_id=1, source_target_pairs={{0,2},{2,0},{4,6},{6,4},{8,10},{10,8},{12,14},{14,12},{16,18},{18,... | collective-permute-start | bytes 786440 | tf_op jit(solution)/shard_map/ppermute | solution.py:352
  45.8 2.1 %copy-start.2 = (s32[2]{0:T(128)S(1)}, s32[2]{0:T(128)}, u32[]{:S(2)}) copy-start(s32[2]{0:T(128)} %reach_ref.1) | copy-start | bytes 28
  48.9 1.8 %collective-permute-start.19 = (bf16[2,12,64,128]{3,2,1,0:T(8,128)(2,1)S(1)}, bf16[2,12,64,128]{3,2,1,0:T(8,128)(2,1)S(1)}, u32[]{:S(2)}, u32[]{:S(2)}) collective-permute-start(bf16[2,12,64,128]{3,2,1,0:T(8,128)(2,1)S(1)} %get-tuple-element.48), channel_id=1, source_target_pairs={{0,1},{1,0},{2,3},{3,2},{4,5},{5,4},{6,7},{7,6},{8,9},{9,8},{10,11... | collective-permute-start | bytes 1179656 | tf_op jit(solution)/shard_map/ppermute | solution.py:372

commit v5 on v4

v5 whole, which is shorter than its diff:
```python
import functools

import jax
import jax.numpy as jnp
import numpy as np
from jax import lax
from jax.experimental import pallas as pl
from jax.experimental.pallas import tpu as pltpu
from jax.sharding import PartitionSpec as P

OUT_BAND = 24
TILE = 128
SLOTS = 8
SUMS = 17
NO_TERM = 17
RC = ("row", "col")


STEPS = (
    (1, (
        (1, 1, 0), (3, 3, 1), (4, 4, 1), (5, 5, 1), (6, 6, 1), (7, 7, 1), (8, 8, 0), (9, 9, 0),
        (10, 10, 1), (11, 11, 1), (13, 13, 0), (14, 14, 0), (15, 15, 0),
    )),
    (0, (
        (2, 2, 0), (4, 4, 0), (5, 5, 0), (6, 6, 0), (7, 7, 1), (8, 8, 1), (9, 9, 0),
        (10, 10, 1), (11, 11, 1), (12, 12, 0), (14, 14, 0), (15, 15, 0),
    )),
    (8, (
        (2, 2, 1), (4, 4, 1), (5, 5, 1), (6, 6, 1), (8, 8, 0), (9, 9, 1), (10, 10, 0),
        (11, 11, 0), (12, 12, 0), (13, 13, 0), (14, 14, 0), (15, 15, 0),
    )),
    (1, (
        (1, 1, 1), (3, 3, 0), (4, 4, 0), (5, 5, 0), (6, 6, 0), (7, 7, 0), (8, 8, 1), (9, 9, 1),
        (10, 10, 0), (11, 11, 0),
    )),
    (0, (
        (2, 3, 1), (4, 5, 1), (5, 4, 1), (6, 6, 1), (7, 6, 1), (8, 9, 0), (10, 10, 0),
        (12, 13, 0), (14, 15, 0), (15, 14, 0),
    )),
    (9, (
        (1, 5, 0), (2, 6, 0), (5, 4, 1), (6, 7, 1), (8, 9, 0), (9, 8, 0), (10, 11, 1),
        (11, 10, 1), (12, 8, 1), (13, 9, 0), (14, 10, 1), (15, 14, 0),
    )),
    (1, (
        (0, 8, 0), (1, 5, 0), (3, 11, 0), (4, 12, 0), (5, 6, 1), (8, 12, 0), (13, 14, 0),
        (14, 13, 0),
    )),
    (0, (
        (0, 8, 0), (1, 9, 1), (2, 10, 0), (3, 11, 0), (4, 4, 1), (5, 6, 1), (6, 7, 1),
        (7, 7, 0), (11, 10, 0), (12, 4, 1), (13, 13, 0), (14, 13, 0),
    )),
    (9, (
        (1, 9, 1), (2, 3, 0), (4, 5, 0), (5, 4, 0), (6, 7, 0), (8, 9, 1), (9, 8, 1),
        (10, 2, 1), (11, 10, 0), (12, 9, 0), (14, 10, 0), (15, 11, 1),
    )),
    (1, (
        (0, 9, 0), (1, 6, 0), (2, 5, 0), (3, 10, 1), (4, 8, 1), (5, 7, 1), (6, 5, 1),
        (7, 14, 0), (9, 11, 1), (10, 8, 0), (13, 10, 1), (14, 9, 0),
    )),
    (0, (
        (1, 6, 0), (2, 11, 0), (3, 10, 1), (4, 6, 1), (5, 7, 1), (6, 5, 1), (7, 6, 0),
        (12, 14, 0), (14, 9, 0),
    )),
    (9, (
        (1, 4, 1), (2, 3, 1), (5, 12, 0), (6, 10, 0), (10, 11, 0), (12, 13, 0), (14, 15, 0),
        (15, 13, 0),
    )),
    (1, (
        (0, 4, 0), (1, 3, 0), (2, 9, 1), (3, 7, 0), (4, 9, 0), (5, 7, 0), (6, 4, 0),
        (7, 11, 1), (9, 2, 1), (10, 8, 1), (13, 10, 0),
    )),
    (0, (
        (0, 6, 0), (1, 8, 0), (2, 10, 1), (3, 10, 0), (4, 7, 1), (5, 8, 1), (7, 5, 1),
        (8, 11, 1), (9, 11, 1), (10, 8, 0), (11, 8, 0), (12, 10, 1), (13, 10, 1),
    )),
    (9, (
        (1, 9, 0), (2, 2, 0), (5, 8, 1), (6, 11, 0), (9, 12, 0), (10, 15, 0), (11, 8, 0),
        (12, 10, 1), (15, 9, 0),
    )),
    (1, (
        (0, 5, 1), (1, 3, 1), (2, 4, 1), (4, 13, 0), (5, 10, 0), (6, 12, 0), (7, 13, 0),
        (8, 14, 0), (9, 11, 0), (10, 13, 0), (13, 15, 0),
    )),
    (0, (
        (0, 9, 1), (2, 9, 1), (3, 9, 1), (4, 7, 0), (5, 7, 0), (6, 4, 0), (7, 4, 0),
        (12, 10, 0), (13, 10, 0),
    )),
    (7, (
        (1, 8, 1), (2, 2, 1), (8, 2, 1), (11, 8, 1), (12, 11, 1), (13, 11, 1), (14, 8, 0),
        (15, 8, 0),
    )),
    (1, (
        (1, 2, 0), (2, 9, 0), (3, 8, 0), (4, 10, 1), (5, 11, 0), (6, 8, 1), (7, 9, 0),
        (9, 15, 0), (10, 12, 0),
    )),
)


def partner(kind, chip):
    z, row = chip % 4, chip // 4
    if kind < 6:
        return chip ^ (4, 1, 8, 2, 3, 12)[kind]
    if z in (1, 2) and (kind - 6) >> (row % 2) & 1:
        return chip ^ 3
    return chip ^ 8


def grid_plan():
    ops = []
    for kind, sends in STEPS:
        sent = {source: (block, part) for source, block, part in sends}
        ops.append([(c, partner(kind, c), sent.get(c)) for c in range(16)])
    return ops, frozenset(range(12, 16))


def direct_plan(chips):
    ops = []
    for m in range(1, 9):
        for part in range(2 if m < 8 else 1):
            ops.append([(r + m, r, (r + m, part)) for r in range(chips - m)])
    return ops, frozenset()


def first_slot(k, core):
    return (k - core + ((core + k) & 1)) // 2


def left_tiles(block, part, chip, packed):
    m = block - chip
    ks = [2 * m + part] * 2
    if packed:
        ks = [2 * m, 2 * m + 1] if part == 0 else [NO_TERM, NO_TERM]
    return [k if m >= 0 and k < NO_TERM else NO_TERM for k in ks]


def by_chip(values, chip):
    if len(set(values)) == 1:
        return values[0]
    word = 0
    for at in range(0, len(values), 6):
        bits = sum(v << 5 * i for i, v in enumerate(values[at : at + 6]))
        word = jnp.where(chip >= at, bits, word)
    return (word >> 5 * (chip % 6)) & 31


def position():
    chip = lax.axis_index("row") * lax.axis_size("col") + lax.axis_index("col")
    return chip, lax.axis_index("depth")


VMEM = pl.BlockSpec(memory_space=pltpu.VMEM)
SMEM = pl.BlockSpec(memory_space=pltpu.SMEM)
HBM = pl.BlockSpec(memory_space=pltpu.HBM)
VMEM_LIMIT = 12 * 2**20
FIRST = 4
LAG = 4
ADD_AT = (9, 12, 15, 18)
LAST = (2, 1)


def units_kernel(packed_from, choice_masks, fill_hbm, band_hbm, *refs):
    outs, flags, (fill_ref, band_ref, sems) = refs[:2], refs[2], refs[3:]
    fill_copy = pltpu.make_async_copy(fill_hbm, fill_ref, sems.at[2])
    copies = [
        pltpu.make_async_copy(band_hbm.at[row], band_ref.at[row], sems.at[row]) for row in range(2)
    ]
    for copy in (fill_copy, *copies):
        copy.start()
    chip, core = position()
    for i, mask in enumerate(choice_masks):
        bit = ((mask >> chip) & 1).astype(jnp.float32)
        flags[i : i + 1, :] = jnp.full((1, flags.shape[1]), bit, flags.dtype)
    packed = chip >= packed_from
    for copy in (fill_copy, *copies):
        copy.wait()
    for part, unit in enumerate(outs):
        for slot in range(SLOTS):
            row, t = part, slot
            if part == 0:
                row = jnp.where(packed, slot // 4, 0)
                t = jnp.where(packed, slot % 4, slot)
            entry = 2 * t + ((core + row) & 1)
            fill = fill_ref[row, entry].astype(jnp.float32)
            tile = band_ref[row, entry].astype(jnp.float32) * fill
            unit[:, slot * TILE : (slot + 1) * TILE] = tile.astype(jnp.bfloat16)


def add_terms(terms, left_ref, units, sums):
    width = SLOTS // 2 * TILE
    chip, core = position()
    for (first, second), unit in zip(terms, units):
        ks = [by_chip(first, chip), by_chip(second, chip)]
        slots = [first_slot(k, core) for k in ks]
        slots[1] = jnp.where(ks[0] == ks[1], slots[0] + SLOTS // 2, slots[1])
        for half, (k, slot) in enumerate(zip(ks, slots)):
            product = jnp.dot(
                left_ref[k],
                unit[:, half * width : (half + 1) * width],
                preferred_element_type=jnp.float32,
            )
            for q in range(SLOTS // 2):
                sums[slot + q] += product[:, q * TILE : (q + 1) * TILE]


def first_kernel(terms, reach_hbm, fill_hbm, band_hbm, *refs):
    units, (left, keep, token, sums) = refs[:2], refs[2:6]
    reach_ref, fill_ref, band_ref, sems = refs[6:]
    copies = [
        pltpu.make_async_copy(source, target, sems.at[i])
        for i, (source, target) in enumerate(
            [(reach_hbm, reach_ref), (fill_hbm, fill_ref), (band_hbm, band_ref)]
        )
    ]
    for copy in copies:
        copy.start()
    sums[...] = jnp.zeros(sums.shape, jnp.float32)
    for copy in copies:
        copy.wait()
    token[...] = jnp.zeros(token.shape, token.dtype)
    _, core = position()
    for row in range(2):
        for s in range(OUT_BAND // 2):
            kept = 2 * s + ((core + row) & 1) < reach_ref[row]
            value = jnp.where(kept, 1.0, 0.0).astype(jnp.float32)
            keep[row, s : s + 1, :] = jnp.full((1, TILE), value, jnp.float32)
    zero = jnp.zeros((TILE, TILE), jnp.bfloat16)
    left[0, TILE:] = zero
    left[16, :TILE] = zero
    left[NO_TERM] = jnp.zeros((2 * TILE, TILE), jnp.bfloat16)
    for row in range(2):
        for entry in range(16):
            fill = fill_ref[row, entry].astype(jnp.float32)
            tile = band_ref[row, entry].astype(jnp.float32) * fill
            left[entry + row, row * TILE : (row + 1) * TILE] = tile.astype(jnp.bfloat16)
    add_terms(terms, left, units, sums)


def more_kernel(terms, left_ref, after_ref, *refs):
    units, (token, sums) = refs[:-3], refs[-2:]
    token[...] = jnp.zeros(token.shape, token.dtype)
    add_terms(terms, left_ref, units, sums)


def last_kernel(terms, left_ref, keep_ref, *refs):
    units, kept, given, sums = refs[:-4], refs[-3], refs[-2], refs[-1]
    add_terms(terms, left_ref, units, sums)
    _, core = position()
    half = TILE // 2
    for row in range(2):
        shift = 0 if row == 0 else 1 - core
        for s in range(OUT_BAND // 2):
            keep = keep_ref[row, s : s + 1, :] > 0.5
            for out, side in ((kept, core), (given, 1 - core)):
                start = pl.multiple_of(row * TILE + side * half, half)
                tile = sums[s + shift, pl.ds(start, half), :]
                out[row, s] = jnp.where(keep, tile, 0.0).astype(jnp.bfloat16)


def place_kernel(partner, tiles, *refs):
    out, sems = refs[-2:]
    _, core = position()
    copies = []
    for row in range(2):
        odd = (core + row + partner) & 1
        copies.append(pltpu.make_async_copy(tiles.at[row], out.at[row, :, odd], sems.at[row]))
    for copy in copies:
        copy.start()
    for copy in copies:
        copy.wait()


def lookup(plan, chips):
    ops, packed = plan
    held = {"n0": [(r, 0) for r in range(chips)], "n1": [(r, 1) for r in range(chips)]}
    order = ["n0", "n1"] + list(range(len(ops)))
    picks = np.zeros((chips, len(ops)), np.int32)
    choices = []
    for o, moves in enumerate(ops):
        names = []
        got = [None] * chips
        for source, target, unit in moves:
            if unit is None:
                continue
            name = next(n for n in order if n in held and held[n][source] == unit)
            if name not in names:
                names.append(name)
            picks[source, o] = names.index(name)
            got[target] = unit
        held[o] = got
        choices.append(names)
    terms = {n: [[], []] for n in order}
    for r in range(chips):
        done = set()
        for n in order:
            unit = held[n][r]
            fresh = unit is not None and unit not in done
            done.add(unit)
            ks = left_tiles(*unit, r, unit[0] in packed) if fresh else [NO_TERM] * 2
            for half in range(2):
                terms[n][half].append(ks[half])
    if not packed:
        terms = {n: [[max(k, key=k.count)] for k in ks] for n, ks in terms.items()}
    return terms, picks, choices


def per_device(plan, chips, a_band, a_fill, c_reach):
    ops, packed = plan
    terms, picks, choices = lookup(plan, chips)
    reach = pltpu.with_memory_space_constraint(c_reach, pltpu.HBM)
    fill = pltpu.with_memory_space_constraint(a_fill, pltpu.HBM)
    band = pltpu.with_memory_space_constraint(a_band, pltpu.HBM)
    params = pltpu.CompilerParams(vmem_limit_bytes=VMEM_LIMIT)
    unit_shape = jax.ShapeDtypeStruct((TILE, SLOTS * TILE), jnp.bfloat16)
    token_shape = jax.ShapeDtypeStruct((1, SLOTS * TILE), jnp.float32)
    sums_shape = jax.ShapeDtypeStruct((SUMS, 2 * TILE, TILE), jnp.float32)
    choice_masks, flag_at = [], {}
    for o, names in enumerate(choices):
        flag_at[o] = len(choice_masks)
        for i in range(len(names) - 1):
            choice_masks.append(sum(int(picks[r, o] == i) << r for r in range(chips)))
    flags_shape = jax.ShapeDtypeStruct((max(8, len(choice_masks)), SLOTS * TILE), jnp.float32)
    n0, n1, flags = pl.pallas_call(
        functools.partial(units_kernel, min(packed, default=chips), choice_masks),
        out_shape=(unit_shape, unit_shape, flags_shape),
        in_specs=[HBM, HBM],
        out_specs=(VMEM,) * 3,
        scratch_shapes=[
            pltpu.SMEM(a_fill.shape, a_fill.dtype),
            pltpu.VMEM(a_band.shape, a_band.dtype),
            pltpu.SemaphoreType.DMA((3,)),
        ],
        compiler_params=params,
        name="units",
    )(fill, band)
    buffers = {"n0": n0, "n1": n1}
    payload = left = keep = sums = None
    added = 0

    def start():
        return pl.pallas_call(
            functools.partial(first_kernel, [terms["n0"], terms["n1"]]),
            out_shape=(
                jax.ShapeDtypeStruct((NO_TERM + 1, 2 * TILE, TILE), jnp.bfloat16),
                jax.ShapeDtypeStruct((2, OUT_BAND // 2, TILE), jnp.float32),
                token_shape,
                sums_shape,
            ),
            in_specs=[HBM, HBM, HBM, VMEM, VMEM],
            out_specs=(VMEM,) * 4,
            scratch_shapes=[
                pltpu.SMEM(c_reach.shape, c_reach.dtype),
                pltpu.SMEM(a_fill.shape, a_fill.dtype),
                pltpu.VMEM(a_band.shape, a_band.dtype),
                pltpu.SemaphoreType.DMA((3,)),
            ],
            compiler_params=params,
            name="first",
        )(reach, fill, band, n0, n1)

    def more(after, sums, names):
        units = [buffers[n] for n in names]
        return pl.pallas_call(
            functools.partial(more_kernel, [terms[n] for n in names]),
            out_shape=(token_shape, sums_shape),
            in_specs=[VMEM] * (3 + len(units)),
            out_specs=(VMEM, VMEM),
            input_output_aliases={2 + len(units): 1},
            compiler_params=params,
            name="more",
        )(left, after, *units, sums)

    for o, moves in enumerate(ops):
        sources = [buffers[n] for n in choices[o]]
        order = 0 * payload[:1].astype(jnp.float32) if o > 0 else 0
        if o == FIRST:
            left, keep, token, sums = start()
            order += token
        elif o in ADD_AT:
            token, sums = more(payload, sums, range(added, o - LAG))
            added = o - LAG
            order += token
        payload = sources[-1]
        if len(sources) == 1:
            payload = jnp.where(order > 0.5, n0, payload)
        for i in reversed(range(len(sources) - 1)):
            at = flag_at[o] + i
            payload = jnp.where(flags[at : at + 1] + order > 0.5, sources[i], payload)
        buffers[o] = lax.ppermute(payload, RC, [(s, t) for s, t, _ in moves])
    if sums is None:
        left, keep, _, sums = start()
    for count in LAST:
        _, sums = more(buffers[added], sums, range(added, len(ops) - count))
        added = len(ops) - count

    piece = jax.ShapeDtypeStruct((2, OUT_BAND // 2, TILE // 2, TILE), jnp.bfloat16)
    units = [buffers[n] for n in range(added, len(ops))]
    n_in = 2 + len(units)
    kept, given, _ = pl.pallas_call(
        functools.partial(last_kernel, [terms[n] for n in range(added, len(ops))]),
        out_shape=(piece, piece, sums_shape),
        in_specs=[VMEM] * (n_in + 1),
        out_specs=(VMEM, VMEM, VMEM),
        input_output_aliases={n_in: 2},
        compiler_params=params,
        name="last",
    )(left, keep, *units, sums)
    taken = lax.ppermute(given, "depth", [(0, 1), (1, 0)])
    out = None
    for partner, tiles in enumerate((kept, taken)):
        out = pl.pallas_call(
            functools.partial(place_kernel, partner),
            out_shape=jax.ShapeDtypeStruct(
                (2, OUT_BAND // 2, 2, TILE // 2, TILE), jnp.bfloat16
            ),
            in_specs=[VMEM, HBM][: 1 + partner],
            out_specs=HBM,
            scratch_shapes=[pltpu.SemaphoreType.DMA((2,))],
            input_output_aliases={1: 0} if partner else {},
            compiler_params=params,
            name="place",
        )(*[tiles, out][: 1 + partner])
    return out.reshape(2, OUT_BAND, TILE // 2, TILE)


def solution(mesh):
    rows, cols = mesh.shape["row"], mesh.shape["col"]
    plan = grid_plan() if (rows, cols) == (4, 4) else direct_plan(rows * cols)
    in_specs = (P(RC, None, None, None), P(RC, None), P(RC))
    out_specs = P(RC, None, "depth", None)
    return jax.shard_map(
        functools.partial(per_device, plan, rows * cols),
        mesh=mesh,
        in_specs=in_specs,
        out_specs=out_specs,
        check_vma=False,
    )
```

time: 51.9 us -> 50.1 us (0.965)
  Pallas kernels: 12.5 us -> 9.53 us
  local copies, waits for them, and re-layouts: 2.6 us -> 0 us
  starting transfers between devices: 28.1 us -> 30.7 us
  waiting for transfers between devices: 6.66 us -> 7.68 us
    pallas_call x9 -> x10, Pallas kernels: 10.8 us -> 8.17 us  [the longest x6 4.42 us: more(): pl.pallas_call(functools.partial(more_kernel, [terms[n] for n in names]),...]
    ppermute x19, starting transfers between devices: 28 us -> 30.6 us  [per_device(): buffers[o] = lax.ppermute(payload, RC, [(s, t) for s, t, _ in moves])]
    unnamed x6 -> x0, local copies, waits for them, and re-layouts: 1.91 us -> none
    ppermute x19, waiting for transfers between devices: 4.95 us -> 6.74 us  [per_device(): buffers[o] = lax.ppermute(payload, RC, [(s, t) for s, t, _ in moves])]
    ppermute x1, waiting for transfers between devices: 1.71 us -> 0.94 us  [per_device(): taken = lax.ppermute(given, 'depth', [(0, 1), (1, 0)])]
    squeeze x1 -> x0, local copies, waits for them, and re-layouts: 0.69 us -> none  [per_device(): table = jnp.asarray(table)[lax.axis_index(RC + ('depth',))]]
  transfers between devices with their start and end apart: 20 -> 20, of which waited for: 7 -> 10; matrix products, arithmetic and copies ran while one was open for 4% -> 4% of each run, Pallas kernels for 17% -> 14%
where the time goes in v5:
time: 50.1 us; the launch traced here: 49.9 us
  starting transfers between devices  30.7 us (61%)
  Pallas kernels  9.53 us (19%)
  waiting for transfers between devices  7.68 us (15%)
  other arithmetic  1.85 us (4%)
    ppermute x19, starting transfers between devices, per_device(): buffers[o] = lax.ppermute(payload, RC, [(s, t) for s, t, _ in moves])  30.6 us
    ppermute x19, waiting for transfers between devices, per_device(): buffers[o] = lax.ppermute(payload, RC, [(s, t) for s, t, _ in moves])  6.74 us
    pallas_call x6, Pallas kernels, more(): pl.pallas_call(functools.partial(more_kernel, [terms[n] for n in names]),...  4.42 us
    pallas_call x1, Pallas kernels, start(): pl.pallas_call(functools.partial(first_kernel, [terms['n0'], terms['n1']]...  1.84 us
    pallas_call x2, Pallas kernels, per_device(): pl.pallas_call(functools.partial(place_kernel, partner), out_shape=jax.Sh...  1.52 us
    pallas_call x1, Pallas kernels, per_device(): pl.pallas_call(functools.partial(units_kernel, min(packed, default=chips)...  1.36 us
  transfers between devices with their start and end apart: 20, of which 10 were waited for; matrix products, arithmetic and copies ran while one was open for 4% of the time, Pallas kernels for 14%

profile of v5, /device:TPU:0, one launch (start us, length us, event | category | flops | bytes accessed | tf_op | source)
XLA Modules:
  0.0 49.9 jit_solution(6887017659384315073)
XLA Ops:
  0.0 1.4 %units.1 = (bf16[128,1024]{1,0:T(8,128)(2,1)S(1)}, bf16[128,1024]{1,0:T(8,128)(2,1)S(1)}, f32[38,1024]{1,0:T(8,128)S(1)}) custom-call(s32[2,16]{1,0:T(2,128)} %fill_hbm.3, bf16[2,16,128,128]{3,2,1,0:T(8,128)(2,1)} %band_hbm.3), custom_call_target="tpu_custom_call" | custom-call | tf_op jit(solution)/shard_map/units/pallas_call | solution.py:322
  1.4 3.1 %collective-permute-start = (bf16[128,1024]{1,0:T(8,128)(2,1)S(1)}, bf16[128,1024]{1,0:T(8,128)(2,1)S(1)}, u32[]{:S(2)}, u32[]{:S(2)}) collective-permute-start(bf16[128,1024]{1,0:T(8,128)(2,1)S(1)} %broadcast_select_fusion.8), channel_id=1, source_target_pairs={{0,2},{2,0},{4,6},{6,4},{8,10},{10,8},{12,14},{14,12},{16,18},{18,... | collective-permute-start | bytes 786440 | tf_op jit(solution)/shard_map/ppermute | solution.py:388
  4.6 1.6 %collective-permute-start.1 = (bf16[128,1024]{1,0:T(8,128)(2,1)S(1)}, bf16[128,1024]{1,0:T(8,128)(2,1)S(1)}, u32[]{:S(2)}, u32[]{:S(2)}) collective-permute-start(bf16[128,1024]{1,0:T(8,128)(2,1)S(1)} %broadcast_select_fusion.7), channel_id=1, source_target_pairs={{0,8},{2,10},{4,12},{6,14},{8,0},{10,2},{12,4},{14,6},{16,24},{18,... | collective-permute-start | bytes 786440 | tf_op jit(solution)/shard_map/ppermute | solution.py:388
  6.2 1.6 %collective-permute-start.2 = (bf16[128,1024]{1,0:T(8,128)(2,1)S(1)}, bf16[128,1024]{1,0:T(8,128)(2,1)S(1)}, u32[]{:S(2)}, u32[]{:S(2)}) collective-permute-start(bf16[128,1024]{1,0:T(8,128)(2,1)S(1)} %broadcast_select_fusion.6), channel_id=1, source_target_pairs={{0,16},{2,18},{4,20},{6,22},{8,24},{10,12},{12,10},{14,30},{16,0},... | collective-permute-start | bytes 786440 | tf_op jit(solution)/shard_map/ppermute | solution.py:388
  8.4 1.8 %first.1 = (bf16[18,256,128]{2,1,0:T(8,128)(2,1)S(1)}, f32[2,12,128]{2,1,0:T(8,128)S(1)}, f32[1,1024]{1,0:T(1,128)S(1)}, f32[17,256,128]{2,1,0:T(8,128)S(1)}) custom-call(s32[2]{0:T(128)} %reach_hbm.1, s32[2,16]{1,0:T(2,128)} %fill_hbm.3, bf16[2,16,128,128]{3,2,1,0:T(8,128)(2,1)} %band_hbm.3, bf16[128,1024]{1,0:T(8,128)(2,1)S(1)} %get-tuple-element.24.refs_0_, ...), custom_call_target="tpu_custom_call" | custom-call | tf_op jit(solution)/shard_map/first/pallas_call | solution.py:340
  10.3 1.4 %collective-permute-done.refs_0_ = bf16[128,1024]{1,0:T(8,128)(2,1)S(1)} collective-permute-done((bf16[128,1024]{1,0:T(8,128)(2,1)S(1)}, bf16[128,1024]{1,0:T(8,128)(2,1)S(1)}, u32[]{:S(2)}, u32[]{:S(2)}) %collective-permute-start) | collective-permute-done | bytes 262176 | tf_op jit(solution)/shard_map/ppermute | solution.py:388
  11.7 2.0 %collective-permute-start.4 = (bf16[128,1024]{1,0:T(8,128)(2,1)S(1)}, bf16[128,1024]{1,0:T(8,128)(2,1)S(1)}, u32[]{:S(2)}, u32[]{:S(2)}) collective-permute-start(bf16[128,1024]{1,0:T(8,128)(2,1)S(1)} %select_select_fusion.9), channel_id=1, source_target_pairs={{0,8},{2,10},{4,12},{6,14},{8,0},{10,2},{12,4},{14,6},{16,24},{18,... | collective-permute-start | bytes 786440 | tf_op jit(solution)/shard_map/ppermute | solution.py:388
  13.8 1.6 %collective-permute-start.5 = (bf16[128,1024]{1,0:T(8,128)(2,1)S(1)}, bf16[128,1024]{1,0:T(8,128)(2,1)S(1)}, u32[]{:S(2)}, u32[]{:S(2)}) collective-permute-start(bf16[128,1024]{1,0:T(8,128)(2,1)S(1)} %broadcast_select_fusion.4), channel_id=1, source_target_pairs={{0,16},{2,4},{4,2},{6,22},{8,24},{10,12},{12,10},{14,30},{16,0},{1... | collective-permute-start | bytes 786440 | tf_op jit(solution)/shard_map/ppermute | solution.py:388
  15.5 1.7 %collective-permute-start.6 = (bf16[128,1024]{1,0:T(8,128)(2,1)S(1)}, bf16[128,1024]{1,0:T(8,128)(2,1)S(1)}, u32[]{:S(2)}, u32[]{:S(2)}) collective-permute-start(bf16[128,1024]{1,0:T(8,128)(2,1)S(1)} %broadcast_select_fusion.3), channel_id=1, source_target_pairs={{0,2},{2,0},{4,6},{6,4},{8,10},{10,8},{12,14},{14,12},{16,18},{18,... | collective-permute-start | bytes 786440 | tf_op jit(solution)/shard_map/ppermute | solution.py:388
  17.4 2.0 %collective-permute-start.7 = (bf16[128,1024]{1,0:T(8,128)(2,1)S(1)}, bf16[128,1024]{1,0:T(8,128)(2,1)S(1)}, u32[]{:S(2)}, u32[]{:S(2)}) collective-permute-start(bf16[128,1024]{1,0:T(8,128)(2,1)S(1)} %select_select_fusion.8), channel_id=1, source_target_pairs={{0,8},{2,10},{4,12},{6,14},{8,0},{10,2},{12,4},{14,6},{16,24},{18,... | collective-permute-start | bytes 786440 | tf_op jit(solution)/shard_map/ppermute | solution.py:388
  19.6 1.6 %collective-permute-start.8 = (bf16[128,1024]{1,0:T(8,128)(2,1)S(1)}, bf16[128,1024]{1,0:T(8,128)(2,1)S(1)}, u32[]{:S(2)}, u32[]{:S(2)}) collective-permute-start(bf16[128,1024]{1,0:T(8,128)(2,1)S(1)} %select_select_fusion.7.after_ref), channel_id=1, source_target_pairs={{0,16},{2,4},{4,2},{6,22},{8,24},{10,12},{12,10},{14,30},{16,0},{1... | collective-permute-start | bytes 786440 | tf_op jit(solution)/shard_map/ppermute | solution.py:388
  21.1 0.8 %more.6 = (f32[1,1024]{1,0:T(1,128)S(1)}, f32[17,256,128]{2,1,0:T(8,128)S(1)}) custom-call(bf16[18,256,128]{2,1,0:T(8,128)(2,1)S(1)} %get-tuple-element.26.left_ref, bf16[128,1024]{1,0:T(8,128)(2,1)S(1)} %select_select_fusion.7.after_ref, bf16[128,1024]{1,0:T(8,128)(2,1)S(1)} %collective-permute-done.refs_0_, ...), custom_call_target="tpu_custom_call", output_to_operand_aliasing={{1}: (7, {})} | custom-call | tf_op jit(solution)/shard_map/more/pallas_call | solution.py:362
  22.1 1.7 %collective-permute-start.9 = (bf16[128,1024]{1,0:T(8,128)(2,1)S(1)}, bf16[128,1024]{1,0:T(8,128)(2,1)S(1)}, u32[]{:S(2)}, u32[]{:S(2)}) collective-permute-start(bf16[128,1024]{1,0:T(8,128)(2,1)S(1)} %broadcast_select_fusion.2), channel_id=1, source_target_pairs={{0,2},{2,0},{4,6},{6,4},{8,10},{10,8},{12,14},{14,12},{16,18},{18,... | collective-permute-start | bytes 786440 | tf_op jit(solution)/shard_map/ppermute | solution.py:388
  23.9 1.1 %collective-permute-start.10 = (bf16[128,1024]{1,0:T(8,128)(2,1)S(1)}, bf16[128,1024]{1,0:T(8,128)(2,1)S(1)}, u32[]{:S(2)}, u32[]{:S(2)}) collective-permute-start(bf16[128,1024]{1,0:T(8,128)(2,1)S(1)} %select_select_fusion.6), channel_id=1, source_target_pairs={{0,8},{2,10},{4,12},{6,14},{8,0},{10,2},{12,4},{14,6},{16,24},{18,... | collective-permute-start | bytes 786440 | tf_op jit(solution)/shard_map/ppermute | solution.py:388
  25.2 1.7 %collective-permute-start.11 = (bf16[128,1024]{1,0:T(8,128)(2,1)S(1)}, bf16[128,1024]{1,0:T(8,128)(2,1)S(1)}, u32[]{:S(2)}, u32[]{:S(2)}) collective-permute-start(bf16[128,1024]{1,0:T(8,128)(2,1)S(1)} %select_select_fusion.5.after_ref), channel_id=1, source_target_pairs={{0,16},{2,4},{4,2},{6,22},{8,24},{10,12},{12,10},{14,30},{16,0},{1... | collective-permute-start | bytes 786440 | tf_op jit(solution)/shard_map/ppermute | solution.py:388
  27.5 1.6 %collective-permute-start.12 = (bf16[128,1024]{1,0:T(8,128)(2,1)S(1)}, bf16[128,1024]{1,0:T(8,128)(2,1)S(1)}, u32[]{:S(2)}, u32[]{:S(2)}) collective-permute-start(bf16[128,1024]{1,0:T(8,128)(2,1)S(1)} %select_select_fusion.4), channel_id=1, source_target_pairs={{0,2},{2,0},{4,6},{6,4},{8,10},{10,8},{12,14},{14,12},{16,18},{18,... | collective-permute-start | bytes 786440 | tf_op jit(solution)/shard_map/ppermute | solution.py:388
  29.7 1.3 %collective-permute-start.13 = (bf16[128,1024]{1,0:T(8,128)(2,1)S(1)}, bf16[128,1024]{1,0:T(8,128)(2,1)S(1)}, u32[]{:S(2)}, u32[]{:S(2)}) collective-permute-start(bf16[128,1024]{1,0:T(8,128)(2,1)S(1)} %select_select_fusion.3), channel_id=1, source_target_pairs={{0,8},{2,10},{4,12},{6,14},{8,0},{10,2},{12,4},{14,6},{16,24},{18,... | collective-permute-start | bytes 786440 | tf_op jit(solution)/shard_map/ppermute | solution.py:388
  31.1 0.6 %collective-permute-done.10.refs_2_ = bf16[128,1024]{1,0:T(8,128)(2,1)S(1)} collective-permute-done((bf16[128,1024]{1,0:T(8,128)(2,1)S(1)}, bf16[128,1024]{1,0:T(8,128)(2,1)S(1)}, u32[]{:S(2)}, u32[]{:S(2)}) %collective-permute-start.10) | collective-permute-done | bytes 262176 | tf_op jit(solution)/shard_map/ppermute | solution.py:388
  31.8 1.6 %collective-permute-start.14 = (bf16[128,1024]{1,0:T(8,128)(2,1)S(1)}, bf16[128,1024]{1,0:T(8,128)(2,1)S(1)}, u32[]{:S(2)}, u32[]{:S(2)}) collective-permute-start(bf16[128,1024]{1,0:T(8,128)(2,1)S(1)} %select_select_fusion.2.after_ref), channel_id=1, source_target_pairs={{0,16},{2,4},{4,2},{6,22},{8,24},{10,12},{12,10},{14,30},{16,0},{1... | collective-permute-start | bytes 786440 | tf_op jit(solution)/shard_map/ppermute | solution.py:388
  34.1 1.6 %collective-permute-start.17 = (bf16[128,1024]{1,0:T(8,128)(2,1)S(1)}, bf16[128,1024]{1,0:T(8,128)(2,1)S(1)}, u32[]{:S(2)}, u32[]{:S(2)}) collective-permute-start(bf16[128,1024]{1,0:T(8,128)(2,1)S(1)} %select_select_fusion.1), channel_id=1, source_target_pairs={{0,2},{2,0},{4,6},{6,4},{8,10},{10,8},{12,14},{14,12},{16,18},{18,... | collective-permute-start | bytes 786440 | tf_op jit(solution)/shard_map/ppermute | solution.py:388
  35.7 0.6 %collective-permute-done.12.refs_1_ = bf16[128,1024]{1,0:T(8,128)(2,1)S(1)} collective-permute-done((bf16[128,1024]{1,0:T(8,128)(2,1)S(1)}, bf16[128,1024]{1,0:T(8,128)(2,1)S(1)}, u32[]{:S(2)}, u32[]{:S(2)}) %collective-permute-start.12) | collective-permute-done | bytes 262176 | tf_op jit(solution)/shard_map/ppermute | solution.py:388
  36.4 0.9 %collective-permute-start.18 = (bf16[128,1024]{1,0:T(8,128)(2,1)S(1)}, bf16[128,1024]{1,0:T(8,128)(2,1)S(1)}, u32[]{:S(2)}, u32[]{:S(2)}) collective-permute-start(bf16[128,1024]{1,0:T(8,128)(2,1)S(1)} %broadcast_select_fusion.1), channel_id=1, source_target_pairs={{0,8},{2,10},{4,12},{6,14},{8,0},{10,2},{12,4},{14,6},{16,24},{18,... | collective-permute-start | bytes 786440 | tf_op jit(solution)/shard_map/ppermute | solution.py:388
  37.3 0.9 %collective-permute-done.13.refs_2_ = bf16[128,1024]{1,0:T(8,128)(2,1)S(1)} collective-permute-done((bf16[128,1024]{1,0:T(8,128)(2,1)S(1)}, bf16[128,1024]{1,0:T(8,128)(2,1)S(1)}, u32[]{:S(2)}, u32[]{:S(2)}) %collective-permute-start.13) | collective-permute-done | bytes 262176 | tf_op jit(solution)/shard_map/ppermute | solution.py:388
  38.2 1.5 %collective-permute-start.16 = (bf16[128,1024]{1,0:T(8,128)(2,1)S(1)}, bf16[128,1024]{1,0:T(8,128)(2,1)S(1)}, u32[]{:S(2)}, u32[]{:S(2)}) collective-permute-start(bf16[128,1024]{1,0:T(8,128)(2,1)S(1)} %select_select_fusion.after_ref), channel_id=1, source_target_pairs={{0,16},{2,4},{4,2},{6,22},{8,24},{10,26},{12,28},{14,30},{16,0},{1... | collective-permute-start | bytes 786440 | tf_op jit(solution)/shard_map/ppermute | solution.py:388
  40.6 2.0 %collective-permute-start.15 = (bf16[128,1024]{1,0:T(8,128)(2,1)S(1)}, bf16[128,1024]{1,0:T(8,128)(2,1)S(1)}, u32[]{:S(2)}, u32[]{:S(2)}) collective-permute-start(bf16[128,1024]{1,0:T(8,128)(2,1)S(1)} %broadcast_select_fusion), channel_id=1, source_target_pairs={{0,2},{2,0},{4,6},{6,4},{8,10},{10,8},{12,14},{14,12},{16,18},{18,... | collective-permute-start | bytes 786440 | tf_op jit(solution)/shard_map/ppermute | solution.py:388
  43.0 1.1 %more.10 = (f32[1,1024]{1,0:T(1,128)}, f32[17,256,128]{2,1,0:T(8,128)S(1)}) custom-call(bf16[18,256,128]{2,1,0:T(8,128)(2,1)S(1)} %get-tuple-element.26.left_ref, bf16[128,1024]{1,0:T(8,128)(2,1)S(1)} %collective-permute-done.14.after_ref.refs_0_, bf16[128,1024]{1,0:T(8,128)(2,1)S(1)} %collective-permute-done.14.after_ref.refs_0_, ...), custom_call_target="tpu_custom_call", output_to_operand_aliasing={{1}: (5, {})} | custom-call | tf_op jit(solution)/shard_map/more/pallas_call | solution.py:362
  44.1 0.6 %collective-permute-done.16.after_ref.refs_0_ = bf16[128,1024]{1,0:T(8,128)(2,1)S(1)} collective-permute-done((bf16[128,1024]{1,0:T(8,128)(2,1)S(1)}, bf16[128,1024]{1,0:T(8,128)(2,1)S(1)}, u32[]{:S(2)}, u32[]{:S(2)}) %collective-permute-start.16) | collective-permute-done | bytes 262176 | tf_op jit(solution)/shard_map/ppermute | solution.py:388
  44.6 0.8 %more.11 = (f32[1,1024]{1,0:T(1,128)}, f32[17,256,128]{2,1,0:T(8,128)S(1)}) custom-call(bf16[18,256,128]{2,1,0:T(8,128)(2,1)S(1)} %get-tuple-element.26.left_ref, bf16[128,1024]{1,0:T(8,128)(2,1)S(1)} %collective-permute-done.16.after_ref.refs_0_, bf16[128,1024]{1,0:T(8,128)(2,1)S(1)} %collective-permute-done.16.after_ref.refs_0_, ...), custom_call_target="tpu_custom_call", output_to_operand_aliasing={{1}: (3, {})} | custom-call | tf_op jit(solution)/shard_map/more/pallas_call | solution.py:362
  45.4 1.5 %collective-permute-done.15.refs_0_ = bf16[128,1024]{1,0:T(8,128)(2,1)S(1)} collective-permute-done((bf16[128,1024]{1,0:T(8,128)(2,1)S(1)}, bf16[128,1024]{1,0:T(8,128)(2,1)S(1)}, u32[]{:S(2)}, u32[]{:S(2)}) %collective-permute-start.15) | collective-permute-done | bytes 262176 | tf_op jit(solution)/shard_map/ppermute | solution.py:388
  47.5 0.8 %place.2.refs_0_ = bf16[2,12,2,64,128]{4,3,2,1,0:T(8,128)(2,1)} custom-call(bf16[2,12,64,128]{3,2,1,0:T(8,128)(2,1)S(1)} %get-tuple-element.42.tiles), custom_call_target="tpu_custom_call" | custom-call | tf_op jit(solution)/shard_map/place/pallas_call | solution.py:410
  48.2 0.9 %collective-permute-done.19.tiles = bf16[2,12,64,128]{3,2,1,0:T(8,128)(2,1)S(1)} collective-permute-done((bf16[2,12,64,128]{3,2,1,0:T(8,128)(2,1)S(1)}, bf16[2,12,64,128]{3,2,1,0:T(8,128)(2,1)S(1)}, u32[]{:S(2)}, u32[]{:S(2)}) %collective-permute-start.19) | collective-permute-done | bytes 393248 | tf_op jit(solution)/shard_map/ppermute | solution.py:407
  49.2 0.8 %place.3 = bf16[2,12,2,64,128]{4,3,2,1,0:T(8,128)(2,1)} custom-call(bf16[2,12,64,128]{3,2,1,0:T(8,128)(2,1)S(1)} %collective-permute-done.19.tiles, bf16[2,12,2,64,128]{4,3,2,1,0:T(8,128)(2,1)} %place.2.refs_0_), custom_call_target="tpu_custom_call", output_to_operand_aliasing={{}: (1, {})} | custom-call | tf_op jit(solution)/shard_map/place/pallas_call | solution.py:410
  (57 shorter events, 5.7 us)
Async XLA Ops:
  1.4 10.2 %collective-permute-start = (bf16[128,1024]{1,0:T(8,128)(2,1)S(1)}, bf16[128,1024]{1,0:T(8,128)(2,1)S(1)}, u32[]{:S(2)}, u32[]{:S(2)}) collective-permute-start(bf16[128,1024]{1,0:T(8,128)(2,1)S(1)} %broadcast_select_fusion.8), channel_id=1, source_target_pairs={{0,2},{2,0},{4,6},{6,4},{8,10},{10,8},{12,14},{14,12},{16,18},{18,... | collective-permute-start | bytes 786440 | tf_op jit(solution)/shard_map/ppermute | solution.py:388
  4.6 9.2 %collective-permute-start.1 = (bf16[128,1024]{1,0:T(8,128)(2,1)S(1)}, bf16[128,1024]{1,0:T(8,128)(2,1)S(1)}, u32[]{:S(2)}, u32[]{:S(2)}) collective-permute-start(bf16[128,1024]{1,0:T(8,128)(2,1)S(1)} %broadcast_select_fusion.7), channel_id=1, source_target_pairs={{0,8},{2,10},{4,12},{6,14},{8,0},{10,2},{12,4},{14,6},{16,24},{18,... | collective-permute-start | bytes 786440 | tf_op jit(solution)/shard_map/ppermute | solution.py:388
  6.2 9.2 %collective-permute-start.2 = (bf16[128,1024]{1,0:T(8,128)(2,1)S(1)}, bf16[128,1024]{1,0:T(8,128)(2,1)S(1)}, u32[]{:S(2)}, u32[]{:S(2)}) collective-permute-start(bf16[128,1024]{1,0:T(8,128)(2,1)S(1)} %broadcast_select_fusion.6), channel_id=1, source_target_pairs={{0,16},{2,18},{4,20},{6,22},{8,24},{10,12},{12,10},{14,30},{16,0},... | collective-permute-start | bytes 786440 | tf_op jit(solution)/shard_map/ppermute | solution.py:388
  7.9 9.4 %collective-permute-start.3 = (bf16[128,1024]{1,0:T(8,128)(2,1)S(1)}, bf16[128,1024]{1,0:T(8,128)(2,1)S(1)}, u32[]{:S(2)}, u32[]{:S(2)}) collective-permute-start(bf16[128,1024]{1,0:T(8,128)(2,1)S(1)} %broadcast_select_fusion.5), channel_id=1, source_target_pairs={{0,2},{2,0},{4,6},{6,4},{8,10},{10,8},{12,14},{14,12},{16,18},{18,... | collective-permute-start | bytes 786440 | tf_op jit(solution)/shard_map/ppermute | solution.py:388
  11.7 7.8 %collective-permute-start.4 = (bf16[128,1024]{1,0:T(8,128)(2,1)S(1)}, bf16[128,1024]{1,0:T(8,128)(2,1)S(1)}, u32[]{:S(2)}, u32[]{:S(2)}) collective-permute-start(bf16[128,1024]{1,0:T(8,128)(2,1)S(1)} %select_select_fusion.9), channel_id=1, source_target_pairs={{0,8},{2,10},{4,12},{6,14},{8,0},{10,2},{12,4},{14,6},{16,24},{18,... | collective-permute-start | bytes 786440 | tf_op jit(solution)/shard_map/ppermute | solution.py:388
  13.8 8.2 %collective-permute-start.5 = (bf16[128,1024]{1,0:T(8,128)(2,1)S(1)}, bf16[128,1024]{1,0:T(8,128)(2,1)S(1)}, u32[]{:S(2)}, u32[]{:S(2)}) collective-permute-start(bf16[128,1024]{1,0:T(8,128)(2,1)S(1)} %broadcast_select_fusion.4), channel_id=1, source_target_pairs={{0,16},{2,4},{4,2},{6,22},{8,24},{10,12},{12,10},{14,30},{16,0},{1... | collective-permute-start | bytes 786440 | tf_op jit(solution)/shard_map/ppermute | solution.py:388
  15.5 8.4 %collective-permute-start.6 = (bf16[128,1024]{1,0:T(8,128)(2,1)S(1)}, bf16[128,1024]{1,0:T(8,128)(2,1)S(1)}, u32[]{:S(2)}, u32[]{:S(2)}) collective-permute-start(bf16[128,1024]{1,0:T(8,128)(2,1)S(1)} %broadcast_select_fusion.3), channel_id=1, source_target_pairs={{0,2},{2,0},{4,6},{6,4},{8,10},{10,8},{12,14},{14,12},{16,18},{18,... | collective-permute-start | bytes 786440 | tf_op jit(solution)/shard_map/ppermute | solution.py:388
  17.4 7.7 %collective-permute-start.7 = (bf16[128,1024]{1,0:T(8,128)(2,1)S(1)}, bf16[128,1024]{1,0:T(8,128)(2,1)S(1)}, u32[]{:S(2)}, u32[]{:S(2)}) collective-permute-start(bf16[128,1024]{1,0:T(8,128)(2,1)S(1)} %select_select_fusion.8), channel_id=1, source_target_pairs={{0,8},{2,10},{4,12},{6,14},{8,0},{10,2},{12,4},{14,6},{16,24},{18,... | collective-permute-start | bytes 786440 | tf_op jit(solution)/shard_map/ppermute | solution.py:388
  19.6 7.9 %collective-permute-start.8 = (bf16[128,1024]{1,0:T(8,128)(2,1)S(1)}, bf16[128,1024]{1,0:T(8,128)(2,1)S(1)}, u32[]{:S(2)}, u32[]{:S(2)}) collective-permute-start(bf16[128,1024]{1,0:T(8,128)(2,1)S(1)} %select_select_fusion.7.after_ref), channel_id=1, source_target_pairs={{0,16},{2,4},{4,2},{6,22},{8,24},{10,12},{12,10},{14,30},{16,0},{1... | collective-permute-start | bytes 786440 | tf_op jit(solution)/shard_map/ppermute | solution.py:388
  22.1 7.6 %collective-permute-start.9 = (bf16[128,1024]{1,0:T(8,128)(2,1)S(1)}, bf16[128,1024]{1,0:T(8,128)(2,1)S(1)}, u32[]{:S(2)}, u32[]{:S(2)}) collective-permute-start(bf16[128,1024]{1,0:T(8,128)(2,1)S(1)} %broadcast_select_fusion.2), channel_id=1, source_target_pairs={{0,2},{2,0},{4,6},{6,4},{8,10},{10,8},{12,14},{14,12},{16,18},{18,... | collective-permute-start | bytes 786440 | tf_op jit(solution)/shard_map/ppermute | solution.py:388
  23.9 7.8 %collective-permute-start.10 = (bf16[128,1024]{1,0:T(8,128)(2,1)S(1)}, bf16[128,1024]{1,0:T(8,128)(2,1)S(1)}, u32[]{:S(2)}, u32[]{:S(2)}) collective-permute-start(bf16[128,1024]{1,0:T(8,128)(2,1)S(1)} %select_select_fusion.6), channel_id=1, source_target_pairs={{0,8},{2,10},{4,12},{6,14},{8,0},{10,2},{12,4},{14,6},{16,24},{18,... | collective-permute-start | bytes 786440 | tf_op jit(solution)/shard_map/ppermute | solution.py:388
  25.2 8.8 %collective-permute-start.11 = (bf16[128,1024]{1,0:T(8,128)(2,1)S(1)}, bf16[128,1024]{1,0:T(8,128)(2,1)S(1)}, u32[]{:S(2)}, u32[]{:S(2)}) collective-permute-start(bf16[128,1024]{1,0:T(8,128)(2,1)S(1)} %select_select_fusion.5.after_ref), channel_id=1, source_target_pairs={{0,16},{2,4},{4,2},{6,22},{8,24},{10,12},{12,10},{14,30},{16,0},{1... | collective-permute-start | bytes 786440 | tf_op jit(solution)/shard_map/ppermute | solution.py:388
  27.5 8.8 %collective-permute-start.12 = (bf16[128,1024]{1,0:T(8,128)(2,1)S(1)}, bf16[128,1024]{1,0:T(8,128)(2,1)S(1)}, u32[]{:S(2)}, u32[]{:S(2)}) collective-permute-start(bf16[128,1024]{1,0:T(8,128)(2,1)S(1)} %select_select_fusion.4), channel_id=1, source_target_pairs={{0,2},{2,0},{4,6},{6,4},{8,10},{10,8},{12,14},{14,12},{16,18},{18,... | collective-permute-start | bytes 786440 | tf_op jit(solution)/shard_map/ppermute | solution.py:388
  29.7 8.4 %collective-permute-start.13 = (bf16[128,1024]{1,0:T(8,128)(2,1)S(1)}, bf16[128,1024]{1,0:T(8,128)(2,1)S(1)}, u32[]{:S(2)}, u32[]{:S(2)}) collective-permute-start(bf16[128,1024]{1,0:T(8,128)(2,1)S(1)} %select_select_fusion.3), channel_id=1, source_target_pairs={{0,8},{2,10},{4,12},{6,14},{8,0},{10,2},{12,4},{14,6},{16,24},{18,... | collective-permute-start | bytes 786440 | tf_op jit(solution)/shard_map/ppermute | solution.py:388
  31.8 8.7 %collective-permute-start.14 = (bf16[128,1024]{1,0:T(8,128)(2,1)S(1)}, bf16[128,1024]{1,0:T(8,128)(2,1)S(1)}, u32[]{:S(2)}, u32[]{:S(2)}) collective-permute-start(bf16[128,1024]{1,0:T(8,128)(2,1)S(1)} %select_select_fusion.2.after_ref), channel_id=1, source_target_pairs={{0,16},{2,4},{4,2},{6,22},{8,24},{10,12},{12,10},{14,30},{16,0},{1... | collective-permute-start | bytes 786440 | tf_op jit(solution)/shard_map/ppermute | solution.py:388
  34.1 8.9 %collective-permute-start.17 = (bf16[128,1024]{1,0:T(8,128)(2,1)S(1)}, bf16[128,1024]{1,0:T(8,128)(2,1)S(1)}, u32[]{:S(2)}, u32[]{:S(2)}) collective-permute-start(bf16[128,1024]{1,0:T(8,128)(2,1)S(1)} %select_select_fusion.1), channel_id=1, source_target_pairs={{0,2},{2,0},{4,6},{6,4},{8,10},{10,8},{12,14},{14,12},{16,18},{18,... | collective-permute-start | bytes 786440 | tf_op jit(solution)/shard_map/ppermute | solution.py:388
  36.4 6.6 %collective-permute-start.18 = (bf16[128,1024]{1,0:T(8,128)(2,1)S(1)}, bf16[128,1024]{1,0:T(8,128)(2,1)S(1)}, u32[]{:S(2)}, u32[]{:S(2)}) collective-permute-start(bf16[128,1024]{1,0:T(8,128)(2,1)S(1)} %broadcast_select_fusion.1), channel_id=1, source_target_pairs={{0,8},{2,10},{4,12},{6,14},{8,0},{10,2},{12,4},{14,6},{16,24},{18,... | collective-permute-start | bytes 786440 | tf_op jit(solution)/shard_map/ppermute | solution.py:388
  38.2 6.4 %collective-permute-start.16 = (bf16[128,1024]{1,0:T(8,128)(2,1)S(1)}, bf16[128,1024]{1,0:T(8,128)(2,1)S(1)}, u32[]{:S(2)}, u32[]{:S(2)}) collective-permute-start(bf16[128,1024]{1,0:T(8,128)(2,1)S(1)} %select_select_fusion.after_ref), channel_id=1, source_target_pairs={{0,16},{2,4},{4,2},{6,22},{8,24},{10,26},{12,28},{14,30},{16,0},{1... | collective-permute-start | bytes 786440 | tf_op jit(solution)/shard_map/ppermute | solution.py:388
  40.6 6.4 %collective-permute-start.15 = (bf16[128,1024]{1,0:T(8,128)(2,1)S(1)}, bf16[128,1024]{1,0:T(8,128)(2,1)S(1)}, u32[]{:S(2)}, u32[]{:S(2)}) collective-permute-start(bf16[128,1024]{1,0:T(8,128)(2,1)S(1)} %broadcast_select_fusion), channel_id=1, source_target_pairs={{0,2},{2,0},{4,6},{6,4},{8,10},{10,8},{12,14},{14,12},{16,18},{18,... | collective-permute-start | bytes 786440 | tf_op jit(solution)/shard_map/ppermute | solution.py:388
  47.4 1.8 %collective-permute-start.19 = (bf16[2,12,64,128]{3,2,1,0:T(8,128)(2,1)S(1)}, bf16[2,12,64,128]{3,2,1,0:T(8,128)(2,1)S(1)}, u32[]{:S(2)}, u32[]{:S(2)}) collective-permute-start(bf16[2,12,64,128]{3,2,1,0:T(8,128)(2,1)S(1)} %get-tuple-element.41), channel_id=1, source_target_pairs={{0,1},{1,0},{2,3},{3,2},{4,5},{5,4},{6,7},{7,6},{8,9},{9,8},{10,11... | collective-permute-start | bytes 1179656 | tf_op jit(solution)/shard_map/ppermute | solution.py:407

commit v6 on v5

--- a/solution.py
+++ b/solution.py
@@ -154,7 +154,7 @@
 VMEM_LIMIT = 12 * 2**20
 FIRST = 4
 LAG = 4
-ADD_AT = (9, 12, 15, 18)
+ADD_AT = (9, 12, 16)
 LAST = (2, 1)
 
 
@@ -236,8 +236,9 @@
 
 
 def more_kernel(terms, left_ref, after_ref, *refs):
-    units, (token, sums) = refs[:-3], refs[-2:]
-    token[...] = jnp.zeros(token.shape, token.dtype)
+    units, sums = refs[: len(terms)], refs[-1]
+    for token in refs[len(terms) + 1 : -1]:
+        token[...] = jnp.zeros(token.shape, token.dtype)
     add_terms(terms, left_ref, units, sums)
 
 
@@ -357,14 +358,14 @@
             name="first",
         )(reach, fill, band, n0, n1)
 
-    def more(after, sums, names):
+    def more(after, sums, names, tokens=1):
         units = [buffers[n] for n in names]
         return pl.pallas_call(
             functools.partial(more_kernel, [terms[n] for n in names]),
-            out_shape=(token_shape, sums_shape),
+            out_shape=(token_shape,) * tokens + (sums_shape,),
             in_specs=[VMEM] * (3 + len(units)),
-            out_specs=(VMEM, VMEM),
-            input_output_aliases={2 + len(units): 1},
+            out_specs=(VMEM,) * (tokens + 1),
+            input_output_aliases={2 + len(units): tokens},
             compiler_params=params,
             name="more",
         )(left, after, *units, sums)
@@ -389,7 +390,7 @@
     if sums is None:
         left, keep, _, sums = start()
     for count in LAST:
-        _, sums = more(buffers[added], sums, range(added, len(ops) - count))
+        (sums,) = more(buffers[added], sums, range(added, len(ops) - count), tokens=0)
         added = len(ops) - count
 
     piece = jax.ShapeDtypeStruct((2, OUT_BAND // 2, TILE // 2, TILE), jnp.bfloat16)

time: 50.1 us -> 50.1 us (level)
  waiting for transfers between devices: 7.68 us -> 9.1 us
  Pallas kernels: 9.53 us -> 8.32 us
    ppermute x19, waiting for transfers between devices: 6.74 us -> 8.17 us  [per_device(): buffers[o] = lax.ppermute(payload, RC, [(s, t) for s, t, _ in moves])]
    pallas_call x6 -> x5, Pallas kernels: 4.42 us -> 3.21 us  [more(): pl.pallas_call(functools.partial(more_kernel, [terms[n] for n in names]),...]
  transfers between devices with their start and end apart: 20 -> 20, of which waited for: 10 -> 11; matrix products, arithmetic and copies ran while one was open for 4% -> 4% of each run, Pallas kernels for 14% -> 12%
where the time goes in v6:
time: 50.1 us; the launch traced here: 49.9 us
  starting transfers between devices  30.5 us (61%)
  waiting for transfers between devices  9.1 us (18%)
  Pallas kernels  8.32 us (17%)
  other arithmetic  1.85 us (4%)
    ppermute x19, starting transfers between devices, per_device(): buffers[o] = lax.ppermute(payload, RC, [(s, t) for s, t, _ in moves])  30.4 us
    ppermute x19, waiting for transfers between devices, per_device(): buffers[o] = lax.ppermute(payload, RC, [(s, t) for s, t, _ in moves])  8.17 us
    pallas_call x5, Pallas kernels, more(): pl.pallas_call(functools.partial(more_kernel, [terms[n] for n in names]),...  3.21 us
    pallas_call x1, Pallas kernels, start(): pl.pallas_call(functools.partial(first_kernel, [terms['n0'], terms['n1']]...  1.84 us
    pallas_call x2, Pallas kernels, per_device(): pl.pallas_call(functools.partial(place_kernel, partner), out_shape=jax.Sh...  1.52 us
    pallas_call x1, Pallas kernels, per_device(): pl.pallas_call(functools.partial(units_kernel, min(packed, default=chips)...  1.36 us
  transfers between devices with their start and end apart: 20, of which 11 were waited for; matrix products, arithmetic and copies ran while one was open for 4% of the time, Pallas kernels for 12%

profile of v6, /device:TPU:0, one launch (start us, length us, event | category | flops | bytes accessed | tf_op | source)
XLA Modules:
  0.0 49.9 jit_solution(12915334688811788939)
XLA Ops:
  0.0 1.4 %units.1 = (bf16[128,1024]{1,0:T(8,128)(2,1)S(1)}, bf16[128,1024]{1,0:T(8,128)(2,1)S(1)}, f32[38,1024]{1,0:T(8,128)S(1)}) custom-call(s32[2,16]{1,0:T(2,128)} %fill_hbm.3, bf16[2,16,128,128]{3,2,1,0:T(8,128)(2,1)} %band_hbm.3), custom_call_target="tpu_custom_call" | custom-call | tf_op jit(solution)/shard_map/units/pallas_call | solution.py:323
  1.4 3.1 %collective-permute-start = (bf16[128,1024]{1,0:T(8,128)(2,1)S(1)}, bf16[128,1024]{1,0:T(8,128)(2,1)S(1)}, u32[]{:S(2)}, u32[]{:S(2)}) collective-permute-start(bf16[128,1024]{1,0:T(8,128)(2,1)S(1)} %broadcast_select_fusion.8), channel_id=1, source_target_pairs={{0,2},{2,0},{4,6},{6,4},{8,10},{10,8},{12,14},{14,12},{16,18},{18,... | collective-permute-start | bytes 786440 | tf_op jit(solution)/shard_map/ppermute | solution.py:389
  4.6 1.6 %collective-permute-start.1 = (bf16[128,1024]{1,0:T(8,128)(2,1)S(1)}, bf16[128,1024]{1,0:T(8,128)(2,1)S(1)}, u32[]{:S(2)}, u32[]{:S(2)}) collective-permute-start(bf16[128,1024]{1,0:T(8,128)(2,1)S(1)} %broadcast_select_fusion.7), channel_id=1, source_target_pairs={{0,8},{2,10},{4,12},{6,14},{8,0},{10,2},{12,4},{14,6},{16,24},{18,... | collective-permute-start | bytes 786440 | tf_op jit(solution)/shard_map/ppermute | solution.py:389
  6.2 1.6 %collective-permute-start.2 = (bf16[128,1024]{1,0:T(8,128)(2,1)S(1)}, bf16[128,1024]{1,0:T(8,128)(2,1)S(1)}, u32[]{:S(2)}, u32[]{:S(2)}) collective-permute-start(bf16[128,1024]{1,0:T(8,128)(2,1)S(1)} %broadcast_select_fusion.6), channel_id=1, source_target_pairs={{0,16},{2,18},{4,20},{6,22},{8,24},{10,12},{12,10},{14,30},{16,0},... | collective-permute-start | bytes 786440 | tf_op jit(solution)/shard_map/ppermute | solution.py:389
  8.4 1.8 %first.1 = (bf16[18,256,128]{2,1,0:T(8,128)(2,1)S(1)}, f32[2,12,128]{2,1,0:T(8,128)S(1)}, f32[1,1024]{1,0:T(1,128)S(1)}, f32[17,256,128]{2,1,0:T(8,128)S(1)}) custom-call(s32[2]{0:T(128)} %reach_hbm.1, s32[2,16]{1,0:T(2,128)} %fill_hbm.3, bf16[2,16,128,128]{3,2,1,0:T(8,128)(2,1)} %band_hbm.3, bf16[128,1024]{1,0:T(8,128)(2,1)S(1)} %get-tuple-element.20.refs_0_, ...), custom_call_target="tpu_custom_call" | custom-call | tf_op jit(solution)/shard_map/first/pallas_call | solution.py:341
  10.3 1.4 %collective-permute-done.refs_0_ = bf16[128,1024]{1,0:T(8,128)(2,1)S(1)} collective-permute-done((bf16[128,1024]{1,0:T(8,128)(2,1)S(1)}, bf16[128,1024]{1,0:T(8,128)(2,1)S(1)}, u32[]{:S(2)}, u32[]{:S(2)}) %collective-permute-start) | collective-permute-done | bytes 262176 | tf_op jit(solution)/shard_map/ppermute | solution.py:389
  11.7 2.0 %collective-permute-start.4 = (bf16[128,1024]{1,0:T(8,128)(2,1)S(1)}, bf16[128,1024]{1,0:T(8,128)(2,1)S(1)}, u32[]{:S(2)}, u32[]{:S(2)}) collective-permute-start(bf16[128,1024]{1,0:T(8,128)(2,1)S(1)} %select_select_fusion.9), channel_id=1, source_target_pairs={{0,8},{2,10},{4,12},{6,14},{8,0},{10,2},{12,4},{14,6},{16,24},{18,... | collective-permute-start | bytes 786440 | tf_op jit(solution)/shard_map/ppermute | solution.py:389
  13.8 1.6 %collective-permute-start.5 = (bf16[128,1024]{1,0:T(8,128)(2,1)S(1)}, bf16[128,1024]{1,0:T(8,128)(2,1)S(1)}, u32[]{:S(2)}, u32[]{:S(2)}) collective-permute-start(bf16[128,1024]{1,0:T(8,128)(2,1)S(1)} %broadcast_select_fusion.4), channel_id=1, source_target_pairs={{0,16},{2,4},{4,2},{6,22},{8,24},{10,12},{12,10},{14,30},{16,0},{1... | collective-permute-start | bytes 786440 | tf_op jit(solution)/shard_map/ppermute | solution.py:389
  15.5 1.7 %collective-permute-start.6 = (bf16[128,1024]{1,0:T(8,128)(2,1)S(1)}, bf16[128,1024]{1,0:T(8,128)(2,1)S(1)}, u32[]{:S(2)}, u32[]{:S(2)}) collective-permute-start(bf16[128,1024]{1,0:T(8,128)(2,1)S(1)} %broadcast_select_fusion.3), channel_id=1, source_target_pairs={{0,2},{2,0},{4,6},{6,4},{8,10},{10,8},{12,14},{14,12},{16,18},{18,... | collective-permute-start | bytes 786440 | tf_op jit(solution)/shard_map/ppermute | solution.py:389
  17.4 2.0 %collective-permute-start.7 = (bf16[128,1024]{1,0:T(8,128)(2,1)S(1)}, bf16[128,1024]{1,0:T(8,128)(2,1)S(1)}, u32[]{:S(2)}, u32[]{:S(2)}) collective-permute-start(bf16[128,1024]{1,0:T(8,128)(2,1)S(1)} %select_select_fusion.8), channel_id=1, source_target_pairs={{0,8},{2,10},{4,12},{6,14},{8,0},{10,2},{12,4},{14,6},{16,24},{18,... | collective-permute-start | bytes 786440 | tf_op jit(solution)/shard_map/ppermute | solution.py:389
  19.6 1.6 %collective-permute-start.8 = (bf16[128,1024]{1,0:T(8,128)(2,1)S(1)}, bf16[128,1024]{1,0:T(8,128)(2,1)S(1)}, u32[]{:S(2)}, u32[]{:S(2)}) collective-permute-start(bf16[128,1024]{1,0:T(8,128)(2,1)S(1)} %select_select_fusion.7.after_ref), channel_id=1, source_target_pairs={{0,16},{2,4},{4,2},{6,22},{8,24},{10,12},{12,10},{14,30},{16,0},{1... | collective-permute-start | bytes 786440 | tf_op jit(solution)/shard_map/ppermute | solution.py:389
  21.1 0.8 %more.5 = (f32[1,1024]{1,0:T(1,128)S(1)}, f32[17,256,128]{2,1,0:T(8,128)S(1)}) custom-call(bf16[18,256,128]{2,1,0:T(8,128)(2,1)S(1)} %get-tuple-element.22.left_ref, bf16[128,1024]{1,0:T(8,128)(2,1)S(1)} %select_select_fusion.7.after_ref, bf16[128,1024]{1,0:T(8,128)(2,1)S(1)} %collective-permute-done.refs_0_, ...), custom_call_target="tpu_custom_call", output_to_operand_aliasing={{1}: (7, {})} | custom-call | tf_op jit(solution)/shard_map/more/pallas_call | solution.py:363
  22.1 1.7 %collective-permute-start.9 = (bf16[128,1024]{1,0:T(8,128)(2,1)S(1)}, bf16[128,1024]{1,0:T(8,128)(2,1)S(1)}, u32[]{:S(2)}, u32[]{:S(2)}) collective-permute-start(bf16[128,1024]{1,0:T(8,128)(2,1)S(1)} %broadcast_select_fusion.2), channel_id=1, source_target_pairs={{0,2},{2,0},{4,6},{6,4},{8,10},{10,8},{12,14},{14,12},{16,18},{18,... | collective-permute-start | bytes 786440 | tf_op jit(solution)/shard_map/ppermute | solution.py:389
  23.9 1.1 %collective-permute-start.10 = (bf16[128,1024]{1,0:T(8,128)(2,1)S(1)}, bf16[128,1024]{1,0:T(8,128)(2,1)S(1)}, u32[]{:S(2)}, u32[]{:S(2)}) collective-permute-start(bf16[128,1024]{1,0:T(8,128)(2,1)S(1)} %select_select_fusion.6), channel_id=1, source_target_pairs={{0,8},{2,10},{4,12},{6,14},{8,0},{10,2},{12,4},{14,6},{16,24},{18,... | collective-permute-start | bytes 786440 | tf_op jit(solution)/shard_map/ppermute | solution.py:389
  25.2 1.7 %collective-permute-start.11 = (bf16[128,1024]{1,0:T(8,128)(2,1)S(1)}, bf16[128,1024]{1,0:T(8,128)(2,1)S(1)}, u32[]{:S(2)}, u32[]{:S(2)}) collective-permute-start(bf16[128,1024]{1,0:T(8,128)(2,1)S(1)} %select_select_fusion.5.after_ref), channel_id=1, source_target_pairs={{0,16},{2,4},{4,2},{6,22},{8,24},{10,12},{12,10},{14,30},{16,0},{1... | collective-permute-start | bytes 786440 | tf_op jit(solution)/shard_map/ppermute | solution.py:389
  27.5 1.6 %collective-permute-start.12 = (bf16[128,1024]{1,0:T(8,128)(2,1)S(1)}, bf16[128,1024]{1,0:T(8,128)(2,1)S(1)}, u32[]{:S(2)}, u32[]{:S(2)}) collective-permute-start(bf16[128,1024]{1,0:T(8,128)(2,1)S(1)} %select_select_fusion.4), channel_id=1, source_target_pairs={{0,2},{2,0},{4,6},{6,4},{8,10},{10,8},{12,14},{14,12},{16,18},{18,... | collective-permute-start | bytes 786440 | tf_op jit(solution)/shard_map/ppermute | solution.py:389
  29.7 1.3 %collective-permute-start.13 = (bf16[128,1024]{1,0:T(8,128)(2,1)S(1)}, bf16[128,1024]{1,0:T(8,128)(2,1)S(1)}, u32[]{:S(2)}, u32[]{:S(2)}) collective-permute-start(bf16[128,1024]{1,0:T(8,128)(2,1)S(1)} %select_select_fusion.3), channel_id=1, source_target_pairs={{0,8},{2,10},{4,12},{6,14},{8,0},{10,2},{12,4},{14,6},{16,24},{18,... | collective-permute-start | bytes 786440 | tf_op jit(solution)/shard_map/ppermute | solution.py:389
  31.8 1.6 %collective-permute-start.14 = (bf16[128,1024]{1,0:T(8,128)(2,1)S(1)}, bf16[128,1024]{1,0:T(8,128)(2,1)S(1)}, u32[]{:S(2)}, u32[]{:S(2)}) collective-permute-start(bf16[128,1024]{1,0:T(8,128)(2,1)S(1)} %select_select_fusion.2), channel_id=1, source_target_pairs={{0,16},{2,4},{4,2},{6,22},{8,24},{10,12},{12,10},{14,30},{16,0},{1... | collective-permute-start | bytes 786440 | tf_op jit(solution)/shard_map/ppermute | solution.py:389
  33.5 1.6 %collective-permute-start.17 = (bf16[128,1024]{1,0:T(8,128)(2,1)S(1)}, bf16[128,1024]{1,0:T(8,128)(2,1)S(1)}, u32[]{:S(2)}, u32[]{:S(2)}) collective-permute-start(bf16[128,1024]{1,0:T(8,128)(2,1)S(1)} %select_select_fusion.1.after_ref), channel_id=1, source_target_pairs={{0,2},{2,0},{4,6},{6,4},{8,10},{10,8},{12,14},{14,12},{16,18},{18,... | collective-permute-start | bytes 786440 | tf_op jit(solution)/shard_map/ppermute | solution.py:389
  35.1 0.7 %more.7 = (f32[1,1024]{1,0:T(1,128)S(1)}, f32[17,256,128]{2,1,0:T(8,128)S(1)}) custom-call(bf16[18,256,128]{2,1,0:T(8,128)(2,1)S(1)} %get-tuple-element.22.left_ref, bf16[128,1024]{1,0:T(8,128)(2,1)S(1)} %select_select_fusion.1.after_ref, bf16[128,1024]{1,0:T(8,128)(2,1)S(1)} %collective-permute-done.8.refs_0_, ...), custom_call_target="tpu_custom_call", output_to_operand_aliasing={{1}: (6, {})} | custom-call | tf_op jit(solution)/shard_map/more/pallas_call | solution.py:363
  35.9 0.8 %collective-permute-done.12.after_ref.refs_0_ = bf16[128,1024]{1,0:T(8,128)(2,1)S(1)} collective-permute-done((bf16[128,1024]{1,0:T(8,128)(2,1)S(1)}, bf16[128,1024]{1,0:T(8,128)(2,1)S(1)}, u32[]{:S(2)}, u32[]{:S(2)}) %collective-permute-start.12) | collective-permute-done | bytes 262176 | tf_op jit(solution)/shard_map/ppermute | solution.py:389
  36.7 0.7 %collective-permute-start.18 = (bf16[128,1024]{1,0:T(8,128)(2,1)S(1)}, bf16[128,1024]{1,0:T(8,128)(2,1)S(1)}, u32[]{:S(2)}, u32[]{:S(2)}) collective-permute-start(bf16[128,1024]{1,0:T(8,128)(2,1)S(1)} %broadcast_select_fusion.1), channel_id=1, source_target_pairs={{0,8},{2,10},{4,12},{6,14},{8,0},{10,2},{12,4},{14,6},{16,24},{18,... | collective-permute-start | bytes 786440 | tf_op jit(solution)/shard_map/ppermute | solution.py:389
  37.4 0.7 %collective-permute-done.13.refs_1_ = bf16[128,1024]{1,0:T(8,128)(2,1)S(1)} collective-permute-done((bf16[128,1024]{1,0:T(8,128)(2,1)S(1)}, bf16[128,1024]{1,0:T(8,128)(2,1)S(1)}, u32[]{:S(2)}, u32[]{:S(2)}) %collective-permute-start.13) | collective-permute-done | bytes 262176 | tf_op jit(solution)/shard_map/ppermute | solution.py:389
  38.2 1.4 %collective-permute-start.16 = (bf16[128,1024]{1,0:T(8,128)(2,1)S(1)}, bf16[128,1024]{1,0:T(8,128)(2,1)S(1)}, u32[]{:S(2)}, u32[]{:S(2)}) collective-permute-start(bf16[128,1024]{1,0:T(8,128)(2,1)S(1)} %select_select_fusion), channel_id=1, source_target_pairs={{0,16},{2,4},{4,2},{6,22},{8,24},{10,26},{12,28},{14,30},{16,0},{1... | collective-permute-start | bytes 786440 | tf_op jit(solution)/shard_map/ppermute | solution.py:389
  39.7 0.8 %collective-permute-done.14.refs_2_ = bf16[128,1024]{1,0:T(8,128)(2,1)S(1)} collective-permute-done((bf16[128,1024]{1,0:T(8,128)(2,1)S(1)}, bf16[128,1024]{1,0:T(8,128)(2,1)S(1)}, u32[]{:S(2)}, u32[]{:S(2)}) %collective-permute-start.14) | collective-permute-done | bytes 262176 | tf_op jit(solution)/shard_map/ppermute | solution.py:389
  40.5 2.0 %collective-permute-start.15 = (bf16[128,1024]{1,0:T(8,128)(2,1)S(1)}, bf16[128,1024]{1,0:T(8,128)(2,1)S(1)}, u32[]{:S(2)}, u32[]{:S(2)}) collective-permute-start(bf16[128,1024]{1,0:T(8,128)(2,1)S(1)} %broadcast_select_fusion), channel_id=1, source_target_pairs={{0,2},{2,0},{4,6},{6,4},{8,10},{10,8},{12,14},{14,12},{16,18},{18,... | collective-permute-start | bytes 786440 | tf_op jit(solution)/shard_map/ppermute | solution.py:389
  43.1 0.8 %more.8.refs_1_ = f32[17,256,128]{2,1,0:T(8,128)S(1)} custom-call(bf16[18,256,128]{2,1,0:T(8,128)(2,1)S(1)} %get-tuple-element.22.left_ref, bf16[128,1024]{1,0:T(8,128)(2,1)S(1)} %collective-permute-done.12.after_ref.refs_0_, bf16[128,1024]{1,0:T(8,128)(2,1)S(1)} %collective-permute-done.12.after_ref.refs_0_, ...), custom_call_target="tpu_custom_call", output_to_operand_aliasing={{}: (7, {})} | custom-call | tf_op jit(solution)/shard_map/more/pallas_call | solution.py:363
  44.0 0.7 %collective-permute-done.16.after_ref.refs_0_ = bf16[128,1024]{1,0:T(8,128)(2,1)S(1)} collective-permute-done((bf16[128,1024]{1,0:T(8,128)(2,1)S(1)}, bf16[128,1024]{1,0:T(8,128)(2,1)S(1)}, u32[]{:S(2)}, u32[]{:S(2)}) %collective-permute-start.16) | collective-permute-done | bytes 262176 | tf_op jit(solution)/shard_map/ppermute | solution.py:389
  44.9 2.1 %collective-permute-done.15.refs_0_ = bf16[128,1024]{1,0:T(8,128)(2,1)S(1)} collective-permute-done((bf16[128,1024]{1,0:T(8,128)(2,1)S(1)}, bf16[128,1024]{1,0:T(8,128)(2,1)S(1)}, u32[]{:S(2)}, u32[]{:S(2)}) %collective-permute-start.15) | collective-permute-done | bytes 262176 | tf_op jit(solution)/shard_map/ppermute | solution.py:389
  47.5 0.8 %place.2.refs_0_ = bf16[2,12,2,64,128]{4,3,2,1,0:T(8,128)(2,1)} custom-call(bf16[2,12,64,128]{3,2,1,0:T(8,128)(2,1)S(1)} %get-tuple-element.34.tiles), custom_call_target="tpu_custom_call" | custom-call | tf_op jit(solution)/shard_map/place/pallas_call | solution.py:411
  48.2 0.9 %collective-permute-done.19.tiles = bf16[2,12,64,128]{3,2,1,0:T(8,128)(2,1)S(1)} collective-permute-done((bf16[2,12,64,128]{3,2,1,0:T(8,128)(2,1)S(1)}, bf16[2,12,64,128]{3,2,1,0:T(8,128)(2,1)S(1)}, u32[]{:S(2)}, u32[]{:S(2)}) %collective-permute-start.19) | collective-permute-done | bytes 393248 | tf_op jit(solution)/shard_map/ppermute | solution.py:408
  49.2 0.8 %place.3 = bf16[2,12,2,64,128]{4,3,2,1,0:T(8,128)(2,1)} custom-call(bf16[2,12,64,128]{3,2,1,0:T(8,128)(2,1)S(1)} %collective-permute-done.19.tiles, bf16[2,12,2,64,128]{4,3,2,1,0:T(8,128)(2,1)} %place.2.refs_0_), custom_call_target="tpu_custom_call", output_to_operand_aliasing={{}: (1, {})} | custom-call | tf_op jit(solution)/shard_map/place/pallas_call | solution.py:411
  (56 shorter events, 5.4 us)
Async XLA Ops:
  1.4 10.2 %collective-permute-start = (bf16[128,1024]{1,0:T(8,128)(2,1)S(1)}, bf16[128,1024]{1,0:T(8,128)(2,1)S(1)}, u32[]{:S(2)}, u32[]{:S(2)}) collective-permute-start(bf16[128,1024]{1,0:T(8,128)(2,1)S(1)} %broadcast_select_fusion.8), channel_id=1, source_target_pairs={{0,2},{2,0},{4,6},{6,4},{8,10},{10,8},{12,14},{14,12},{16,18},{18,... | collective-permute-start | bytes 786440 | tf_op jit(solution)/shard_map/ppermute | solution.py:389
  4.6 9.2 %collective-permute-start.1 = (bf16[128,1024]{1,0:T(8,128)(2,1)S(1)}, bf16[128,1024]{1,0:T(8,128)(2,1)S(1)}, u32[]{:S(2)}, u32[]{:S(2)}) collective-permute-start(bf16[128,1024]{1,0:T(8,128)(2,1)S(1)} %broadcast_select_fusion.7), channel_id=1, source_target_pairs={{0,8},{2,10},{4,12},{6,14},{8,0},{10,2},{12,4},{14,6},{16,24},{18,... | collective-permute-start | bytes 786440 | tf_op jit(solution)/shard_map/ppermute | solution.py:389
  6.2 9.2 %collective-permute-start.2 = (bf16[128,1024]{1,0:T(8,128)(2,1)S(1)}, bf16[128,1024]{1,0:T(8,128)(2,1)S(1)}, u32[]{:S(2)}, u32[]{:S(2)}) collective-permute-start(bf16[128,1024]{1,0:T(8,128)(2,1)S(1)} %broadcast_select_fusion.6), channel_id=1, source_target_pairs={{0,16},{2,18},{4,20},{6,22},{8,24},{10,12},{12,10},{14,30},{16,0},... | collective-permute-start | bytes 786440 | tf_op jit(solution)/shard_map/ppermute | solution.py:389
  7.9 9.4 %collective-permute-start.3 = (bf16[128,1024]{1,0:T(8,128)(2,1)S(1)}, bf16[128,1024]{1,0:T(8,128)(2,1)S(1)}, u32[]{:S(2)}, u32[]{:S(2)}) collective-permute-start(bf16[128,1024]{1,0:T(8,128)(2,1)S(1)} %broadcast_select_fusion.5), channel_id=1, source_target_pairs={{0,2},{2,0},{4,6},{6,4},{8,10},{10,8},{12,14},{14,12},{16,18},{18,... | collective-permute-start | bytes 786440 | tf_op jit(solution)/shard_map/ppermute | solution.py:389
  11.7 7.8 %collective-permute-start.4 = (bf16[128,1024]{1,0:T(8,128)(2,1)S(1)}, bf16[128,1024]{1,0:T(8,128)(2,1)S(1)}, u32[]{:S(2)}, u32[]{:S(2)}) collective-permute-start(bf16[128,1024]{1,0:T(8,128)(2,1)S(1)} %select_select_fusion.9), channel_id=1, source_target_pairs={{0,8},{2,10},{4,12},{6,14},{8,0},{10,2},{12,4},{14,6},{16,24},{18,... | collective-permute-start | bytes 786440 | tf_op jit(solution)/shard_map/ppermute | solution.py:389
  13.8 8.2 %collective-permute-start.5 = (bf16[128,1024]{1,0:T(8,128)(2,1)S(1)}, bf16[128,1024]{1,0:T(8,128)(2,1)S(1)}, u32[]{:S(2)}, u32[]{:S(2)}) collective-permute-start(bf16[128,1024]{1,0:T(8,128)(2,1)S(1)} %broadcast_select_fusion.4), channel_id=1, source_target_pairs={{0,16},{2,4},{4,2},{6,22},{8,24},{10,12},{12,10},{14,30},{16,0},{1... | collective-permute-start | bytes 786440 | tf_op jit(solution)/shard_map/ppermute | solution.py:389
  15.5 8.4 %collective-permute-start.6 = (bf16[128,1024]{1,0:T(8,128)(2,1)S(1)}, bf16[128,1024]{1,0:T(8,128)(2,1)S(1)}, u32[]{:S(2)}, u32[]{:S(2)}) collective-permute-start(bf16[128,1024]{1,0:T(8,128)(2,1)S(1)} %broadcast_select_fusion.3), channel_id=1, source_target_pairs={{0,2},{2,0},{4,6},{6,4},{8,10},{10,8},{12,14},{14,12},{16,18},{18,... | collective-permute-start | bytes 786440 | tf_op jit(solution)/shard_map/ppermute | solution.py:389
  17.4 7.7 %collective-permute-start.7 = (bf16[128,1024]{1,0:T(8,128)(2,1)S(1)}, bf16[128,1024]{1,0:T(8,128)(2,1)S(1)}, u32[]{:S(2)}, u32[]{:S(2)}) collective-permute-start(bf16[128,1024]{1,0:T(8,128)(2,1)S(1)} %select_select_fusion.8), channel_id=1, source_target_pairs={{0,8},{2,10},{4,12},{6,14},{8,0},{10,2},{12,4},{14,6},{16,24},{18,... | collective-permute-start | bytes 786440 | tf_op jit(solution)/shard_map/ppermute | solution.py:389
  19.6 7.9 %collective-permute-start.8 = (bf16[128,1024]{1,0:T(8,128)(2,1)S(1)}, bf16[128,1024]{1,0:T(8,128)(2,1)S(1)}, u32[]{:S(2)}, u32[]{:S(2)}) collective-permute-start(bf16[128,1024]{1,0:T(8,128)(2,1)S(1)} %select_select_fusion.7.after_ref), channel_id=1, source_target_pairs={{0,16},{2,4},{4,2},{6,22},{8,24},{10,12},{12,10},{14,30},{16,0},{1... | collective-permute-start | bytes 786440 | tf_op jit(solution)/shard_map/ppermute | solution.py:389
  22.1 7.6 %collective-permute-start.9 = (bf16[128,1024]{1,0:T(8,128)(2,1)S(1)}, bf16[128,1024]{1,0:T(8,128)(2,1)S(1)}, u32[]{:S(2)}, u32[]{:S(2)}) collective-permute-start(bf16[128,1024]{1,0:T(8,128)(2,1)S(1)} %broadcast_select_fusion.2), channel_id=1, source_target_pairs={{0,2},{2,0},{4,6},{6,4},{8,10},{10,8},{12,14},{14,12},{16,18},{18,... | collective-permute-start | bytes 786440 | tf_op jit(solution)/shard_map/ppermute | solution.py:389
  23.9 7.8 %collective-permute-start.10 = (bf16[128,1024]{1,0:T(8,128)(2,1)S(1)}, bf16[128,1024]{1,0:T(8,128)(2,1)S(1)}, u32[]{:S(2)}, u32[]{:S(2)}) collective-permute-start(bf16[128,1024]{1,0:T(8,128)(2,1)S(1)} %select_select_fusion.6), channel_id=1, source_target_pairs={{0,8},{2,10},{4,12},{6,14},{8,0},{10,2},{12,4},{14,6},{16,24},{18,... | collective-permute-start | bytes 786440 | tf_op jit(solution)/shard_map/ppermute | solution.py:389
  25.2 8.3 %collective-permute-start.11 = (bf16[128,1024]{1,0:T(8,128)(2,1)S(1)}, bf16[128,1024]{1,0:T(8,128)(2,1)S(1)}, u32[]{:S(2)}, u32[]{:S(2)}) collective-permute-start(bf16[128,1024]{1,0:T(8,128)(2,1)S(1)} %select_select_fusion.5.after_ref), channel_id=1, source_target_pairs={{0,16},{2,4},{4,2},{6,22},{8,24},{10,12},{12,10},{14,30},{16,0},{1... | collective-permute-start | bytes 786440 | tf_op jit(solution)/shard_map/ppermute | solution.py:389
  27.5 9.1 %collective-permute-start.12 = (bf16[128,1024]{1,0:T(8,128)(2,1)S(1)}, bf16[128,1024]{1,0:T(8,128)(2,1)S(1)}, u32[]{:S(2)}, u32[]{:S(2)}) collective-permute-start(bf16[128,1024]{1,0:T(8,128)(2,1)S(1)} %select_select_fusion.4), channel_id=1, source_target_pairs={{0,2},{2,0},{4,6},{6,4},{8,10},{10,8},{12,14},{14,12},{16,18},{18,... | collective-permute-start | bytes 786440 | tf_op jit(solution)/shard_map/ppermute | solution.py:389
  29.7 8.4 %collective-permute-start.13 = (bf16[128,1024]{1,0:T(8,128)(2,1)S(1)}, bf16[128,1024]{1,0:T(8,128)(2,1)S(1)}, u32[]{:S(2)}, u32[]{:S(2)}) collective-permute-start(bf16[128,1024]{1,0:T(8,128)(2,1)S(1)} %select_select_fusion.3), channel_id=1, source_target_pairs={{0,8},{2,10},{4,12},{6,14},{8,0},{10,2},{12,4},{14,6},{16,24},{18,... | collective-permute-start | bytes 786440 | tf_op jit(solution)/shard_map/ppermute | solution.py:389
  31.8 8.7 %collective-permute-start.14 = (bf16[128,1024]{1,0:T(8,128)(2,1)S(1)}, bf16[128,1024]{1,0:T(8,128)(2,1)S(1)}, u32[]{:S(2)}, u32[]{:S(2)}) collective-permute-start(bf16[128,1024]{1,0:T(8,128)(2,1)S(1)} %select_select_fusion.2), channel_id=1, source_target_pairs={{0,16},{2,4},{4,2},{6,22},{8,24},{10,12},{12,10},{14,30},{16,0},{1... | collective-permute-start | bytes 786440 | tf_op jit(solution)/shard_map/ppermute | solution.py:389
  33.5 9.0 %collective-permute-start.17 = (bf16[128,1024]{1,0:T(8,128)(2,1)S(1)}, bf16[128,1024]{1,0:T(8,128)(2,1)S(1)}, u32[]{:S(2)}, u32[]{:S(2)}) collective-permute-start(bf16[128,1024]{1,0:T(8,128)(2,1)S(1)} %select_select_fusion.1.after_ref), channel_id=1, source_target_pairs={{0,2},{2,0},{4,6},{6,4},{8,10},{10,8},{12,14},{14,12},{16,18},{18,... | collective-permute-start | bytes 786440 | tf_op jit(solution)/shard_map/ppermute | solution.py:389
  36.7 6.4 %collective-permute-start.18 = (bf16[128,1024]{1,0:T(8,128)(2,1)S(1)}, bf16[128,1024]{1,0:T(8,128)(2,1)S(1)}, u32[]{:S(2)}, u32[]{:S(2)}) collective-permute-start(bf16[128,1024]{1,0:T(8,128)(2,1)S(1)} %broadcast_select_fusion.1), channel_id=1, source_target_pairs={{0,8},{2,10},{4,12},{6,14},{8,0},{10,2},{12,4},{14,6},{16,24},{18,... | collective-permute-start | bytes 786440 | tf_op jit(solution)/shard_map/ppermute | solution.py:389
  38.2 6.4 %collective-permute-start.16 = (bf16[128,1024]{1,0:T(8,128)(2,1)S(1)}, bf16[128,1024]{1,0:T(8,128)(2,1)S(1)}, u32[]{:S(2)}, u32[]{:S(2)}) collective-permute-start(bf16[128,1024]{1,0:T(8,128)(2,1)S(1)} %select_select_fusion), channel_id=1, source_target_pairs={{0,16},{2,4},{4,2},{6,22},{8,24},{10,26},{12,28},{14,30},{16,0},{1... | collective-permute-start | bytes 786440 | tf_op jit(solution)/shard_map/ppermute | solution.py:389
  40.5 6.4 %collective-permute-start.15 = (bf16[128,1024]{1,0:T(8,128)(2,1)S(1)}, bf16[128,1024]{1,0:T(8,128)(2,1)S(1)}, u32[]{:S(2)}, u32[]{:S(2)}) collective-permute-start(bf16[128,1024]{1,0:T(8,128)(2,1)S(1)} %broadcast_select_fusion), channel_id=1, source_target_pairs={{0,2},{2,0},{4,6},{6,4},{8,10},{10,8},{12,14},{14,12},{16,18},{18,... | collective-permute-start | bytes 786440 | tf_op jit(solution)/shard_map/ppermute | solution.py:389
  47.4 1.8 %collective-permute-start.19 = (bf16[2,12,64,128]{3,2,1,0:T(8,128)(2,1)S(1)}, bf16[2,12,64,128]{3,2,1,0:T(8,128)(2,1)S(1)}, u32[]{:S(2)}, u32[]{:S(2)}) collective-permute-start(bf16[2,12,64,128]{3,2,1,0:T(8,128)(2,1)S(1)} %get-tuple-element.33), channel_id=1, source_target_pairs={{0,1},{1,0},{2,3},{3,2},{4,5},{5,4},{6,7},{7,6},{8,9},{9,8},{10,11... | collective-permute-start | bytes 1179656 | tf_op jit(solution)/shard_map/ppermute | solution.py:408

commit v7 on v6

--- a/solution.py
+++ b/solution.py
@@ -164,16 +164,16 @@
     copies = [
         pltpu.make_async_copy(band_hbm.at[row], band_ref.at[row], sems.at[row]) for row in range(2)
     ]
-    for copy in (fill_copy, *copies):
+    for copy in (fill_copy, copies[1], copies[0]):
         copy.start()
     chip, core = position()
     for i, mask in enumerate(choice_masks):
         bit = ((mask >> chip) & 1).astype(jnp.float32)
         flags[i : i + 1, :] = jnp.full((1, flags.shape[1]), bit, flags.dtype)
     packed = chip >= packed_from
-    for copy in (fill_copy, *copies):
-        copy.wait()
-    for part, unit in enumerate(outs):
+    fill_copy.wait()
+    for part, unit in ((1, outs[1]), (0, outs[0])):
+        copies[part].wait()
         for slot in range(SLOTS):
             row, t = part, slot
             if part == 0:

time: 50.1 us -> 50 us (level)
  no operation moved by 1% of the time
where the time goes in v7:
time: 50 us; the launch traced here: 49.9 us
  starting transfers between devices  30.5 us (61%)
  waiting for transfers between devices  9.1 us (18%)
  Pallas kernels  8.25 us (16%)
  other arithmetic  1.85 us (4%)
    ppermute x19, starting transfers between devices, per_device(): buffers[o] = lax.ppermute(payload, RC, [(s, t) for s, t, _ in moves])  30.4 us
    ppermute x19, waiting for transfers between devices, per_device(): buffers[o] = lax.ppermute(payload, RC, [(s, t) for s, t, _ in moves])  8.17 us
    pallas_call x5, Pallas kernels, more(): pl.pallas_call(functools.partial(more_kernel, [terms[n] for n in names]),...  3.21 us
    pallas_call x1, Pallas kernels, start(): pl.pallas_call(functools.partial(first_kernel, [terms['n0'], terms['n1']]...  1.84 us
    pallas_call x2, Pallas kernels, per_device(): pl.pallas_call(functools.partial(place_kernel, partner), out_shape=jax.Sh...  1.52 us
    pallas_call x1, Pallas kernels, per_device(): pl.pallas_call(functools.partial(units_kernel, min(packed, default=chips)...  1.3 us
  transfers between devices with their start and end apart: 20, of which 11 were waited for; matrix products, arithmetic and copies ran while one was open for 4% of the time, Pallas kernels for 12%

profile of v7, /device:TPU:0, one launch (start us, length us, event | category | flops | bytes accessed | tf_op | source)
XLA Modules:
  0.0 49.9 jit_solution(15183113964686774121)
XLA Ops:
  0.0 1.3 %units.1 = (bf16[128,1024]{1,0:T(8,128)(2,1)S(1)}, bf16[128,1024]{1,0:T(8,128)(2,1)S(1)}, f32[38,1024]{1,0:T(8,128)S(1)}) custom-call(s32[2,16]{1,0:T(2,128)} %fill_hbm.3, bf16[2,16,128,128]{3,2,1,0:T(8,128)(2,1)} %band_hbm.3), custom_call_target="tpu_custom_call" | custom-call | tf_op jit(solution)/shard_map/units/pallas_call | solution.py:323
  1.4 3.1 %collective-permute-start = (bf16[128,1024]{1,0:T(8,128)(2,1)S(1)}, bf16[128,1024]{1,0:T(8,128)(2,1)S(1)}, u32[]{:S(2)}, u32[]{:S(2)}) collective-permute-start(bf16[128,1024]{1,0:T(8,128)(2,1)S(1)} %broadcast_select_fusion.8), channel_id=1, source_target_pairs={{0,2},{2,0},{4,6},{6,4},{8,10},{10,8},{12,14},{14,12},{16,18},{18,... | collective-permute-start | bytes 786440 | tf_op jit(solution)/shard_map/ppermute | solution.py:389
  4.5 1.6 %collective-permute-start.1 = (bf16[128,1024]{1,0:T(8,128)(2,1)S(1)}, bf16[128,1024]{1,0:T(8,128)(2,1)S(1)}, u32[]{:S(2)}, u32[]{:S(2)}) collective-permute-start(bf16[128,1024]{1,0:T(8,128)(2,1)S(1)} %broadcast_select_fusion.7), channel_id=1, source_target_pairs={{0,8},{2,10},{4,12},{6,14},{8,0},{10,2},{12,4},{14,6},{16,24},{18,... | collective-permute-start | bytes 786440 | tf_op jit(solution)/shard_map/ppermute | solution.py:389
  6.1 1.6 %collective-permute-start.2 = (bf16[128,1024]{1,0:T(8,128)(2,1)S(1)}, bf16[128,1024]{1,0:T(8,128)(2,1)S(1)}, u32[]{:S(2)}, u32[]{:S(2)}) collective-permute-start(bf16[128,1024]{1,0:T(8,128)(2,1)S(1)} %broadcast_select_fusion.6), channel_id=1, source_target_pairs={{0,16},{2,18},{4,20},{6,22},{8,24},{10,12},{12,10},{14,30},{16,0},... | collective-permute-start | bytes 786440 | tf_op jit(solution)/shard_map/ppermute | solution.py:389
  8.3 1.8 %first.1 = (bf16[18,256,128]{2,1,0:T(8,128)(2,1)S(1)}, f32[2,12,128]{2,1,0:T(8,128)S(1)}, f32[1,1024]{1,0:T(1,128)S(1)}, f32[17,256,128]{2,1,0:T(8,128)S(1)}) custom-call(s32[2]{0:T(128)} %reach_hbm.1, s32[2,16]{1,0:T(2,128)} %fill_hbm.3, bf16[2,16,128,128]{3,2,1,0:T(8,128)(2,1)} %band_hbm.3, bf16[128,1024]{1,0:T(8,128)(2,1)S(1)} %get-tuple-element.20.refs_0_, ...), custom_call_target="tpu_custom_call" | custom-call | tf_op jit(solution)/shard_map/first/pallas_call | solution.py:341
  10.2 1.4 %collective-permute-done.refs_0_ = bf16[128,1024]{1,0:T(8,128)(2,1)S(1)} collective-permute-done((bf16[128,1024]{1,0:T(8,128)(2,1)S(1)}, bf16[128,1024]{1,0:T(8,128)(2,1)S(1)}, u32[]{:S(2)}, u32[]{:S(2)}) %collective-permute-start) | collective-permute-done | bytes 262176 | tf_op jit(solution)/shard_map/ppermute | solution.py:389
  11.6 2.0 %collective-permute-start.4 = (bf16[128,1024]{1,0:T(8,128)(2,1)S(1)}, bf16[128,1024]{1,0:T(8,128)(2,1)S(1)}, u32[]{:S(2)}, u32[]{:S(2)}) collective-permute-start(bf16[128,1024]{1,0:T(8,128)(2,1)S(1)} %select_select_fusion.9), channel_id=1, source_target_pairs={{0,8},{2,10},{4,12},{6,14},{8,0},{10,2},{12,4},{14,6},{16,24},{18,... | collective-permute-start | bytes 786440 | tf_op jit(solution)/shard_map/ppermute | solution.py:389
  13.8 1.6 %collective-permute-start.5 = (bf16[128,1024]{1,0:T(8,128)(2,1)S(1)}, bf16[128,1024]{1,0:T(8,128)(2,1)S(1)}, u32[]{:S(2)}, u32[]{:S(2)}) collective-permute-start(bf16[128,1024]{1,0:T(8,128)(2,1)S(1)} %broadcast_select_fusion.4), channel_id=1, source_target_pairs={{0,16},{2,4},{4,2},{6,22},{8,24},{10,12},{12,10},{14,30},{16,0},{1... | collective-permute-start | bytes 786440 | tf_op jit(solution)/shard_map/ppermute | solution.py:389
  15.4 1.7 %collective-permute-start.6 = (bf16[128,1024]{1,0:T(8,128)(2,1)S(1)}, bf16[128,1024]{1,0:T(8,128)(2,1)S(1)}, u32[]{:S(2)}, u32[]{:S(2)}) collective-permute-start(bf16[128,1024]{1,0:T(8,128)(2,1)S(1)} %broadcast_select_fusion.3), channel_id=1, source_target_pairs={{0,2},{2,0},{4,6},{6,4},{8,10},{10,8},{12,14},{14,12},{16,18},{18,... | collective-permute-start | bytes 786440 | tf_op jit(solution)/shard_map/ppermute | solution.py:389
  17.3 2.0 %collective-permute-start.7 = (bf16[128,1024]{1,0:T(8,128)(2,1)S(1)}, bf16[128,1024]{1,0:T(8,128)(2,1)S(1)}, u32[]{:S(2)}, u32[]{:S(2)}) collective-permute-start(bf16[128,1024]{1,0:T(8,128)(2,1)S(1)} %select_select_fusion.8), channel_id=1, source_target_pairs={{0,8},{2,10},{4,12},{6,14},{8,0},{10,2},{12,4},{14,6},{16,24},{18,... | collective-permute-start | bytes 786440 | tf_op jit(solution)/shard_map/ppermute | solution.py:389
  19.5 1.6 %collective-permute-start.8 = (bf16[128,1024]{1,0:T(8,128)(2,1)S(1)}, bf16[128,1024]{1,0:T(8,128)(2,1)S(1)}, u32[]{:S(2)}, u32[]{:S(2)}) collective-permute-start(bf16[128,1024]{1,0:T(8,128)(2,1)S(1)} %select_select_fusion.7.after_ref), channel_id=1, source_target_pairs={{0,16},{2,4},{4,2},{6,22},{8,24},{10,12},{12,10},{14,30},{16,0},{1... | collective-permute-start | bytes 786440 | tf_op jit(solution)/shard_map/ppermute | solution.py:389
  21.1 0.8 %more.5 = (f32[1,1024]{1,0:T(1,128)S(1)}, f32[17,256,128]{2,1,0:T(8,128)S(1)}) custom-call(bf16[18,256,128]{2,1,0:T(8,128)(2,1)S(1)} %get-tuple-element.22.left_ref, bf16[128,1024]{1,0:T(8,128)(2,1)S(1)} %select_select_fusion.7.after_ref, bf16[128,1024]{1,0:T(8,128)(2,1)S(1)} %collective-permute-done.refs_0_, ...), custom_call_target="tpu_custom_call", output_to_operand_aliasing={{1}: (7, {})} | custom-call | tf_op jit(solution)/shard_map/more/pallas_call | solution.py:363
  22.0 1.7 %collective-permute-start.9 = (bf16[128,1024]{1,0:T(8,128)(2,1)S(1)}, bf16[128,1024]{1,0:T(8,128)(2,1)S(1)}, u32[]{:S(2)}, u32[]{:S(2)}) collective-permute-start(bf16[128,1024]{1,0:T(8,128)(2,1)S(1)} %broadcast_select_fusion.2), channel_id=1, source_target_pairs={{0,2},{2,0},{4,6},{6,4},{8,10},{10,8},{12,14},{14,12},{16,18},{18,... | collective-permute-start | bytes 786440 | tf_op jit(solution)/shard_map/ppermute | solution.py:389
  23.8 1.1 %collective-permute-start.10 = (bf16[128,1024]{1,0:T(8,128)(2,1)S(1)}, bf16[128,1024]{1,0:T(8,128)(2,1)S(1)}, u32[]{:S(2)}, u32[]{:S(2)}) collective-permute-start(bf16[128,1024]{1,0:T(8,128)(2,1)S(1)} %select_select_fusion.6), channel_id=1, source_target_pairs={{0,8},{2,10},{4,12},{6,14},{8,0},{10,2},{12,4},{14,6},{16,24},{18,... | collective-permute-start | bytes 786440 | tf_op jit(solution)/shard_map/ppermute | solution.py:389
  25.1 1.7 %collective-permute-start.11 = (bf16[128,1024]{1,0:T(8,128)(2,1)S(1)}, bf16[128,1024]{1,0:T(8,128)(2,1)S(1)}, u32[]{:S(2)}, u32[]{:S(2)}) collective-permute-start(bf16[128,1024]{1,0:T(8,128)(2,1)S(1)} %select_select_fusion.5.after_ref), channel_id=1, source_target_pairs={{0,16},{2,4},{4,2},{6,22},{8,24},{10,12},{12,10},{14,30},{16,0},{1... | collective-permute-start | bytes 786440 | tf_op jit(solution)/shard_map/ppermute | solution.py:389
  27.5 1.6 %collective-permute-start.12 = (bf16[128,1024]{1,0:T(8,128)(2,1)S(1)}, bf16[128,1024]{1,0:T(8,128)(2,1)S(1)}, u32[]{:S(2)}, u32[]{:S(2)}) collective-permute-start(bf16[128,1024]{1,0:T(8,128)(2,1)S(1)} %select_select_fusion.4), channel_id=1, source_target_pairs={{0,2},{2,0},{4,6},{6,4},{8,10},{10,8},{12,14},{14,12},{16,18},{18,... | collective-permute-start | bytes 786440 | tf_op jit(solution)/shard_map/ppermute | solution.py:389
  29.7 1.3 %collective-permute-start.13 = (bf16[128,1024]{1,0:T(8,128)(2,1)S(1)}, bf16[128,1024]{1,0:T(8,128)(2,1)S(1)}, u32[]{:S(2)}, u32[]{:S(2)}) collective-permute-start(bf16[128,1024]{1,0:T(8,128)(2,1)S(1)} %select_select_fusion.3), channel_id=1, source_target_pairs={{0,8},{2,10},{4,12},{6,14},{8,0},{10,2},{12,4},{14,6},{16,24},{18,... | collective-permute-start | bytes 786440 | tf_op jit(solution)/shard_map/ppermute | solution.py:389
  31.7 1.6 %collective-permute-start.14 = (bf16[128,1024]{1,0:T(8,128)(2,1)S(1)}, bf16[128,1024]{1,0:T(8,128)(2,1)S(1)}, u32[]{:S(2)}, u32[]{:S(2)}) collective-permute-start(bf16[128,1024]{1,0:T(8,128)(2,1)S(1)} %select_select_fusion.2), channel_id=1, source_target_pairs={{0,16},{2,4},{4,2},{6,22},{8,24},{10,12},{12,10},{14,30},{16,0},{1... | collective-permute-start | bytes 786440 | tf_op jit(solution)/shard_map/ppermute | solution.py:389
  33.5 1.6 %collective-permute-start.17 = (bf16[128,1024]{1,0:T(8,128)(2,1)S(1)}, bf16[128,1024]{1,0:T(8,128)(2,1)S(1)}, u32[]{:S(2)}, u32[]{:S(2)}) collective-permute-start(bf16[128,1024]{1,0:T(8,128)(2,1)S(1)} %select_select_fusion.1.after_ref), channel_id=1, source_target_pairs={{0,2},{2,0},{4,6},{6,4},{8,10},{10,8},{12,14},{14,12},{16,18},{18,... | collective-permute-start | bytes 786440 | tf_op jit(solution)/shard_map/ppermute | solution.py:389
  35.1 0.7 %more.7 = (f32[1,1024]{1,0:T(1,128)S(1)}, f32[17,256,128]{2,1,0:T(8,128)S(1)}) custom-call(bf16[18,256,128]{2,1,0:T(8,128)(2,1)S(1)} %get-tuple-element.22.left_ref, bf16[128,1024]{1,0:T(8,128)(2,1)S(1)} %select_select_fusion.1.after_ref, bf16[128,1024]{1,0:T(8,128)(2,1)S(1)} %collective-permute-done.8.refs_0_, ...), custom_call_target="tpu_custom_call", output_to_operand_aliasing={{1}: (6, {})} | custom-call | tf_op jit(solution)/shard_map/more/pallas_call | solution.py:363
  35.8 0.8 %collective-permute-done.12.after_ref.refs_0_ = bf16[128,1024]{1,0:T(8,128)(2,1)S(1)} collective-permute-done((bf16[128,1024]{1,0:T(8,128)(2,1)S(1)}, bf16[128,1024]{1,0:T(8,128)(2,1)S(1)}, u32[]{:S(2)}, u32[]{:S(2)}) %collective-permute-start.12) | collective-permute-done | bytes 262176 | tf_op jit(solution)/shard_map/ppermute | solution.py:389
  36.6 0.7 %collective-permute-start.18 = (bf16[128,1024]{1,0:T(8,128)(2,1)S(1)}, bf16[128,1024]{1,0:T(8,128)(2,1)S(1)}, u32[]{:S(2)}, u32[]{:S(2)}) collective-permute-start(bf16[128,1024]{1,0:T(8,128)(2,1)S(1)} %broadcast_select_fusion.1), channel_id=1, source_target_pairs={{0,8},{2,10},{4,12},{6,14},{8,0},{10,2},{12,4},{14,6},{16,24},{18,... | collective-permute-start | bytes 786440 | tf_op jit(solution)/shard_map/ppermute | solution.py:389
  37.4 0.7 %collective-permute-done.13.refs_1_ = bf16[128,1024]{1,0:T(8,128)(2,1)S(1)} collective-permute-done((bf16[128,1024]{1,0:T(8,128)(2,1)S(1)}, bf16[128,1024]{1,0:T(8,128)(2,1)S(1)}, u32[]{:S(2)}, u32[]{:S(2)}) %collective-permute-start.13) | collective-permute-done | bytes 262176 | tf_op jit(solution)/shard_map/ppermute | solution.py:389
  38.1 1.4 %collective-permute-start.16 = (bf16[128,1024]{1,0:T(8,128)(2,1)S(1)}, bf16[128,1024]{1,0:T(8,128)(2,1)S(1)}, u32[]{:S(2)}, u32[]{:S(2)}) collective-permute-start(bf16[128,1024]{1,0:T(8,128)(2,1)S(1)} %select_select_fusion), channel_id=1, source_target_pairs={{0,16},{2,4},{4,2},{6,22},{8,24},{10,26},{12,28},{14,30},{16,0},{1... | collective-permute-start | bytes 786440 | tf_op jit(solution)/shard_map/ppermute | solution.py:389
  39.6 0.8 %collective-permute-done.14.refs_2_ = bf16[128,1024]{1,0:T(8,128)(2,1)S(1)} collective-permute-done((bf16[128,1024]{1,0:T(8,128)(2,1)S(1)}, bf16[128,1024]{1,0:T(8,128)(2,1)S(1)}, u32[]{:S(2)}, u32[]{:S(2)}) %collective-permute-start.14) | collective-permute-done | bytes 262176 | tf_op jit(solution)/shard_map/ppermute | solution.py:389
  40.5 2.0 %collective-permute-start.15 = (bf16[128,1024]{1,0:T(8,128)(2,1)S(1)}, bf16[128,1024]{1,0:T(8,128)(2,1)S(1)}, u32[]{:S(2)}, u32[]{:S(2)}) collective-permute-start(bf16[128,1024]{1,0:T(8,128)(2,1)S(1)} %broadcast_select_fusion), channel_id=1, source_target_pairs={{0,2},{2,0},{4,6},{6,4},{8,10},{10,8},{12,14},{14,12},{16,18},{18,... | collective-permute-start | bytes 786440 | tf_op jit(solution)/shard_map/ppermute | solution.py:389
  43.0 0.8 %more.8.refs_1_ = f32[17,256,128]{2,1,0:T(8,128)S(1)} custom-call(bf16[18,256,128]{2,1,0:T(8,128)(2,1)S(1)} %get-tuple-element.22.left_ref, bf16[128,1024]{1,0:T(8,128)(2,1)S(1)} %collective-permute-done.12.after_ref.refs_0_, bf16[128,1024]{1,0:T(8,128)(2,1)S(1)} %collective-permute-done.12.after_ref.refs_0_, ...), custom_call_target="tpu_custom_call", output_to_operand_aliasing={{}: (7, {})} | custom-call | tf_op jit(solution)/shard_map/more/pallas_call | solution.py:363
  43.9 0.7 %collective-permute-done.16.after_ref.refs_0_ = bf16[128,1024]{1,0:T(8,128)(2,1)S(1)} collective-permute-done((bf16[128,1024]{1,0:T(8,128)(2,1)S(1)}, bf16[128,1024]{1,0:T(8,128)(2,1)S(1)}, u32[]{:S(2)}, u32[]{:S(2)}) %collective-permute-start.16) | collective-permute-done | bytes 262176 | tf_op jit(solution)/shard_map/ppermute | solution.py:389
  44.9 2.1 %collective-permute-done.15.refs_0_ = bf16[128,1024]{1,0:T(8,128)(2,1)S(1)} collective-permute-done((bf16[128,1024]{1,0:T(8,128)(2,1)S(1)}, bf16[128,1024]{1,0:T(8,128)(2,1)S(1)}, u32[]{:S(2)}, u32[]{:S(2)}) %collective-permute-start.15) | collective-permute-done | bytes 262176 | tf_op jit(solution)/shard_map/ppermute | solution.py:389
  47.4 0.8 %place.2.refs_0_ = bf16[2,12,2,64,128]{4,3,2,1,0:T(8,128)(2,1)} custom-call(bf16[2,12,64,128]{3,2,1,0:T(8,128)(2,1)S(1)} %get-tuple-element.34.tiles), custom_call_target="tpu_custom_call" | custom-call | tf_op jit(solution)/shard_map/place/pallas_call | solution.py:411
  48.2 0.9 %collective-permute-done.19.tiles = bf16[2,12,64,128]{3,2,1,0:T(8,128)(2,1)S(1)} collective-permute-done((bf16[2,12,64,128]{3,2,1,0:T(8,128)(2,1)S(1)}, bf16[2,12,64,128]{3,2,1,0:T(8,128)(2,1)S(1)}, u32[]{:S(2)}, u32[]{:S(2)}) %collective-permute-start.19) | collective-permute-done | bytes 393248 | tf_op jit(solution)/shard_map/ppermute | solution.py:408
  49.1 0.8 %place.3 = bf16[2,12,2,64,128]{4,3,2,1,0:T(8,128)(2,1)} custom-call(bf16[2,12,64,128]{3,2,1,0:T(8,128)(2,1)S(1)} %collective-permute-done.19.tiles, bf16[2,12,2,64,128]{4,3,2,1,0:T(8,128)(2,1)} %place.2.refs_0_), custom_call_target="tpu_custom_call", output_to_operand_aliasing={{}: (1, {})} | custom-call | tf_op jit(solution)/shard_map/place/pallas_call | solution.py:411
  (56 shorter events, 5.4 us)
Async XLA Ops:
  1.4 10.2 %collective-permute-start = (bf16[128,1024]{1,0:T(8,128)(2,1)S(1)}, bf16[128,1024]{1,0:T(8,128)(2,1)S(1)}, u32[]{:S(2)}, u32[]{:S(2)}) collective-permute-start(bf16[128,1024]{1,0:T(8,128)(2,1)S(1)} %broadcast_select_fusion.8), channel_id=1, source_target_pairs={{0,2},{2,0},{4,6},{6,4},{8,10},{10,8},{12,14},{14,12},{16,18},{18,... | collective-permute-start | bytes 786440 | tf_op jit(solution)/shard_map/ppermute | solution.py:389
  4.5 9.2 %collective-permute-start.1 = (bf16[128,1024]{1,0:T(8,128)(2,1)S(1)}, bf16[128,1024]{1,0:T(8,128)(2,1)S(1)}, u32[]{:S(2)}, u32[]{:S(2)}) collective-permute-start(bf16[128,1024]{1,0:T(8,128)(2,1)S(1)} %broadcast_select_fusion.7), channel_id=1, source_target_pairs={{0,8},{2,10},{4,12},{6,14},{8,0},{10,2},{12,4},{14,6},{16,24},{18,... | collective-permute-start | bytes 786440 | tf_op jit(solution)/shard_map/ppermute | solution.py:389
  6.1 9.2 %collective-permute-start.2 = (bf16[128,1024]{1,0:T(8,128)(2,1)S(1)}, bf16[128,1024]{1,0:T(8,128)(2,1)S(1)}, u32[]{:S(2)}, u32[]{:S(2)}) collective-permute-start(bf16[128,1024]{1,0:T(8,128)(2,1)S(1)} %broadcast_select_fusion.6), channel_id=1, source_target_pairs={{0,16},{2,18},{4,20},{6,22},{8,24},{10,12},{12,10},{14,30},{16,0},... | collective-permute-start | bytes 786440 | tf_op jit(solution)/shard_map/ppermute | solution.py:389
  7.8 9.4 %collective-permute-start.3 = (bf16[128,1024]{1,0:T(8,128)(2,1)S(1)}, bf16[128,1024]{1,0:T(8,128)(2,1)S(1)}, u32[]{:S(2)}, u32[]{:S(2)}) collective-permute-start(bf16[128,1024]{1,0:T(8,128)(2,1)S(1)} %broadcast_select_fusion.5), channel_id=1, source_target_pairs={{0,2},{2,0},{4,6},{6,4},{8,10},{10,8},{12,14},{14,12},{16,18},{18,... | collective-permute-start | bytes 786440 | tf_op jit(solution)/shard_map/ppermute | solution.py:389
  11.6 7.8 %collective-permute-start.4 = (bf16[128,1024]{1,0:T(8,128)(2,1)S(1)}, bf16[128,1024]{1,0:T(8,128)(2,1)S(1)}, u32[]{:S(2)}, u32[]{:S(2)}) collective-permute-start(bf16[128,1024]{1,0:T(8,128)(2,1)S(1)} %select_select_fusion.9), channel_id=1, source_target_pairs={{0,8},{2,10},{4,12},{6,14},{8,0},{10,2},{12,4},{14,6},{16,24},{18,... | collective-permute-start | bytes 786440 | tf_op jit(solution)/shard_map/ppermute | solution.py:389
  13.8 8.2 %collective-permute-start.5 = (bf16[128,1024]{1,0:T(8,128)(2,1)S(1)}, bf16[128,1024]{1,0:T(8,128)(2,1)S(1)}, u32[]{:S(2)}, u32[]{:S(2)}) collective-permute-start(bf16[128,1024]{1,0:T(8,128)(2,1)S(1)} %broadcast_select_fusion.4), channel_id=1, source_target_pairs={{0,16},{2,4},{4,2},{6,22},{8,24},{10,12},{12,10},{14,30},{16,0},{1... | collective-permute-start | bytes 786440 | tf_op jit(solution)/shard_map/ppermute | solution.py:389
  15.4 8.4 %collective-permute-start.6 = (bf16[128,1024]{1,0:T(8,128)(2,1)S(1)}, bf16[128,1024]{1,0:T(8,128)(2,1)S(1)}, u32[]{:S(2)}, u32[]{:S(2)}) collective-permute-start(bf16[128,1024]{1,0:T(8,128)(2,1)S(1)} %broadcast_select_fusion.3), channel_id=1, source_target_pairs={{0,2},{2,0},{4,6},{6,4},{8,10},{10,8},{12,14},{14,12},{16,18},{18,... | collective-permute-start | bytes 786440 | tf_op jit(solution)/shard_map/ppermute | solution.py:389
  17.3 7.7 %collective-permute-start.7 = (bf16[128,1024]{1,0:T(8,128)(2,1)S(1)}, bf16[128,1024]{1,0:T(8,128)(2,1)S(1)}, u32[]{:S(2)}, u32[]{:S(2)}) collective-permute-start(bf16[128,1024]{1,0:T(8,128)(2,1)S(1)} %select_select_fusion.8), channel_id=1, source_target_pairs={{0,8},{2,10},{4,12},{6,14},{8,0},{10,2},{12,4},{14,6},{16,24},{18,... | collective-permute-start | bytes 786440 | tf_op jit(solution)/shard_map/ppermute | solution.py:389
  19.5 7.9 %collective-permute-start.8 = (bf16[128,1024]{1,0:T(8,128)(2,1)S(1)}, bf16[128,1024]{1,0:T(8,128)(2,1)S(1)}, u32[]{:S(2)}, u32[]{:S(2)}) collective-permute-start(bf16[128,1024]{1,0:T(8,128)(2,1)S(1)} %select_select_fusion.7.after_ref), channel_id=1, source_target_pairs={{0,16},{2,4},{4,2},{6,22},{8,24},{10,12},{12,10},{14,30},{16,0},{1... | collective-permute-start | bytes 786440 | tf_op jit(solution)/shard_map/ppermute | solution.py:389
  22.0 7.6 %collective-permute-start.9 = (bf16[128,1024]{1,0:T(8,128)(2,1)S(1)}, bf16[128,1024]{1,0:T(8,128)(2,1)S(1)}, u32[]{:S(2)}, u32[]{:S(2)}) collective-permute-start(bf16[128,1024]{1,0:T(8,128)(2,1)S(1)} %broadcast_select_fusion.2), channel_id=1, source_target_pairs={{0,2},{2,0},{4,6},{6,4},{8,10},{10,8},{12,14},{14,12},{16,18},{18,... | collective-permute-start | bytes 786440 | tf_op jit(solution)/shard_map/ppermute | solution.py:389
  23.8 7.8 %collective-permute-start.10 = (bf16[128,1024]{1,0:T(8,128)(2,1)S(1)}, bf16[128,1024]{1,0:T(8,128)(2,1)S(1)}, u32[]{:S(2)}, u32[]{:S(2)}) collective-permute-start(bf16[128,1024]{1,0:T(8,128)(2,1)S(1)} %select_select_fusion.6), channel_id=1, source_target_pairs={{0,8},{2,10},{4,12},{6,14},{8,0},{10,2},{12,4},{14,6},{16,24},{18,... | collective-permute-start | bytes 786440 | tf_op jit(solution)/shard_map/ppermute | solution.py:389
  25.1 8.3 %collective-permute-start.11 = (bf16[128,1024]{1,0:T(8,128)(2,1)S(1)}, bf16[128,1024]{1,0:T(8,128)(2,1)S(1)}, u32[]{:S(2)}, u32[]{:S(2)}) collective-permute-start(bf16[128,1024]{1,0:T(8,128)(2,1)S(1)} %select_select_fusion.5.after_ref), channel_id=1, source_target_pairs={{0,16},{2,4},{4,2},{6,22},{8,24},{10,12},{12,10},{14,30},{16,0},{1... | collective-permute-start | bytes 786440 | tf_op jit(solution)/shard_map/ppermute | solution.py:389
  27.5 9.1 %collective-permute-start.12 = (bf16[128,1024]{1,0:T(8,128)(2,1)S(1)}, bf16[128,1024]{1,0:T(8,128)(2,1)S(1)}, u32[]{:S(2)}, u32[]{:S(2)}) collective-permute-start(bf16[128,1024]{1,0:T(8,128)(2,1)S(1)} %select_select_fusion.4), channel_id=1, source_target_pairs={{0,2},{2,0},{4,6},{6,4},{8,10},{10,8},{12,14},{14,12},{16,18},{18,... | collective-permute-start | bytes 786440 | tf_op jit(solution)/shard_map/ppermute | solution.py:389
  29.7 8.4 %collective-permute-start.13 = (bf16[128,1024]{1,0:T(8,128)(2,1)S(1)}, bf16[128,1024]{1,0:T(8,128)(2,1)S(1)}, u32[]{:S(2)}, u32[]{:S(2)}) collective-permute-start(bf16[128,1024]{1,0:T(8,128)(2,1)S(1)} %select_select_fusion.3), channel_id=1, source_target_pairs={{0,8},{2,10},{4,12},{6,14},{8,0},{10,2},{12,4},{14,6},{16,24},{18,... | collective-permute-start | bytes 786440 | tf_op jit(solution)/shard_map/ppermute | solution.py:389
  31.7 8.7 %collective-permute-start.14 = (bf16[128,1024]{1,0:T(8,128)(2,1)S(1)}, bf16[128,1024]{1,0:T(8,128)(2,1)S(1)}, u32[]{:S(2)}, u32[]{:S(2)}) collective-permute-start(bf16[128,1024]{1,0:T(8,128)(2,1)S(1)} %select_select_fusion.2), channel_id=1, source_target_pairs={{0,16},{2,4},{4,2},{6,22},{8,24},{10,12},{12,10},{14,30},{16,0},{1... | collective-permute-start | bytes 786440 | tf_op jit(solution)/shard_map/ppermute | solution.py:389
  33.5 9.0 %collective-permute-start.17 = (bf16[128,1024]{1,0:T(8,128)(2,1)S(1)}, bf16[128,1024]{1,0:T(8,128)(2,1)S(1)}, u32[]{:S(2)}, u32[]{:S(2)}) collective-permute-start(bf16[128,1024]{1,0:T(8,128)(2,1)S(1)} %select_select_fusion.1.after_ref), channel_id=1, source_target_pairs={{0,2},{2,0},{4,6},{6,4},{8,10},{10,8},{12,14},{14,12},{16,18},{18,... | collective-permute-start | bytes 786440 | tf_op jit(solution)/shard_map/ppermute | solution.py:389
  36.6 6.4 %collective-permute-start.18 = (bf16[128,1024]{1,0:T(8,128)(2,1)S(1)}, bf16[128,1024]{1,0:T(8,128)(2,1)S(1)}, u32[]{:S(2)}, u32[]{:S(2)}) collective-permute-start(bf16[128,1024]{1,0:T(8,128)(2,1)S(1)} %broadcast_select_fusion.1), channel_id=1, source_target_pairs={{0,8},{2,10},{4,12},{6,14},{8,0},{10,2},{12,4},{14,6},{16,24},{18,... | collective-permute-start | bytes 786440 | tf_op jit(solution)/shard_map/ppermute | solution.py:389
  38.1 6.4 %collective-permute-start.16 = (bf16[128,1024]{1,0:T(8,128)(2,1)S(1)}, bf16[128,1024]{1,0:T(8,128)(2,1)S(1)}, u32[]{:S(2)}, u32[]{:S(2)}) collective-permute-start(bf16[128,1024]{1,0:T(8,128)(2,1)S(1)} %select_select_fusion), channel_id=1, source_target_pairs={{0,16},{2,4},{4,2},{6,22},{8,24},{10,26},{12,28},{14,30},{16,0},{1... | collective-permute-start | bytes 786440 | tf_op jit(solution)/shard_map/ppermute | solution.py:389
  40.5 6.4 %collective-permute-start.15 = (bf16[128,1024]{1,0:T(8,128)(2,1)S(1)}, bf16[128,1024]{1,0:T(8,128)(2,1)S(1)}, u32[]{:S(2)}, u32[]{:S(2)}) collective-permute-start(bf16[128,1024]{1,0:T(8,128)(2,1)S(1)} %broadcast_select_fusion), channel_id=1, source_target_pairs={{0,2},{2,0},{4,6},{6,4},{8,10},{10,8},{12,14},{14,12},{16,18},{18,... | collective-permute-start | bytes 786440 | tf_op jit(solution)/shard_map/ppermute | solution.py:389
  47.3 1.8 %collective-permute-start.19 = (bf16[2,12,64,128]{3,2,1,0:T(8,128)(2,1)S(1)}, bf16[2,12,64,128]{3,2,1,0:T(8,128)(2,1)S(1)}, u32[]{:S(2)}, u32[]{:S(2)}) collective-permute-start(bf16[2,12,64,128]{3,2,1,0:T(8,128)(2,1)S(1)} %get-tuple-element.33), channel_id=1, source_target_pairs={{0,1},{1,0},{2,3},{3,2},{4,5},{5,4},{6,7},{7,6},{8,9},{9,8},{10,11... | collective-permute-start | bytes 1179656 | tf_op jit(solution)/shard_map/ppermute | solution.py:408

commit v8 on v6

--- a/solution.py
+++ b/solution.py
@@ -154,7 +154,7 @@
 VMEM_LIMIT = 12 * 2**20
 FIRST = 4
 LAG = 4
-ADD_AT = (9, 12, 16)
+ADD_AT = (9, 12, 15)
 LAST = (2, 1)
 
 

time: 50.1 us -> 50.1 us (level)
  transfers between devices with their start and end apart: 20 -> 20, of which waited for: 11 -> 10; matrix products, arithmetic and copies ran while one was open for 4% -> 4% of each run, Pallas kernels for 12% -> 12%
where the time goes in v8:
time: 50.1 us; the launch traced here: 49.9 us
  starting transfers between devices  30.7 us (61%)
  waiting for transfers between devices  8.87 us (18%)
  Pallas kernels  8.33 us (17%)
  other arithmetic  1.85 us (4%)
    ppermute x19, starting transfers between devices, per_device(): buffers[o] = lax.ppermute(payload, RC, [(s, t) for s, t, _ in moves])  30.6 us
    ppermute x19, waiting for transfers between devices, per_device(): buffers[o] = lax.ppermute(payload, RC, [(s, t) for s, t, _ in moves])  7.94 us
    pallas_call x5, Pallas kernels, more(): pl.pallas_call(functools.partial(more_kernel, [terms[n] for n in names]),...  3.22 us
    pallas_call x1, Pallas kernels, start(): pl.pallas_call(functools.partial(first_kernel, [terms['n0'], terms['n1']]...  1.84 us
    pallas_call x2, Pallas kernels, per_device(): pl.pallas_call(functools.partial(place_kernel, partner), out_shape=jax.Sh...  1.52 us
    pallas_call x1, Pallas kernels, per_device(): pl.pallas_call(functools.partial(units_kernel, min(packed, default=chips)...  1.36 us
  transfers between devices with their start and end apart: 20, of which 10 were waited for; matrix products, arithmetic and copies ran while one was open for 4% of the time, Pallas kernels for 12%

profile of v8, /device:TPU:0, one launch (start us, length us, event | category | flops | bytes accessed | tf_op | source)
XLA Modules:
  0.0 49.9 jit_solution(13859859834909216784)
XLA Ops:
  0.0 1.4 %units.1 = (bf16[128,1024]{1,0:T(8,128)(2,1)S(1)}, bf16[128,1024]{1,0:T(8,128)(2,1)S(1)}, f32[38,1024]{1,0:T(8,128)S(1)}) custom-call(s32[2,16]{1,0:T(2,128)} %fill_hbm.3, bf16[2,16,128,128]{3,2,1,0:T(8,128)(2,1)} %band_hbm.3), custom_call_target="tpu_custom_call" | custom-call | tf_op jit(solution)/shard_map/units/pallas_call | solution.py:323
  1.4 3.1 %collective-permute-start = (bf16[128,1024]{1,0:T(8,128)(2,1)S(1)}, bf16[128,1024]{1,0:T(8,128)(2,1)S(1)}, u32[]{:S(2)}, u32[]{:S(2)}) collective-permute-start(bf16[128,1024]{1,0:T(8,128)(2,1)S(1)} %broadcast_select_fusion.8), channel_id=1, source_target_pairs={{0,2},{2,0},{4,6},{6,4},{8,10},{10,8},{12,14},{14,12},{16,18},{18,... | collective-permute-start | bytes 786440 | tf_op jit(solution)/shard_map/ppermute | solution.py:389
  4.6 1.6 %collective-permute-start.1 = (bf16[128,1024]{1,0:T(8,128)(2,1)S(1)}, bf16[128,1024]{1,0:T(8,128)(2,1)S(1)}, u32[]{:S(2)}, u32[]{:S(2)}) collective-permute-start(bf16[128,1024]{1,0:T(8,128)(2,1)S(1)} %broadcast_select_fusion.7), channel_id=1, source_target_pairs={{0,8},{2,10},{4,12},{6,14},{8,0},{10,2},{12,4},{14,6},{16,24},{18,... | collective-permute-start | bytes 786440 | tf_op jit(solution)/shard_map/ppermute | solution.py:389
  6.2 1.6 %collective-permute-start.2 = (bf16[128,1024]{1,0:T(8,128)(2,1)S(1)}, bf16[128,1024]{1,0:T(8,128)(2,1)S(1)}, u32[]{:S(2)}, u32[]{:S(2)}) collective-permute-start(bf16[128,1024]{1,0:T(8,128)(2,1)S(1)} %broadcast_select_fusion.6), channel_id=1, source_target_pairs={{0,16},{2,18},{4,20},{6,22},{8,24},{10,12},{12,10},{14,30},{16,0},... | collective-permute-start | bytes 786440 | tf_op jit(solution)/shard_map/ppermute | solution.py:389
  8.4 1.8 %first.1 = (bf16[18,256,128]{2,1,0:T(8,128)(2,1)S(1)}, f32[2,12,128]{2,1,0:T(8,128)S(1)}, f32[1,1024]{1,0:T(1,128)S(1)}, f32[17,256,128]{2,1,0:T(8,128)S(1)}) custom-call(s32[2]{0:T(128)} %reach_hbm.1, s32[2,16]{1,0:T(2,128)} %fill_hbm.3, bf16[2,16,128,128]{3,2,1,0:T(8,128)(2,1)} %band_hbm.3, bf16[128,1024]{1,0:T(8,128)(2,1)S(1)} %get-tuple-element.20.refs_0_, ...), custom_call_target="tpu_custom_call" | custom-call | tf_op jit(solution)/shard_map/first/pallas_call | solution.py:341
  10.3 1.4 %collective-permute-done.refs_0_ = bf16[128,1024]{1,0:T(8,128)(2,1)S(1)} collective-permute-done((bf16[128,1024]{1,0:T(8,128)(2,1)S(1)}, bf16[128,1024]{1,0:T(8,128)(2,1)S(1)}, u32[]{:S(2)}, u32[]{:S(2)}) %collective-permute-start) | collective-permute-done | bytes 262176 | tf_op jit(solution)/shard_map/ppermute | solution.py:389
  11.7 2.0 %collective-permute-start.4 = (bf16[128,1024]{1,0:T(8,128)(2,1)S(1)}, bf16[128,1024]{1,0:T(8,128)(2,1)S(1)}, u32[]{:S(2)}, u32[]{:S(2)}) collective-permute-start(bf16[128,1024]{1,0:T(8,128)(2,1)S(1)} %select_select_fusion.9), channel_id=1, source_target_pairs={{0,8},{2,10},{4,12},{6,14},{8,0},{10,2},{12,4},{14,6},{16,24},{18,... | collective-permute-start | bytes 786440 | tf_op jit(solution)/shard_map/ppermute | solution.py:389
  13.8 1.6 %collective-permute-start.5 = (bf16[128,1024]{1,0:T(8,128)(2,1)S(1)}, bf16[128,1024]{1,0:T(8,128)(2,1)S(1)}, u32[]{:S(2)}, u32[]{:S(2)}) collective-permute-start(bf16[128,1024]{1,0:T(8,128)(2,1)S(1)} %broadcast_select_fusion.4), channel_id=1, source_target_pairs={{0,16},{2,4},{4,2},{6,22},{8,24},{10,12},{12,10},{14,30},{16,0},{1... | collective-permute-start | bytes 786440 | tf_op jit(solution)/shard_map/ppermute | solution.py:389
  15.5 1.7 %collective-permute-start.6 = (bf16[128,1024]{1,0:T(8,128)(2,1)S(1)}, bf16[128,1024]{1,0:T(8,128)(2,1)S(1)}, u32[]{:S(2)}, u32[]{:S(2)}) collective-permute-start(bf16[128,1024]{1,0:T(8,128)(2,1)S(1)} %broadcast_select_fusion.3), channel_id=1, source_target_pairs={{0,2},{2,0},{4,6},{6,4},{8,10},{10,8},{12,14},{14,12},{16,18},{18,... | collective-permute-start | bytes 786440 | tf_op jit(solution)/shard_map/ppermute | solution.py:389
  17.4 2.0 %collective-permute-start.7 = (bf16[128,1024]{1,0:T(8,128)(2,1)S(1)}, bf16[128,1024]{1,0:T(8,128)(2,1)S(1)}, u32[]{:S(2)}, u32[]{:S(2)}) collective-permute-start(bf16[128,1024]{1,0:T(8,128)(2,1)S(1)} %select_select_fusion.8), channel_id=1, source_target_pairs={{0,8},{2,10},{4,12},{6,14},{8,0},{10,2},{12,4},{14,6},{16,24},{18,... | collective-permute-start | bytes 786440 | tf_op jit(solution)/shard_map/ppermute | solution.py:389
  19.6 1.6 %collective-permute-start.8 = (bf16[128,1024]{1,0:T(8,128)(2,1)S(1)}, bf16[128,1024]{1,0:T(8,128)(2,1)S(1)}, u32[]{:S(2)}, u32[]{:S(2)}) collective-permute-start(bf16[128,1024]{1,0:T(8,128)(2,1)S(1)} %select_select_fusion.7.after_ref), channel_id=1, source_target_pairs={{0,16},{2,4},{4,2},{6,22},{8,24},{10,12},{12,10},{14,30},{16,0},{1... | collective-permute-start | bytes 786440 | tf_op jit(solution)/shard_map/ppermute | solution.py:389
  21.1 0.8 %more.5 = (f32[1,1024]{1,0:T(1,128)S(1)}, f32[17,256,128]{2,1,0:T(8,128)S(1)}) custom-call(bf16[18,256,128]{2,1,0:T(8,128)(2,1)S(1)} %get-tuple-element.22.left_ref, bf16[128,1024]{1,0:T(8,128)(2,1)S(1)} %select_select_fusion.7.after_ref, bf16[128,1024]{1,0:T(8,128)(2,1)S(1)} %collective-permute-done.refs_0_, ...), custom_call_target="tpu_custom_call", output_to_operand_aliasing={{1}: (7, {})} | custom-call | tf_op jit(solution)/shard_map/more/pallas_call | solution.py:363
  22.1 1.7 %collective-permute-start.9 = (bf16[128,1024]{1,0:T(8,128)(2,1)S(1)}, bf16[128,1024]{1,0:T(8,128)(2,1)S(1)}, u32[]{:S(2)}, u32[]{:S(2)}) collective-permute-start(bf16[128,1024]{1,0:T(8,128)(2,1)S(1)} %broadcast_select_fusion.2), channel_id=1, source_target_pairs={{0,2},{2,0},{4,6},{6,4},{8,10},{10,8},{12,14},{14,12},{16,18},{18,... | collective-permute-start | bytes 786440 | tf_op jit(solution)/shard_map/ppermute | solution.py:389
  23.9 1.1 %collective-permute-start.10 = (bf16[128,1024]{1,0:T(8,128)(2,1)S(1)}, bf16[128,1024]{1,0:T(8,128)(2,1)S(1)}, u32[]{:S(2)}, u32[]{:S(2)}) collective-permute-start(bf16[128,1024]{1,0:T(8,128)(2,1)S(1)} %select_select_fusion.6), channel_id=1, source_target_pairs={{0,8},{2,10},{4,12},{6,14},{8,0},{10,2},{12,4},{14,6},{16,24},{18,... | collective-permute-start | bytes 786440 | tf_op jit(solution)/shard_map/ppermute | solution.py:389
  25.2 1.7 %collective-permute-start.11 = (bf16[128,1024]{1,0:T(8,128)(2,1)S(1)}, bf16[128,1024]{1,0:T(8,128)(2,1)S(1)}, u32[]{:S(2)}, u32[]{:S(2)}) collective-permute-start(bf16[128,1024]{1,0:T(8,128)(2,1)S(1)} %select_select_fusion.5.after_ref), channel_id=1, source_target_pairs={{0,16},{2,4},{4,2},{6,22},{8,24},{10,12},{12,10},{14,30},{16,0},{1... | collective-permute-start | bytes 786440 | tf_op jit(solution)/shard_map/ppermute | solution.py:389
  27.5 1.6 %collective-permute-start.12 = (bf16[128,1024]{1,0:T(8,128)(2,1)S(1)}, bf16[128,1024]{1,0:T(8,128)(2,1)S(1)}, u32[]{:S(2)}, u32[]{:S(2)}) collective-permute-start(bf16[128,1024]{1,0:T(8,128)(2,1)S(1)} %select_select_fusion.4), channel_id=1, source_target_pairs={{0,2},{2,0},{4,6},{6,4},{8,10},{10,8},{12,14},{14,12},{16,18},{18,... | collective-permute-start | bytes 786440 | tf_op jit(solution)/shard_map/ppermute | solution.py:389
  29.7 1.3 %collective-permute-start.13 = (bf16[128,1024]{1,0:T(8,128)(2,1)S(1)}, bf16[128,1024]{1,0:T(8,128)(2,1)S(1)}, u32[]{:S(2)}, u32[]{:S(2)}) collective-permute-start(bf16[128,1024]{1,0:T(8,128)(2,1)S(1)} %select_select_fusion.3), channel_id=1, source_target_pairs={{0,8},{2,10},{4,12},{6,14},{8,0},{10,2},{12,4},{14,6},{16,24},{18,... | collective-permute-start | bytes 786440 | tf_op jit(solution)/shard_map/ppermute | solution.py:389
  31.1 0.6 %collective-permute-done.10.refs_2_ = bf16[128,1024]{1,0:T(8,128)(2,1)S(1)} collective-permute-done((bf16[128,1024]{1,0:T(8,128)(2,1)S(1)}, bf16[128,1024]{1,0:T(8,128)(2,1)S(1)}, u32[]{:S(2)}, u32[]{:S(2)}) %collective-permute-start.10) | collective-permute-done | bytes 262176 | tf_op jit(solution)/shard_map/ppermute | solution.py:389
  31.8 1.6 %collective-permute-start.14 = (bf16[128,1024]{1,0:T(8,128)(2,1)S(1)}, bf16[128,1024]{1,0:T(8,128)(2,1)S(1)}, u32[]{:S(2)}, u32[]{:S(2)}) collective-permute-start(bf16[128,1024]{1,0:T(8,128)(2,1)S(1)} %select_select_fusion.2.after_ref), channel_id=1, source_target_pairs={{0,16},{2,4},{4,2},{6,22},{8,24},{10,12},{12,10},{14,30},{16,0},{1... | collective-permute-start | bytes 786440 | tf_op jit(solution)/shard_map/ppermute | solution.py:389
  34.1 1.6 %collective-permute-start.17 = (bf16[128,1024]{1,0:T(8,128)(2,1)S(1)}, bf16[128,1024]{1,0:T(8,128)(2,1)S(1)}, u32[]{:S(2)}, u32[]{:S(2)}) collective-permute-start(bf16[128,1024]{1,0:T(8,128)(2,1)S(1)} %select_select_fusion.1), channel_id=1, source_target_pairs={{0,2},{2,0},{4,6},{6,4},{8,10},{10,8},{12,14},{14,12},{16,18},{18,... | collective-permute-start | bytes 786440 | tf_op jit(solution)/shard_map/ppermute | solution.py:389
  35.7 0.6 %collective-permute-done.12.refs_1_ = bf16[128,1024]{1,0:T(8,128)(2,1)S(1)} collective-permute-done((bf16[128,1024]{1,0:T(8,128)(2,1)S(1)}, bf16[128,1024]{1,0:T(8,128)(2,1)S(1)}, u32[]{:S(2)}, u32[]{:S(2)}) %collective-permute-start.12) | collective-permute-done | bytes 262176 | tf_op jit(solution)/shard_map/ppermute | solution.py:389
  36.4 0.9 %collective-permute-start.18 = (bf16[128,1024]{1,0:T(8,128)(2,1)S(1)}, bf16[128,1024]{1,0:T(8,128)(2,1)S(1)}, u32[]{:S(2)}, u32[]{:S(2)}) collective-permute-start(bf16[128,1024]{1,0:T(8,128)(2,1)S(1)} %broadcast_select_fusion.1), channel_id=1, source_target_pairs={{0,8},{2,10},{4,12},{6,14},{8,0},{10,2},{12,4},{14,6},{16,24},{18,... | collective-permute-start | bytes 786440 | tf_op jit(solution)/shard_map/ppermute | solution.py:389
  37.3 0.9 %collective-permute-done.13.refs_2_ = bf16[128,1024]{1,0:T(8,128)(2,1)S(1)} collective-permute-done((bf16[128,1024]{1,0:T(8,128)(2,1)S(1)}, bf16[128,1024]{1,0:T(8,128)(2,1)S(1)}, u32[]{:S(2)}, u32[]{:S(2)}) %collective-permute-start.13) | collective-permute-done | bytes 262176 | tf_op jit(solution)/shard_map/ppermute | solution.py:389
  38.2 1.5 %collective-permute-start.16 = (bf16[128,1024]{1,0:T(8,128)(2,1)S(1)}, bf16[128,1024]{1,0:T(8,128)(2,1)S(1)}, u32[]{:S(2)}, u32[]{:S(2)}) collective-permute-start(bf16[128,1024]{1,0:T(8,128)(2,1)S(1)} %select_select_fusion), channel_id=1, source_target_pairs={{0,16},{2,4},{4,2},{6,22},{8,24},{10,26},{12,28},{14,30},{16,0},{1... | collective-permute-start | bytes 786440 | tf_op jit(solution)/shard_map/ppermute | solution.py:389
  39.7 0.8 %collective-permute-done.14.refs_3_ = bf16[128,1024]{1,0:T(8,128)(2,1)S(1)} collective-permute-done((bf16[128,1024]{1,0:T(8,128)(2,1)S(1)}, bf16[128,1024]{1,0:T(8,128)(2,1)S(1)}, u32[]{:S(2)}, u32[]{:S(2)}) %collective-permute-start.14) | collective-permute-done | bytes 262176 | tf_op jit(solution)/shard_map/ppermute | solution.py:389
  40.6 2.0 %collective-permute-start.15 = (bf16[128,1024]{1,0:T(8,128)(2,1)S(1)}, bf16[128,1024]{1,0:T(8,128)(2,1)S(1)}, u32[]{:S(2)}, u32[]{:S(2)}) collective-permute-start(bf16[128,1024]{1,0:T(8,128)(2,1)S(1)} %broadcast_select_fusion), channel_id=1, source_target_pairs={{0,2},{2,0},{4,6},{6,4},{8,10},{10,8},{12,14},{14,12},{16,18},{18,... | collective-permute-start | bytes 786440 | tf_op jit(solution)/shard_map/ppermute | solution.py:389
  42.5 0.6 %collective-permute-done.17.refs_4_ = bf16[128,1024]{1,0:T(8,128)(2,1)S(1)} collective-permute-done((bf16[128,1024]{1,0:T(8,128)(2,1)S(1)}, bf16[128,1024]{1,0:T(8,128)(2,1)S(1)}, u32[]{:S(2)}, u32[]{:S(2)}) %collective-permute-start.17) | collective-permute-done | bytes 262176 | tf_op jit(solution)/shard_map/ppermute | solution.py:389
  43.1 1.0 %more.8.refs_1_ = f32[17,256,128]{2,1,0:T(8,128)S(1)} custom-call(bf16[18,256,128]{2,1,0:T(8,128)(2,1)S(1)} %get-tuple-element.22.left_ref, bf16[128,1024]{1,0:T(8,128)(2,1)S(1)} %collective-permute-done.11.after_ref.refs_0_, bf16[128,1024]{1,0:T(8,128)(2,1)S(1)} %collective-permute-done.11.after_ref.refs_0_, ...), custom_call_target="tpu_custom_call", output_to_operand_aliasing={{}: (8, {})} | custom-call | tf_op jit(solution)/shard_map/more/pallas_call | solution.py:363
  44.9 2.1 %collective-permute-done.15.refs_0_ = bf16[128,1024]{1,0:T(8,128)(2,1)S(1)} collective-permute-done((bf16[128,1024]{1,0:T(8,128)(2,1)S(1)}, bf16[128,1024]{1,0:T(8,128)(2,1)S(1)}, u32[]{:S(2)}, u32[]{:S(2)}) %collective-permute-start.15) | collective-permute-done | bytes 262176 | tf_op jit(solution)/shard_map/ppermute | solution.py:389
  47.5 0.8 %place.2.refs_0_ = bf16[2,12,2,64,128]{4,3,2,1,0:T(8,128)(2,1)} custom-call(bf16[2,12,64,128]{3,2,1,0:T(8,128)(2,1)S(1)} %get-tuple-element.34.tiles), custom_call_target="tpu_custom_call" | custom-call | tf_op jit(solution)/shard_map/place/pallas_call | solution.py:411
  48.2 0.9 %collective-permute-done.19.tiles = bf16[2,12,64,128]{3,2,1,0:T(8,128)(2,1)S(1)} collective-permute-done((bf16[2,12,64,128]{3,2,1,0:T(8,128)(2,1)S(1)}, bf16[2,12,64,128]{3,2,1,0:T(8,128)(2,1)S(1)}, u32[]{:S(2)}, u32[]{:S(2)}) %collective-permute-start.19) | collective-permute-done | bytes 393248 | tf_op jit(solution)/shard_map/ppermute | solution.py:408
  49.2 0.8 %place.3 = bf16[2,12,2,64,128]{4,3,2,1,0:T(8,128)(2,1)} custom-call(bf16[2,12,64,128]{3,2,1,0:T(8,128)(2,1)S(1)} %collective-permute-done.19.tiles, bf16[2,12,2,64,128]{4,3,2,1,0:T(8,128)(2,1)} %place.2.refs_0_), custom_call_target="tpu_custom_call", output_to_operand_aliasing={{}: (1, {})} | custom-call | tf_op jit(solution)/shard_map/place/pallas_call | solution.py:411
  (56 shorter events, 5.2 us)
Async XLA Ops:
  1.4 10.2 %collective-permute-start = (bf16[128,1024]{1,0:T(8,128)(2,1)S(1)}, bf16[128,1024]{1,0:T(8,128)(2,1)S(1)}, u32[]{:S(2)}, u32[]{:S(2)}) collective-permute-start(bf16[128,1024]{1,0:T(8,128)(2,1)S(1)} %broadcast_select_fusion.8), channel_id=1, source_target_pairs={{0,2},{2,0},{4,6},{6,4},{8,10},{10,8},{12,14},{14,12},{16,18},{18,... | collective-permute-start | bytes 786440 | tf_op jit(solution)/shard_map/ppermute | solution.py:389
  4.6 9.2 %collective-permute-start.1 = (bf16[128,1024]{1,0:T(8,128)(2,1)S(1)}, bf16[128,1024]{1,0:T(8,128)(2,1)S(1)}, u32[]{:S(2)}, u32[]{:S(2)}) collective-permute-start(bf16[128,1024]{1,0:T(8,128)(2,1)S(1)} %broadcast_select_fusion.7), channel_id=1, source_target_pairs={{0,8},{2,10},{4,12},{6,14},{8,0},{10,2},{12,4},{14,6},{16,24},{18,... | collective-permute-start | bytes 786440 | tf_op jit(solution)/shard_map/ppermute | solution.py:389
  6.2 9.2 %collective-permute-start.2 = (bf16[128,1024]{1,0:T(8,128)(2,1)S(1)}, bf16[128,1024]{1,0:T(8,128)(2,1)S(1)}, u32[]{:S(2)}, u32[]{:S(2)}) collective-permute-start(bf16[128,1024]{1,0:T(8,128)(2,1)S(1)} %broadcast_select_fusion.6), channel_id=1, source_target_pairs={{0,16},{2,18},{4,20},{6,22},{8,24},{10,12},{12,10},{14,30},{16,0},... | collective-permute-start | bytes 786440 | tf_op jit(solution)/shard_map/ppermute | solution.py:389
  7.9 9.4 %collective-permute-start.3 = (bf16[128,1024]{1,0:T(8,128)(2,1)S(1)}, bf16[128,1024]{1,0:T(8,128)(2,1)S(1)}, u32[]{:S(2)}, u32[]{:S(2)}) collective-permute-start(bf16[128,1024]{1,0:T(8,128)(2,1)S(1)} %broadcast_select_fusion.5), channel_id=1, source_target_pairs={{0,2},{2,0},{4,6},{6,4},{8,10},{10,8},{12,14},{14,12},{16,18},{18,... | collective-permute-start | bytes 786440 | tf_op jit(solution)/shard_map/ppermute | solution.py:389
  11.7 7.8 %collective-permute-start.4 = (bf16[128,1024]{1,0:T(8,128)(2,1)S(1)}, bf16[128,1024]{1,0:T(8,128)(2,1)S(1)}, u32[]{:S(2)}, u32[]{:S(2)}) collective-permute-start(bf16[128,1024]{1,0:T(8,128)(2,1)S(1)} %select_select_fusion.9), channel_id=1, source_target_pairs={{0,8},{2,10},{4,12},{6,14},{8,0},{10,2},{12,4},{14,6},{16,24},{18,... | collective-permute-start | bytes 786440 | tf_op jit(solution)/shard_map/ppermute | solution.py:389
  13.8 8.2 %collective-permute-start.5 = (bf16[128,1024]{1,0:T(8,128)(2,1)S(1)}, bf16[128,1024]{1,0:T(8,128)(2,1)S(1)}, u32[]{:S(2)}, u32[]{:S(2)}) collective-permute-start(bf16[128,1024]{1,0:T(8,128)(2,1)S(1)} %broadcast_select_fusion.4), channel_id=1, source_target_pairs={{0,16},{2,4},{4,2},{6,22},{8,24},{10,12},{12,10},{14,30},{16,0},{1... | collective-permute-start | bytes 786440 | tf_op jit(solution)/shard_map/ppermute | solution.py:389
  15.5 8.4 %collective-permute-start.6 = (bf16[128,1024]{1,0:T(8,128)(2,1)S(1)}, bf16[128,1024]{1,0:T(8,128)(2,1)S(1)}, u32[]{:S(2)}, u32[]{:S(2)}) collective-permute-start(bf16[128,1024]{1,0:T(8,128)(2,1)S(1)} %broadcast_select_fusion.3), channel_id=1, source_target_pairs={{0,2},{2,0},{4,6},{6,4},{8,10},{10,8},{12,14},{14,12},{16,18},{18,... | collective-permute-start | bytes 786440 | tf_op jit(solution)/shard_map/ppermute | solution.py:389
  17.4 7.7 %collective-permute-start.7 = (bf16[128,1024]{1,0:T(8,128)(2,1)S(1)}, bf16[128,1024]{1,0:T(8,128)(2,1)S(1)}, u32[]{:S(2)}, u32[]{:S(2)}) collective-permute-start(bf16[128,1024]{1,0:T(8,128)(2,1)S(1)} %select_select_fusion.8), channel_id=1, source_target_pairs={{0,8},{2,10},{4,12},{6,14},{8,0},{10,2},{12,4},{14,6},{16,24},{18,... | collective-permute-start | bytes 786440 | tf_op jit(solution)/shard_map/ppermute | solution.py:389
  19.6 7.9 %collective-permute-start.8 = (bf16[128,1024]{1,0:T(8,128)(2,1)S(1)}, bf16[128,1024]{1,0:T(8,128)(2,1)S(1)}, u32[]{:S(2)}, u32[]{:S(2)}) collective-permute-start(bf16[128,1024]{1,0:T(8,128)(2,1)S(1)} %select_select_fusion.7.after_ref), channel_id=1, source_target_pairs={{0,16},{2,4},{4,2},{6,22},{8,24},{10,12},{12,10},{14,30},{16,0},{1... | collective-permute-start | bytes 786440 | tf_op jit(solution)/shard_map/ppermute | solution.py:389
  22.1 7.6 %collective-permute-start.9 = (bf16[128,1024]{1,0:T(8,128)(2,1)S(1)}, bf16[128,1024]{1,0:T(8,128)(2,1)S(1)}, u32[]{:S(2)}, u32[]{:S(2)}) collective-permute-start(bf16[128,1024]{1,0:T(8,128)(2,1)S(1)} %broadcast_select_fusion.2), channel_id=1, source_target_pairs={{0,2},{2,0},{4,6},{6,4},{8,10},{10,8},{12,14},{14,12},{16,18},{18,... | collective-permute-start | bytes 786440 | tf_op jit(solution)/shard_map/ppermute | solution.py:389
  23.9 7.8 %collective-permute-start.10 = (bf16[128,1024]{1,0:T(8,128)(2,1)S(1)}, bf16[128,1024]{1,0:T(8,128)(2,1)S(1)}, u32[]{:S(2)}, u32[]{:S(2)}) collective-permute-start(bf16[128,1024]{1,0:T(8,128)(2,1)S(1)} %select_select_fusion.6), channel_id=1, source_target_pairs={{0,8},{2,10},{4,12},{6,14},{8,0},{10,2},{12,4},{14,6},{16,24},{18,... | collective-permute-start | bytes 786440 | tf_op jit(solution)/shard_map/ppermute | solution.py:389
  25.2 8.8 %collective-permute-start.11 = (bf16[128,1024]{1,0:T(8,128)(2,1)S(1)}, bf16[128,1024]{1,0:T(8,128)(2,1)S(1)}, u32[]{:S(2)}, u32[]{:S(2)}) collective-permute-start(bf16[128,1024]{1,0:T(8,128)(2,1)S(1)} %select_select_fusion.5.after_ref), channel_id=1, source_target_pairs={{0,16},{2,4},{4,2},{6,22},{8,24},{10,12},{12,10},{14,30},{16,0},{1... | collective-permute-start | bytes 786440 | tf_op jit(solution)/shard_map/ppermute | solution.py:389
  27.5 8.8 %collective-permute-start.12 = (bf16[128,1024]{1,0:T(8,128)(2,1)S(1)}, bf16[128,1024]{1,0:T(8,128)(2,1)S(1)}, u32[]{:S(2)}, u32[]{:S(2)}) collective-permute-start(bf16[128,1024]{1,0:T(8,128)(2,1)S(1)} %select_select_fusion.4), channel_id=1, source_target_pairs={{0,2},{2,0},{4,6},{6,4},{8,10},{10,8},{12,14},{14,12},{16,18},{18,... | collective-permute-start | bytes 786440 | tf_op jit(solution)/shard_map/ppermute | solution.py:389
  29.7 8.4 %collective-permute-start.13 = (bf16[128,1024]{1,0:T(8,128)(2,1)S(1)}, bf16[128,1024]{1,0:T(8,128)(2,1)S(1)}, u32[]{:S(2)}, u32[]{:S(2)}) collective-permute-start(bf16[128,1024]{1,0:T(8,128)(2,1)S(1)} %select_select_fusion.3), channel_id=1, source_target_pairs={{0,8},{2,10},{4,12},{6,14},{8,0},{10,2},{12,4},{14,6},{16,24},{18,... | collective-permute-start | bytes 786440 | tf_op jit(solution)/shard_map/ppermute | solution.py:389
  31.8 8.7 %collective-permute-start.14 = (bf16[128,1024]{1,0:T(8,128)(2,1)S(1)}, bf16[128,1024]{1,0:T(8,128)(2,1)S(1)}, u32[]{:S(2)}, u32[]{:S(2)}) collective-permute-start(bf16[128,1024]{1,0:T(8,128)(2,1)S(1)} %select_select_fusion.2.after_ref), channel_id=1, source_target_pairs={{0,16},{2,4},{4,2},{6,22},{8,24},{10,12},{12,10},{14,30},{16,0},{1... | collective-permute-start | bytes 786440 | tf_op jit(solution)/shard_map/ppermute | solution.py:389
  34.1 9.1 %collective-permute-start.17 = (bf16[128,1024]{1,0:T(8,128)(2,1)S(1)}, bf16[128,1024]{1,0:T(8,128)(2,1)S(1)}, u32[]{:S(2)}, u32[]{:S(2)}) collective-permute-start(bf16[128,1024]{1,0:T(8,128)(2,1)S(1)} %select_select_fusion.1), channel_id=1, source_target_pairs={{0,2},{2,0},{4,6},{6,4},{8,10},{10,8},{12,14},{14,12},{16,18},{18,... | collective-permute-start | bytes 786440 | tf_op jit(solution)/shard_map/ppermute | solution.py:389
  36.4 6.8 %collective-permute-start.18 = (bf16[128,1024]{1,0:T(8,128)(2,1)S(1)}, bf16[128,1024]{1,0:T(8,128)(2,1)S(1)}, u32[]{:S(2)}, u32[]{:S(2)}) collective-permute-start(bf16[128,1024]{1,0:T(8,128)(2,1)S(1)} %broadcast_select_fusion.1), channel_id=1, source_target_pairs={{0,8},{2,10},{4,12},{6,14},{8,0},{10,2},{12,4},{14,6},{16,24},{18,... | collective-permute-start | bytes 786440 | tf_op jit(solution)/shard_map/ppermute | solution.py:389
  38.2 6.4 %collective-permute-start.16 = (bf16[128,1024]{1,0:T(8,128)(2,1)S(1)}, bf16[128,1024]{1,0:T(8,128)(2,1)S(1)}, u32[]{:S(2)}, u32[]{:S(2)}) collective-permute-start(bf16[128,1024]{1,0:T(8,128)(2,1)S(1)} %select_select_fusion), channel_id=1, source_target_pairs={{0,16},{2,4},{4,2},{6,22},{8,24},{10,26},{12,28},{14,30},{16,0},{1... | collective-permute-start | bytes 786440 | tf_op jit(solution)/shard_map/ppermute | solution.py:389
  40.6 6.4 %collective-permute-start.15 = (bf16[128,1024]{1,0:T(8,128)(2,1)S(1)}, bf16[128,1024]{1,0:T(8,128)(2,1)S(1)}, u32[]{:S(2)}, u32[]{:S(2)}) collective-permute-start(bf16[128,1024]{1,0:T(8,128)(2,1)S(1)} %broadcast_select_fusion), channel_id=1, source_target_pairs={{0,2},{2,0},{4,6},{6,4},{8,10},{10,8},{12,14},{14,12},{16,18},{18,... | collective-permute-start | bytes 786440 | tf_op jit(solution)/shard_map/ppermute | solution.py:389
  47.4 1.8 %collective-permute-start.19 = (bf16[2,12,64,128]{3,2,1,0:T(8,128)(2,1)S(1)}, bf16[2,12,64,128]{3,2,1,0:T(8,128)(2,1)S(1)}, u32[]{:S(2)}, u32[]{:S(2)}) collective-permute-start(bf16[2,12,64,128]{3,2,1,0:T(8,128)(2,1)S(1)} %get-tuple-element.33), channel_id=1, source_target_pairs={{0,1},{1,0},{2,3},{3,2},{4,5},{5,4},{6,7},{7,6},{8,9},{9,8},{10,11... | collective-permute-start | bytes 1179656 | tf_op jit(solution)/shard_map/ppermute | solution.py:408
